TPU v7x, 256 devices: a whole 4x4x8 slice. The times are simulated.
256 devices in a mesh: pair: 8 (over x_lo, y), outv: 8 (over z), conv: 4 (over x_hi, core).
Axes of the slice: x: 4 (x_hi: 2, x_lo: 2; x = x_hi * 2 + x_lo), y: 4, z: 8, core: 2. Of those that a mesh axis runs over, the one named last changes fastest.
Arguments:
- amplitudes: bfloat16 [16384, 6144], P('pair', ('conv', 'outv')), may hold values from -6 to 6
- integrals: bfloat16 [6144, 12288], P('conv', ('outv', 'pair')), may hold values from -0.21875 to 0.21875
- amp_mask: int32 [8, 64], P('pair', 'conv'), may hold values from 0 to 1, as said below
- int_mask: int32 [64, 128], P('conv', 'outv'), may hold values 0 or 1
Outputs:
- ladder: bfloat16 [12288, 16384], P(('outv', 'conv'), 'pair')
Inputs may be any that keep to these rules, and one draw needn't show every extreme that they name: `amp_mask`: 0 or 1; the share of ones differs from pair tile to pair tile.
All inputs are finite; a program needn't handle non-finite values. No bound on the sum of `int_mask` on one device may be relied on, other than what follows from the above.
Results may differ from a plain program's by a relative error of at most 0.001.
Values may be sent and summed in bfloat16 or wider, within the bound.
No kernel may reach another device: no remote copies, remote signals or barrier semaphores. Data moves between devices by JAX's collectives and lax.ppermute only.
A program may use at most 64 MiB of HBM per device.

v0:
```python
import jax
import jax.numpy as jnp
from jax import lax
from jax.sharding import PartitionSpec as P

TW = 96


def column_mask(block_mask, first, width):
    tiles = block_mask.shape[1]
    col_tile = (first * width + jnp.arange(width, dtype=jnp.int32)) // TW
    onehot = (col_tile[None, :] == jnp.arange(tiles, dtype=jnp.int32)[:, None]).astype(jnp.float32)
    return jnp.dot(block_mask.astype(jnp.float32), onehot, preferred_element_type=jnp.float32)


def contract(columns, amp_rows):
    dims = (((0,), (1,)), ((), ()))
    return lax.dot_general(columns, amp_rows, dims, preferred_element_type=jnp.float32)


def body(amplitudes, integrals, amp_mask, int_mask):
    width_amp = amplitudes.shape[1]
    amp_cols = column_mask(amp_mask, lax.axis_index("outv"), width_amp)
    amp_local = amplitudes * amp_cols.astype(jnp.bfloat16)
    amp_rows = lax.all_gather(amp_local, "outv", axis=1, tiled=True)
    tiles_k = int_mask.shape[0]
    width_int = integrals.shape[1]
    int_cols = column_mask(int_mask, lax.axis_index("pair"), width_int)
    int_local = (
        integrals.reshape(tiles_k, TW, width_int) * int_cols[:, None, :].astype(jnp.bfloat16)
    ).reshape(tiles_k * TW, width_int)
    int_full = lax.all_gather(int_local, "pair", axis=1, tiled=True)
    summed = lax.psum_scatter(contract(int_full, amp_rows), "conv", scatter_dimension=0, tiled=True)
    return summed.astype(jnp.bfloat16)


def solution(mesh):
    placed = (
        P("pair", ("conv", "outv")),
        P("conv", ("outv", "pair")),
        P("pair", "conv"),
        P("conv", "outv"),
    )
    return jax.shard_map(
        body, mesh=mesh, in_specs=placed, out_specs=P(("outv", "conv"), "pair"), check_vma=False
    )
```

profile of v0, /device:TPU:24, one launch (start us, length us, event | category | flops | bytes accessed | tf_op | source)
XLA Modules:
  0.0 284.7 jit_solution(13967554948303165017)
XLA Ops:
  6.5 0.0 all-gather.3.cloned.1.call-start
  6.6 0.8 fusion
  7.4 0.1 copy.5
  7.5 0.5 mul.26
  8.0 0.9 mul.27
  8.9 2.0 mul.28
  10.9 0.0 all-gather.3.cloned.1.call-update
  10.9 0.0 all-gather.5.cloned.1.call-start
  11.0 0.8 fusion.1
  11.8 2.1 broadcast_multiply_fusion
  13.9 0.0 all-gather.5.cloned.1.call-update
  13.9 0.0 reduce-scatter.2.cloned.1.call-start
  14.0 57.6 %all-gather.3.cloned.1.call-done = bf16[1536,1536]{0,1:T(8,128)(2,1)} async-done(((bf16[1536,192]{0,1:T(8,128)(2,1)}), bf16[1536,1536]{0,1:T(8,128)(2,1)}) %all-gather.3.cloned.1.call-update) | async-done | bytes 4718608 | tf_op jit(solution)/shard_map/all_gather | solution.py:32
  71.6 77.4 %all-gather.5.cloned.1.call-done = bf16[2048,1536]{0,1:T(8,128)(2,1)} async-done(((bf16[2048,192]{0,1:T(8,128)(2,1)}), bf16[2048,1536]{0,1:T(8,128)(2,1)}) %all-gather.5.cloned.1.call-update) | async-done | bytes 6291472 | tf_op jit(solution)/shard_map/all_gather | solution.py:25
  149.0 16.1 %fusion.5 = f32[1536,2048]{1,0:T(8,128)} fusion(bf16[1536,1536]{0,1:T(8,128)(2,1)} %all-gather.3.cloned.1.call-done, bf16[2048,1536]{0,1:T(8,128)(2,1)} %all-gather.5.cloned.1.call-done), kind=kOutput, calls=%fused_computation.12 | convolution fusion | flops 9663676416 | bytes 23592960 | tf_op jit(solution)/shard_map/dot_general | solution.py:18
  165.1 0.0 reduce-scatter.2.cloned.1.call-update
  165.1 109.8 %reduce-scatter.2.cloned.1.call-done = f32[384,2048]{1,0:T(8,128)} async-done(((f32[1536,2048]{1,0:T(8,128)}), f32[384,2048]{1,0:T(8,128)}) %reduce-scatter.2.cloned.1.call-update) | async-done | bytes 3145744 | tf_op jit(solution)/shard_map/reduce_scatter | solution.py:33
  274.9 3.3 %convert_element_type.27 = bf16[384,2048]{1,0:T(8,128)(2,1)} convert(f32[384,2048]{1,0:T(8,128)} %reduce-scatter.2.cloned.1.call-done) | non-fusion elementwise | flops 786432 | bytes 4718592 | tf_op jit(solution)/shard_map/convert_element_type | solution.py:34
  (3 shorter events, 0.0 us)
Async XLA Ops:
  6.5 65.0 %all-gather.3.cloned.1.call-start = ((), (), s32[]{:S(2)}) async-start(), calls=%async_computation.1 | async-start | bytes 5308416 | tf_op jit(solution)/shard_map/all_gather | solution.py:32
  10.9 138.0 %all-gather.5.cloned.1.call-start = ((), (), s32[]{:S(2)}) async-start(), calls=%async_computation.2 | async-start | bytes 7077888 | tf_op jit(solution)/shard_map/all_gather | solution.py:25
  13.9 261.0 %reduce-scatter.2.cloned.1.call-start = ((), (), s32[]{:S(2)}) async-start(), calls=%async_computation.3 | async-start | bytes 15728640 | tf_op jit(solution)/shard_map/reduce_scatter | solution.py:33
Sparse Core Ops, SparseCore 0:
  11.0 60.4 all-gather.2
  73.4 75.5 all-gather.4
  165.2 109.6 reduce-scatter.1
where the time goes:
time: 286 us; the launch traced here: 285 us
  waiting for transfers between devices  245 us (86%)
  matrix products  17.7 us (6%)
  between operations  13.1 us (5%)
  other arithmetic  7.46 us (3%)
    reduce_scatter x1, waiting for transfers between devices, body(): lax.psum_scatter(contract(int_full, amp_rows), 'conv', scatter_dimension=...  110 us
    all_gather x1, waiting for transfers between devices, body(): amp_rows = lax.all_gather(amp_local, 'outv', axis=1, tiled=True)  77.4 us
    all_gather x1, waiting for transfers between devices, body(): int_full = lax.all_gather(int_local, 'pair', axis=1, tiled=True)  57.6 us
    dot_general x1, matrix products, contract(): lax.dot_general(columns, amp_rows, dims, preferred_element_type=jnp.float32)  16.1 us
  transfers between devices with their start and end apart: 3, of which 3 were waited for; matrix products, arithmetic and copies ran while one was open for 1% of the time, Pallas kernels for 0%

commit v1 on v0

v1 whole, which is shorter than its diff:
```python
import jax
import jax.numpy as jnp
from jax import lax
from jax.experimental import pallas as pl
from jax.experimental.pallas import tpu as pltpu
from jax.sharding import PartitionSpec as P

TW = 96
AXES = ("pair", "outv", "conv")
NX, NY, NZ = 4, 4, 8
RCHUNKS = 2
VMEM = pltpu.MemorySpace.VMEM
SMEM = pltpu.MemorySpace.SMEM


def index_of(x, y, z, c):
    x, y, z = x % NX, y % NY, z % NZ
    return ((x % 2) * NY + y) * (NZ * 4) + z * 4 + (x // 2) * 2 + c


def moves(target):
    return [
        (index_of(x, y, z, c), index_of(*target(x, y, z, c)))
        for x in range(NX)
        for y in range(NY)
        for z in range(NZ)
        for c in range(2)
    ]


def sign(i, c):
    return 1 - 2 * ((i + c) % 2)


X_FIRST = moves(lambda x, y, z, c: (x + sign(x, c), y, z, c))
X_OTHER = moves(lambda x, y, z, c: (x - sign(x, c), y, z, c))
Y_FIRST = moves(lambda x, y, z, c: (x, y + sign(y, c), z, c))
Y_OTHER = moves(lambda x, y, z, c: (x, y - sign(y, c), z, c))
Z_FIRST = moves(lambda x, y, z, c: (x, y, z + sign(z, c), c))
Z_OTHER = moves(lambda x, y, z, c: (x, y, z - sign(z, c), c))
X_ACROSS = moves(lambda x, y, z, c: (x + 2, y, z, c))
CORE = moves(lambda x, y, z, c: (x, y, z, 1 - c))
RING4 = (0, 1, -1, -2)
RING8 = (0, 1, -1, -2, 2, 3, -3, -4)


def send(array, plan):
    return lax.ppermute(array, AXES, plan)


def mask_integrals_kernel(place, mask_ref, int_ref, first_ref, second_ref):
    width = int_ref.shape[1]
    half = width // 2
    tile = lax.broadcasted_iota(jnp.int32, (8, width), 1) // TW
    for j in range(int_ref.shape[0] // TW):
        column = place[0] * (int_ref.shape[0] // TW) + j
        row = jnp.zeros((8, width), jnp.float32)
        for k in range(width // TW):
            row = jnp.where(tile == k, mask_ref[k, column].astype(jnp.float32), row)
        row = row[0:1, :].astype(jnp.bfloat16)
        rows = pl.ds(j * TW, TW)
        first_ref[rows, :] = int_ref[rows, :half] * row[:, :half]
        second_ref[rows, :] = int_ref[rows, half:] * row[:, half:]


def mask_integrals(place, int_mask, int_t):
    rows, width = int_t.shape
    shape = jax.ShapeDtypeStruct((rows, width // 2), jnp.bfloat16)
    return pl.pallas_call(
        mask_integrals_kernel,
        in_specs=[pl.BlockSpec(memory_space=SMEM), pl.BlockSpec(memory_space=SMEM), pl.BlockSpec(memory_space=VMEM)],
        out_specs=[pl.BlockSpec(memory_space=VMEM)] * 2,
        out_shape=[shape, shape],
        name="mask_integrals",
    )(place, int_mask, int_t)


def mask_amplitudes_kernel(place, mask_ref, amp_ref, keep_ref, give_ref):
    half = amp_ref.shape[1] // 2
    for j in range(amp_ref.shape[0] // TW):
        value = mask_ref[0, place[1] * (amp_ref.shape[0] // TW) + j].astype(jnp.float32)
        rows = pl.ds(j * TW, TW)
        row = jnp.full((1, half), value, jnp.float32).astype(jnp.bfloat16)
        keep_ref[rows, :] = amp_ref[rows, pl.ds(pl.multiple_of(place[2] * half, 128), half)] * row
        give_ref[rows, :] = amp_ref[rows, pl.ds(pl.multiple_of((1 - place[2]) * half, 128), half)] * row


def mask_amplitudes(place, amp_mask, amp_t):
    rows, width = amp_t.shape
    shape = jax.ShapeDtypeStruct((rows, width // 2), jnp.bfloat16)
    return pl.pallas_call(
        mask_amplitudes_kernel,
        in_specs=[pl.BlockSpec(memory_space=SMEM), pl.BlockSpec(memory_space=SMEM), pl.BlockSpec(memory_space=VMEM)],
        out_specs=[pl.BlockSpec(memory_space=VMEM)] * 2,
        out_shape=[shape, shape],
        name="mask_amplitudes",
    )(place, amp_mask, amp_t)


def ring_of_eight(own):
    got = send(own, Z_FIRST)
    near = jnp.stack([own, got])
    second = send(near, Z_OTHER)
    third = send(second, Z_FIRST)
    fourth = send(third, Z_OTHER)
    return [near, second, third, fourth]


def plane(own, first_axis, second_axis):
    got = send(own, first_axis[0])
    near = jnp.stack([own, got])
    far = send(near, first_axis[1])
    pieces = []
    for group in (near, far):
        step = send(group, second_axis[0])
        pieces += [group, step, send(group, second_axis[1]), send(step, second_axis[1])]
    return pieces


def multiply_kernel(own, rchunk, place, *refs):
    n_int, n_amp = 16, 8
    int_refs, amp_refs = refs[:n_int], refs[n_int : n_int + n_amp]
    rest = list(refs[n_int + n_amp :])
    other_ref = rest.pop(0) if own else None
    outs = [rest.pop(0) for _ in range(2 if own else 1)]
    int_v, amp_v, int_sems, amp_sems = rest
    x, y, z, c = place[3], place[4], place[1], place[5]
    x_hi = place[2]
    core = c if own else 1 - c
    sx, sy, sz = 1 - 2 * ((x + c) % 2), 1 - 2 * ((y + c) % 2), 1 - 2 * ((z + c) % 2)
    rows, depth, width = 192, 768, amp_v.shape[1]

    amp_copies = []
    for chain in range(2):
        hi = x_hi if chain == 0 else 1 - x_hi
        for step in range(4):
            for e in range(2):
                z_from = (z + sz * RING8[2 * step + e] + 8) % 8
                row = pl.multiple_of((hi * 8 + z_from) * rows, rows)
                amp_copies.append(
                    pltpu.make_async_copy(
                        amp_refs[chain * 4 + step].at[e, :, pl.ds(rchunk * width, width)],
                        amp_v.at[pl.ds(row, rows), :],
                        amp_sems.at[len(amp_copies)],
                    )
                )
    int_copies = []
    for half in range(2):
        for group in range(2):
            for step in range(4):
                for e in range(2):
                    near, far = RING4[2 * group + e], RING4[step]
                    dx, dy = (near, far) if half == 0 else (far, near)
                    x_from, y_from = (x + sx * dx + 4) % 4, (y + sy * dy + 4) % 4
                    block = ((x_from % 2 + x_hi + 1) % 2) * 2 + y_from % 2
                    row = pl.multiple_of(block * rows, rows)
                    col = pl.multiple_of((x_from // 2) * 2 * depth + half * depth, 128)
                    copy = pltpu.make_async_copy(
                        int_refs[half * 8 + group * 4 + step].at[e],
                        int_v.at[pl.ds(row, rows), pl.ds(col, depth)],
                        int_sems.at[len(int_copies)],
                    )
                    int_copies.append((y_from // 2 == core, copy))
    for copy in amp_copies:
        copy.start()
    for here, copy in int_copies:
        pl.when(here)(copy.start)
    for copy in amp_copies:
        copy.wait()
    for here, copy in int_copies:
        pl.when(here)(copy.wait)

    size = 128
    for part in range(2):
        @pl.loop(0, 384 // size)
        def _(i):
            src = pl.ds(pl.multiple_of(part * 384 + i * size, size), size)
            total = jnp.dot(int_v[src, :], amp_v[...], preferred_element_type=jnp.float32)
            if own:
                dst = pl.ds(pl.multiple_of(i * size, size), size)
                outs[part][dst, :] = (total + other_ref[src, :]).astype(jnp.bfloat16)
            else:
                outs[0][src, :] = total


def multiply(own, rchunk, place, ints, amps, other=None):
    width = 1024 // RCHUNKS
    if own:
        shapes = [jax.ShapeDtypeStruct((384, width), jnp.bfloat16)] * 2
    else:
        shapes = [jax.ShapeDtypeStruct((768, width), jnp.float32)]
    any_spec = pl.BlockSpec(memory_space=pl.ANY)
    specs = [pl.BlockSpec(memory_space=SMEM)] + [any_spec] * (len(ints) + len(amps))
    args = [place, *ints, *amps]
    if own:
        specs.append(pl.BlockSpec(memory_space=VMEM))
        args.append(other)

    def kernel(*refs):
        multiply_kernel(own, rchunk, *refs)

    out = pl.pallas_call(
        kernel,
        in_specs=specs,
        out_specs=[pl.BlockSpec(memory_space=VMEM)] * len(shapes),
        out_shape=shapes,
        scratch_shapes=[
            pltpu.VMEM((768, 3072), jnp.bfloat16),
            pltpu.VMEM((3072, width), jnp.bfloat16),
            pltpu.SemaphoreType.DMA((32,)),
            pltpu.SemaphoreType.DMA((16,)),
        ],
        compiler_params=pltpu.CompilerParams(vmem_limit_bytes=40 * 1024 * 1024),
        cost_estimate=pl.CostEstimate(
            flops=2 * 768 * 3072 * width, bytes_accessed=768 * 3072 * 2 + 3072 * width * 2 + 768 * width * 4, transcendentals=0
        ),
        name="multiply_own" if own else "multiply_other",
    )(*args)
    return out


def body(amplitudes, integrals, amp_mask, int_mask):
    pair, z, conv = (lax.axis_index(name) for name in AXES)
    x_hi, core = conv // 2, conv % 2
    x_lo, y = pair // NY, pair % NY
    place = jnp.stack([pair, z, x_hi, x_hi * 2 + x_lo, y, core]).astype(jnp.int32)

    first, second = mask_integrals(place, int_mask, integrals.T)
    keep, give = mask_amplitudes(place, amp_mask, amplitudes.T)
    partner = send(give, X_ACROSS)
    amps = ring_of_eight(keep) + ring_of_eight(partner)
    ints = plane(first, (X_FIRST, X_OTHER), (Y_FIRST, Y_OTHER)) + plane(second, (Y_FIRST, Y_OTHER), (X_FIRST, X_OTHER))

    kept, received = [], []
    for r in range(RCHUNKS):
        (partial,) = multiply(False, r, place, ints, amps)
        other = send(partial, CORE)
        theirs, mine = multiply(True, r, place, ints, amps, other)
        kept.append(mine)
        received.append(send(theirs, X_ACROSS))
    low = [jnp.where(x_hi == 0, k, g) for k, g in zip(kept, received)]
    high = [jnp.where(x_hi == 0, g, k) for k, g in zip(kept, received)]
    return jnp.concatenate(low + high, axis=1)


def solution(mesh):
    placed = (
        P("pair", ("conv", "outv")),
        P("conv", ("outv", "pair")),
        P("pair", "conv"),
        P("conv", "outv"),
    )
    return jax.shard_map(
        body, mesh=mesh, in_specs=placed, out_specs=P(("outv", "conv"), "pair"), check_vma=False
    )
```

time: 286 us -> 143 us (0.50)
  waiting for transfers between devices: 245 us -> 43.9 us
  starting transfers between devices: 0.09 us -> 59.3 us
  Pallas kernels: 0 us -> 33.3 us
  matrix products: 17.7 us -> 0 us
  between operations: 13.1 us -> 0.14 us
  other arithmetic: 7.46 us -> 2.68 us
    all_gather x2 -> x0, waiting for transfers between devices: 135 us -> none  [the longest x1 77.4 us: body(): amp_rows = lax.all_gather(amp_local, 'outv', axis=1, tiled=True)]
    reduce_scatter x1 -> x0, waiting for transfers between devices: 110 us -> none  [body(): lax.psum_scatter(contract(int_full, amp_rows), 'conv', scatter_dimension=...]
    ppermute x0 -> x29, starting transfers between devices: none -> 59.3 us  [send(): return lax.ppermute(array, AXES, plan)]
    ppermute x0 -> x29, waiting for transfers between devices: none -> 43.9 us  [send(): return lax.ppermute(array, AXES, plan)]
    pallas_call x0 -> x6, Pallas kernels: none -> 33.3 us  [the longest x4 29.2 us: multiply(): pl.pallas_call(kernel, in_specs=specs, out_specs=[pl.BlockSpec(memory_spa...]
    dot_general x3 -> x0, matrix products: 17.7 us -> none  [the longest x1 16.1 us: contract(): lax.dot_general(columns, amp_rows, dims, preferred_element_type=jnp.float32)]
    mul x2 -> x0, other arithmetic: 4.16 us -> none  [the longest x1 2.13 us: body(): amp_local = amplitudes * amp_cols.astype(jnp.bfloat16)]
    convert_element_type x2 -> x0, other arithmetic: 3.27 us -> none  [the longest x1 3.26 us: body(): return summed.astype(jnp.bfloat16)]
  transfers between devices with their start and end apart: 3 -> 29, of which waited for: 3 -> 11; matrix products, arithmetic and copies ran while one was open for 1% -> 1% of each run, Pallas kernels for 0% -> 17%
where the time goes in v1:
time: 143 us
  starting transfers between devices  59.3 us (41%)
  waiting for transfers between devices  43.9 us (31%)
  Pallas kernels  33.3 us (23%)
  local copies, waits for them, and re-layouts  3.87 us (3%)
  other arithmetic  2.68 us (2%)
    ppermute x29, starting transfers between devices, send(): return lax.ppermute(array, AXES, plan)  59.3 us
    ppermute x29, waiting for transfers between devices, send(): return lax.ppermute(array, AXES, plan)  43.9 us
    pallas_call x4, Pallas kernels, multiply(): pl.pallas_call(kernel, in_specs=specs, out_specs=[pl.BlockSpec(memory_spa...  29.2 us
    unnamed x16, local copies, waits for them, and re-layouts  3.2 us
  transfers between devices with their start and end apart: 29, of which 11 were waited for; matrix products, arithmetic and copies ran while one was open for 1% of the time, Pallas kernels for 17%

profile of v1, /device:TPU:24, one launch (start us, length us, event | category | flops | bytes accessed | tf_op | source)
XLA Modules:
  0.0 143.1 jit_solution(2723068781919687853)
XLA Ops:
  0.0 0.7 stack.63.place.refs_0_
  0.7 2.0 %mask_integrals.1 = (bf16[192,768]{1,0:T(8,128)(2,1)}, bf16[192,768]{1,0:T(8,128)(2,1)}) custom-call(s32[6]{0:T(128)} %stack.63.place.refs_0_, s32[16,16]{1,0:T(8,128)} %mask_ref.2, bf16[192,1536]{1,0:T(8,128)(2,1)} %bitcast.17), custom_call_target="tpu_custom_call" | custom-call | tf_op jit(solution)/shard_map/mask_integrals/pallas_call | solution.py:69
  2.7 0.7 collective-permute-start.8
  3.4 2.1 %mask_amplitudes.1 = (bf16[192,1024]{1,0:T(8,128)(2,1)}, bf16[192,1024]{1,0:T(8,128)(2,1)}) custom-call(s32[6]{0:T(128)} %stack.63.place.refs_0_, s32[1,16]{1,0:T(1,128)} %mask_ref.3, bf16[192,2048]{1,0:T(8,128)(2,1)} %bitcast.16), custom_call_target="tpu_custom_call" | custom-call | tf_op jit(solution)/shard_map/mask_amplitudes/pallas_call | solution.py:91
  5.5 3.0 %collective-permute-start.20 = (bf16[192,1024]{1,0:T(8,128)(2,1)}, bf16[192,1024]{1,0:T(8,128)(2,1)S(1)}, u32[]{:S(2)}, u32[]{:S(2)}) collective-permute-start(bf16[192,1024]{1,0:T(8,128)(2,1)} %get-tuple-element.16), channel_id=1, source_target_pairs={{0,2},{1,3},{4,6},{5,7},{8,10},{9,11},{12,14},{13,15},{16,18},{17,... | collective-permute-start | bytes 1179656 | tf_op jit(solution)/shard_map/ppermute | solution.py:48
  8.5 1.9 %collective-permute-start.16 = (bf16[192,1024]{1,0:T(8,128)(2,1)}, bf16[192,1024]{1,0:T(8,128)(2,1)S(1)}, u32[]{:S(2)}, u32[]{:S(2)}) collective-permute-start(bf16[192,1024]{1,0:T(8,128)(2,1)} %get-tuple-element.15), channel_id=1, source_target_pairs={{0,4},{1,29},{4,0},{5,9},{8,12},{9,5},{12,8},{13,17},{16,20},{17,1... | collective-permute-start | bytes 1179656 | tf_op jit(solution)/shard_map/ppermute | solution.py:48
  10.4 0.6 collective-permute-start
  11.0 1.0 pad_maximum_fusion.4.refs_9_
  12.0 1.1 collective-permute-start.12
  13.2 1.4 %collective-permute-start.9 = (bf16[2,192,768]{2,1,0:T(8,128)(2,1)S(1)}, bf16[2,192,768]{2,1,0:T(8,128)(2,1)S(1)}, u32[]{:S(2)}, u32[]{:S(2)}) collective-permute-start(bf16[2,192,768]{2,1,0:T(8,128)(2,1)S(1)} %pad_maximum_fusion.4.refs_9_), channel_id=1, source_target_pairs={{0,128},{1,131},{4,132},{5,135},{8,136},{9,139},{12,140},{13,143},... | collective-permute-start | bytes 1769480 | tf_op jit(solution)/shard_map/ppermute | solution.py:48
  14.6 2.8 %collective-permute-done.20 = bf16[192,1024]{1,0:T(8,128)(2,1)S(1)} collective-permute-done((bf16[192,1024]{1,0:T(8,128)(2,1)}, bf16[192,1024]{1,0:T(8,128)(2,1)S(1)}, u32[]{:S(2)}, u32[]{:S(2)}) %collective-permute-start.20) | collective-permute-done | bytes 393248 | tf_op jit(solution)/shard_map/ppermute | solution.py:48
  17.4 2.0 %collective-permute-start.21 = (bf16[192,1024]{1,0:T(8,128)(2,1)S(1)}, bf16[192,1024]{1,0:T(8,128)(2,1)S(1)}, u32[]{:S(2)}, u32[]{:S(2)}) collective-permute-start(bf16[192,1024]{1,0:T(8,128)(2,1)S(1)} %collective-permute-done.20), channel_id=1, source_target_pairs={{0,4},{1,29},{4,0},{5,9},{8,12},{9,5},{12,8},{13,17},{16,20},{17,1... | collective-permute-start | bytes 1179656 | tf_op jit(solution)/shard_map/ppermute | solution.py:48
  19.4 1.3 collective-permute-done
  20.6 1.5 %collective-permute-start.10 = (bf16[2,192,768]{2,1,0:T(8,128)(2,1)S(1)}, bf16[2,192,768]{2,1,0:T(8,128)(2,1)S(1)}, u32[]{:S(2)}, u32[]{:S(2)}) collective-permute-start(bf16[2,192,768]{2,1,0:T(8,128)(2,1)S(1)} %pad_maximum_fusion.4.refs_9_), channel_id=1, source_target_pairs={{0,130},{1,129},{4,134},{5,133},{8,138},{9,137},{12,142},{13,141},... | collective-permute-start | bytes 1769480 | tf_op jit(solution)/shard_map/ppermute | solution.py:48
  22.2 1.8 %collective-permute-start.4 = (bf16[2,192,768]{2,1,0:T(8,128)(2,1)S(1)}, bf16[2,192,768]{2,1,0:T(8,128)(2,1)S(1)}, u32[]{:S(2)}, u32[]{:S(2)}) collective-permute-start(bf16[2,192,768]{2,1,0:T(8,128)(2,1)S(1)} %pad_maximum_fusion.3.refs_1_), channel_id=1, source_target_pairs={{0,130},{1,129},{4,134},{5,133},{8,138},{9,137},{12,142},{13,141},... | collective-permute-start | bytes 1769480 | tf_op jit(solution)/shard_map/ppermute | solution.py:48
  24.1 1.0 collective-permute-done.21
  25.2 0.9 collective-permute-start.1
  26.1 6.0 %collective-permute-start.17 = (bf16[2,192,1024]{2,1,0:T(8,128)(2,1)S(1)}, bf16[2,192,1024]{2,1,0:T(8,128)(2,1)S(1)}, u32[]{:S(2)}, u32[]{:S(2)}) collective-permute-start(bf16[2,192,1024]{2,1,0:T(8,128)(2,1)S(1)} %pad_maximum_fusion.1.refs_17_), channel_id=1, source_target_pairs={{0,28},{1,5},{4,8},{5,1},{8,4},{9,13},{12,16},{13,9},{16,12},{17,2... | collective-permute-start | bytes 2359304 | tf_op jit(solution)/shard_map/ppermute | solution.py:48
  32.1 4.4 %collective-permute-start.22 = (bf16[2,192,1024]{2,1,0:T(8,128)(2,1)S(1)}, bf16[2,192,1024]{2,1,0:T(8,128)(2,1)S(1)}, u32[]{:S(2)}, u32[]{:S(2)}) collective-permute-start(bf16[2,192,1024]{2,1,0:T(8,128)(2,1)S(1)} %pad_maximum_fusion.2.refs_21_), channel_id=1, source_target_pairs={{0,28},{1,5},{4,8},{5,1},{8,4},{9,13},{12,16},{13,9},{16,12},{17,2... | collective-permute-start | bytes 2359304 | tf_op jit(solution)/shard_map/ppermute | solution.py:48
  36.5 3.0 %collective-permute-done.4.refs_5_ = bf16[2,192,768]{2,1,0:T(8,128)(2,1)S(1)} collective-permute-done((bf16[2,192,768]{2,1,0:T(8,128)(2,1)S(1)}, bf16[2,192,768]{2,1,0:T(8,128)(2,1)S(1)}, u32[]{:S(2)}, u32[]{:S(2)}) %collective-permute-start.4) | collective-permute-done | bytes 589856 | tf_op jit(solution)/shard_map/ppermute | solution.py:48
  39.5 2.9 %collective-permute-start.2 = (bf16[2,192,768]{2,1,0:T(8,128)(2,1)S(1)}, bf16[2,192,768]{2,1,0:T(8,128)(2,1)S(1)}, u32[]{:S(2)}, u32[]{:S(2)}) collective-permute-start(bf16[2,192,768]{2,1,0:T(8,128)(2,1)S(1)} %pad_maximum_fusion.3.refs_1_), channel_id=1, source_target_pairs={{0,96},{1,33},{4,100},{5,37},{8,104},{9,41},{12,108},{13,45},{16,1... | collective-permute-start | bytes 1769480 | tf_op jit(solution)/shard_map/ppermute | solution.py:48
  42.4 1.5 %collective-permute-start.13 = (bf16[2,192,768]{2,1,0:T(8,128)(2,1)S(1)}, bf16[2,192,768]{2,1,0:T(8,128)(2,1)S(1)}, u32[]{:S(2)}, u32[]{:S(2)}) collective-permute-start(bf16[2,192,768]{2,1,0:T(8,128)(2,1)S(1)} %collective-permute-done.12.refs_13_), channel_id=1, source_target_pairs={{0,128},{1,131},{4,132},{5,135},{8,136},{9,139},{12,140},{13,143},... | collective-permute-start | bytes 1769480 | tf_op jit(solution)/shard_map/ppermute | solution.py:48
  43.9 2.1 %collective-permute-start.11 = (bf16[2,192,768]{2,1,0:T(8,128)(2,1)S(1)}, bf16[2,192,768]{2,1,0:T(8,128)(2,1)S(1)}, u32[]{:S(2)}, u32[]{:S(2)}) collective-permute-start(bf16[2,192,768]{2,1,0:T(8,128)(2,1)S(1)} %collective-permute-done.9.refs_10_), channel_id=1, source_target_pairs={{0,130},{1,129},{4,134},{5,133},{8,138},{9,137},{12,142},{13,141},... | collective-permute-start | bytes 1769480 | tf_op jit(solution)/shard_map/ppermute | solution.py:48
  46.0 1.9 %collective-permute-start.18 = (bf16[2,192,1024]{2,1,0:T(8,128)(2,1)S(1)}, bf16[2,192,1024]{2,1,0:T(8,128)(2,1)S(1)}, u32[]{:S(2)}, u32[]{:S(2)}) collective-permute-start(bf16[2,192,1024]{2,1,0:T(8,128)(2,1)S(1)} %collective-permute-done.17.refs_18_), channel_id=1, source_target_pairs={{0,4},{1,29},{4,0},{5,9},{8,12},{9,5},{12,8},{13,17},{16,20},{17,1... | collective-permute-start | bytes 2359304 | tf_op jit(solution)/shard_map/ppermute | solution.py:48
  47.9 4.7 %collective-permute-done.22.refs_22_ = bf16[2,192,1024]{2,1,0:T(8,128)(2,1)S(1)} collective-permute-done((bf16[2,192,1024]{2,1,0:T(8,128)(2,1)S(1)}, bf16[2,192,1024]{2,1,0:T(8,128)(2,1)S(1)}, u32[]{:S(2)}, u32[]{:S(2)}) %collective-permute-start.22) | collective-permute-done | bytes 786464 | tf_op jit(solution)/shard_map/ppermute | solution.py:48
  52.6 3.5 %collective-permute-start.14 = (bf16[2,192,768]{2,1,0:T(8,128)(2,1)S(1)}, bf16[2,192,768]{2,1,0:T(8,128)(2,1)S(1)}, u32[]{:S(2)}, u32[]{:S(2)}) collective-permute-start(bf16[2,192,768]{2,1,0:T(8,128)(2,1)S(1)} %collective-permute-done.12.refs_13_), channel_id=1, source_target_pairs={{0,130},{1,129},{4,134},{5,133},{8,138},{9,137},{12,142},{13,141},... | collective-permute-start | bytes 1769480 | tf_op jit(solution)/shard_map/ppermute | solution.py:48
  56.1 2.1 %collective-permute-start.5 = (bf16[2,192,768]{2,1,0:T(8,128)(2,1)S(1)}, bf16[2,192,768]{2,1,0:T(8,128)(2,1)S(1)}, u32[]{:S(2)}, u32[]{:S(2)}) collective-permute-start(bf16[2,192,768]{2,1,0:T(8,128)(2,1)S(1)} %collective-permute-done.4.refs_5_), channel_id=1, source_target_pairs={{0,32},{1,97},{4,36},{5,101},{8,40},{9,105},{12,44},{13,109},{16,4... | collective-permute-start | bytes 1769480 | tf_op jit(solution)/shard_map/ppermute | solution.py:48
  58.2 1.9 %collective-permute-start.3 = (bf16[2,192,768]{2,1,0:T(8,128)(2,1)S(1)}, bf16[2,192,768]{2,1,0:T(8,128)(2,1)S(1)}, u32[]{:S(2)}, u32[]{:S(2)}) collective-permute-start(bf16[2,192,768]{2,1,0:T(8,128)(2,1)S(1)} %collective-permute-done.1.refs_2_), channel_id=1, source_target_pairs={{0,96},{1,33},{4,100},{5,37},{8,104},{9,41},{12,108},{13,45},{16,1... | collective-permute-start | bytes 1769480 | tf_op jit(solution)/shard_map/ppermute | solution.py:48
  60.1 4.9 %collective-permute-start.19 = (bf16[2,192,1024]{2,1,0:T(8,128)(2,1)S(1)}, bf16[2,192,1024]{2,1,0:T(8,128)(2,1)S(1)}, u32[]{:S(2)}, u32[]{:S(2)}) collective-permute-start(bf16[2,192,1024]{2,1,0:T(8,128)(2,1)S(1)} %collective-permute-done.18.refs_19_), channel_id=1, source_target_pairs={{0,28},{1,5},{4,8},{5,1},{8,4},{9,13},{12,16},{13,9},{16,12},{17,2... | collective-permute-start | bytes 2359304 | tf_op jit(solution)/shard_map/ppermute | solution.py:48
  64.9 8.6 %collective-permute-done.23.refs_23_ = bf16[2,192,1024]{2,1,0:T(8,128)(2,1)S(1)} collective-permute-done((bf16[2,192,1024]{2,1,0:T(8,128)(2,1)S(1)}, bf16[2,192,1024]{2,1,0:T(8,128)(2,1)S(1)}, u32[]{:S(2)}, u32[]{:S(2)}) %collective-permute-start.23) | collective-permute-done | bytes 786464 | tf_op jit(solution)/shard_map/ppermute | solution.py:48
  73.5 2.3 %collective-permute-start.24 = (bf16[2,192,1024]{2,1,0:T(8,128)(2,1)S(1)}, bf16[2,192,1024]{2,1,0:T(8,128)(2,1)S(1)}, u32[]{:S(2)}, u32[]{:S(2)}) collective-permute-start(bf16[2,192,1024]{2,1,0:T(8,128)(2,1)S(1)} %collective-permute-done.23.refs_23_), channel_id=1, source_target_pairs={{0,28},{1,5},{4,8},{5,1},{8,4},{9,13},{12,16},{13,9},{16,12},{17,2... | collective-permute-start | bytes 2359304 | tf_op jit(solution)/shard_map/ppermute | solution.py:48
  75.8 3.3 %collective-permute-start.15 = (bf16[2,192,768]{2,1,0:T(8,128)(2,1)S(1)}, bf16[2,192,768]{2,1,0:T(8,128)(2,1)S(1)}, u32[]{:S(2)}, u32[]{:S(2)}) collective-permute-start(bf16[2,192,768]{2,1,0:T(8,128)(2,1)S(1)} %collective-permute-done.13.refs_14_), channel_id=1, source_target_pairs={{0,130},{1,129},{4,134},{5,133},{8,138},{9,137},{12,142},{13,141},... | collective-permute-start | bytes 1769480 | tf_op jit(solution)/shard_map/ppermute | solution.py:48
  79.1 3.1 %collective-permute-start.7 = (bf16[2,192,768]{2,1,0:T(8,128)(2,1)S(1)}, bf16[2,192,768]{2,1,0:T(8,128)(2,1)S(1)}, u32[]{:S(2)}, u32[]{:S(2)}) collective-permute-start(bf16[2,192,768]{2,1,0:T(8,128)(2,1)S(1)} %collective-permute-done.5.refs_6_), channel_id=1, source_target_pairs={{0,96},{1,33},{4,100},{5,37},{8,104},{9,41},{12,108},{13,45},{16,1... | collective-permute-start | bytes 1769480 | tf_op jit(solution)/shard_map/ppermute | solution.py:48
  82.3 4.6 %collective-permute-done.6.refs_7_ = bf16[2,192,768]{2,1,0:T(8,128)(2,1)S(1)} collective-permute-done((bf16[2,192,768]{2,1,0:T(8,128)(2,1)S(1)}, bf16[2,192,768]{2,1,0:T(8,128)(2,1)S(1)}, u32[]{:S(2)}, u32[]{:S(2)}) %collective-permute-start.6) | collective-permute-done | bytes 589856 | tf_op jit(solution)/shard_map/ppermute | solution.py:48
  87.0 6.2 %collective-permute-done.7.refs_8_ = bf16[2,192,768]{2,1,0:T(8,128)(2,1)S(1)} collective-permute-done((bf16[2,192,768]{2,1,0:T(8,128)(2,1)S(1)}, bf16[2,192,768]{2,1,0:T(8,128)(2,1)S(1)}, u32[]{:S(2)}, u32[]{:S(2)}) %collective-permute-start.7) | collective-permute-done | bytes 589856 | tf_op jit(solution)/shard_map/ppermute | solution.py:48
  93.3 0.9 copy-done.3
  94.1 7.4 %multiply_other.2 = f32[768,512]{1,0:T(8,128)} custom-call(s32[6]{0:T(128)S(1)} %copy-done.1, bf16[2,192,768]{2,1,0:T(8,128)(2,1)S(1)} %pad_maximum_fusion.3.refs_1_, bf16[2,192,768]{2,1,0:T(8,128)(2,1)S(1)} %collective-permute-done.1.refs_2_, bf16[2,192,768]{2,1,0:T(8,128)(2,1)S(1)} %collective-permute-done.2.refs_3_, ...), custom_call_target="tpu_custom_call" | custom-call | flops 2415919104 | bytes 9437184 | tf_op jit(solution)/shard_map/multiply_other/pallas_call | solution.py:202
  101.7 7.4 %multiply_other.3 = f32[768,512]{1,0:T(8,128)} custom-call(s32[6]{0:T(128)S(1)} %copy-done.1, bf16[2,192,768]{2,1,0:T(8,128)(2,1)S(1)} %pad_maximum_fusion.3.refs_1_, bf16[2,192,768]{2,1,0:T(8,128)(2,1)S(1)} %collective-permute-done.1.refs_2_, bf16[2,192,768]{2,1,0:T(8,128)(2,1)S(1)} %collective-permute-done.2.refs_3_, ...), custom_call_target="tpu_custom_call" | custom-call | flops 2415919104 | bytes 9437184 | tf_op jit(solution)/shard_map/multiply_other/pallas_call | solution.py:202
  109.1 0.6 collective-permute-start.27
  109.6 1.2 copy-done.5
  110.8 7.2 %multiply_own.2 = (bf16[384,512]{1,0:T(8,128)(2,1)S(1)}, bf16[384,512]{1,0:T(8,128)(2,1)S(1)}) custom-call(s32[6]{0:T(128)S(1)} %copy-done.1, bf16[2,192,768]{2,1,0:T(8,128)(2,1)S(1)} %pad_maximum_fusion.3.refs_1_, bf16[2,192,768]{2,1,0:T(8,128)(2,1)S(1)} %collective-permute-done.1.refs_2_, bf16[2,192,768]{2,1,0:T(8,128)(2,1)S(1)} %collective-permute-done.2.refs_3_, ...), custom_call_target="tpu_custom_call" | custom-call | flops 2415919104 | bytes 9437184 | tf_op jit(solution)/shard_map/multiply_own/pallas_call | solution.py:202
  118.0 3.0 %collective-permute-start.26 = (bf16[384,512]{1,0:T(8,128)(2,1)S(1)}, bf16[384,512]{1,0:T(8,128)(2,1)S(1)}, u32[]{:S(2)}, u32[]{:S(2)}) collective-permute-start(bf16[384,512]{1,0:T(8,128)(2,1)S(1)} %get-tuple-element.18), channel_id=1, source_target_pairs={{0,2},{1,3},{4,6},{5,7},{8,10},{9,11},{12,14},{13,15},{16,18},{17,... | collective-permute-start | bytes 1179656 | tf_op jit(solution)/shard_map/ppermute | solution.py:48
  121.0 1.1 copy-done.4
  122.1 7.2 %multiply_own.3 = (bf16[384,512]{1,0:T(8,128)(2,1)S(1)}, bf16[384,512]{1,0:T(8,128)(2,1)S(1)}) custom-call(s32[6]{0:T(128)S(1)} %copy-done.1, bf16[2,192,768]{2,1,0:T(8,128)(2,1)S(1)} %pad_maximum_fusion.3.refs_1_, bf16[2,192,768]{2,1,0:T(8,128)(2,1)S(1)} %collective-permute-done.1.refs_2_, bf16[2,192,768]{2,1,0:T(8,128)(2,1)S(1)} %collective-permute-done.2.refs_3_, ...), custom_call_target="tpu_custom_call" | custom-call | flops 2415919104 | bytes 9437184 | tf_op jit(solution)/shard_map/multiply_own/pallas_call | solution.py:202
  129.3 0.7 collective-permute-start.28
  130.0 0.6 collective-permute-done.26
  130.7 11.0 %collective-permute-done.28 = bf16[384,512]{1,0:T(8,128)(2,1)S(1)} collective-permute-done((bf16[384,512]{1,0:T(8,128)(2,1)S(1)}, bf16[384,512]{1,0:T(8,128)(2,1)S(1)}, u32[]{:S(2)}, u32[]{:S(2)}) %collective-permute-start.28) | collective-permute-done | bytes 393248 | tf_op jit(solution)/shard_map/ppermute | solution.py:48
  141.7 1.3 pad_maximum_fusion
  (40 shorter events, 0.6 us)
Async XLA Ops:
  2.7 19.5 %copy-start.7 = (bf16[192,768]{1,0:T(8,128)(2,1)S(1)}, bf16[192,768]{1,0:T(8,128)(2,1)}, u32[]{:S(2)}) copy-start(bf16[192,768]{1,0:T(8,128)(2,1)} %get-tuple-element.13) | copy-start | bytes 884740
  2.7 8.4 %collective-permute-start.8 = (bf16[192,768]{1,0:T(8,128)(2,1)}, bf16[192,768]{1,0:T(8,128)(2,1)S(1)}, u32[]{:S(2)}, u32[]{:S(2)}) collective-permute-start(bf16[192,768]{1,0:T(8,128)(2,1)} %get-tuple-element.14), channel_id=1, source_target_pairs={{0,32},{1,97},{4,36},{5,101},{8,40},{9,105},{12,44},{13,109},{16,4... | collective-permute-start | bytes 884744 | tf_op jit(solution)/shard_map/ppermute | solution.py:48
  5.5 18.6 %copy-start.6 = (bf16[192,1024]{1,0:T(8,128)(2,1)S(1)}, bf16[192,1024]{1,0:T(8,128)(2,1)}, u32[]{:S(2)}) copy-start(bf16[192,1024]{1,0:T(8,128)(2,1)} %get-tuple-element.15) | copy-start | bytes 1179652
  5.5 11.9 %collective-permute-start.20 = (bf16[192,1024]{1,0:T(8,128)(2,1)}, bf16[192,1024]{1,0:T(8,128)(2,1)S(1)}, u32[]{:S(2)}, u32[]{:S(2)}) collective-permute-start(bf16[192,1024]{1,0:T(8,128)(2,1)} %get-tuple-element.16), channel_id=1, source_target_pairs={{0,2},{1,3},{4,6},{5,7},{8,10},{9,11},{12,14},{13,15},{16,18},{17,... | collective-permute-start | bytes 1179656 | tf_op jit(solution)/shard_map/ppermute | solution.py:48
  8.5 13.7 %collective-permute-start.16 = (bf16[192,1024]{1,0:T(8,128)(2,1)}, bf16[192,1024]{1,0:T(8,128)(2,1)S(1)}, u32[]{:S(2)}, u32[]{:S(2)}) collective-permute-start(bf16[192,1024]{1,0:T(8,128)(2,1)} %get-tuple-element.15), channel_id=1, source_target_pairs={{0,4},{1,29},{4,0},{5,9},{8,12},{9,5},{12,8},{13,17},{16,20},{17,1... | collective-permute-start | bytes 1179656 | tf_op jit(solution)/shard_map/ppermute | solution.py:48
  10.4 10.2 %collective-permute-start = (bf16[192,768]{1,0:T(8,128)(2,1)}, bf16[192,768]{1,0:T(8,128)(2,1)S(1)}, u32[]{:S(2)}, u32[]{:S(2)}) collective-permute-start(bf16[192,768]{1,0:T(8,128)(2,1)} %get-tuple-element.13), channel_id=1, source_target_pairs={{0,128},{1,131},{4,132},{5,135},{8,136},{9,139},{12,140},{13,143},... | collective-permute-start | bytes 884744 | tf_op jit(solution)/shard_map/ppermute | solution.py:48
  12.0 14.1 %collective-permute-start.12 = (bf16[2,192,768]{2,1,0:T(8,128)(2,1)S(1)}, bf16[2,192,768]{2,1,0:T(8,128)(2,1)S(1)}, u32[]{:S(2)}, u32[]{:S(2)}) collective-permute-start(bf16[2,192,768]{2,1,0:T(8,128)(2,1)S(1)} %pad_maximum_fusion.4.refs_9_), channel_id=1, source_target_pairs={{0,96},{1,33},{4,100},{5,37},{8,104},{9,41},{12,108},{13,45},{16,1... | collective-permute-start | bytes 1769480 | tf_op jit(solution)/shard_map/ppermute | solution.py:48
  13.2 19.0 %collective-permute-start.9 = (bf16[2,192,768]{2,1,0:T(8,128)(2,1)S(1)}, bf16[2,192,768]{2,1,0:T(8,128)(2,1)S(1)}, u32[]{:S(2)}, u32[]{:S(2)}) collective-permute-start(bf16[2,192,768]{2,1,0:T(8,128)(2,1)S(1)} %pad_maximum_fusion.4.refs_9_), channel_id=1, source_target_pairs={{0,128},{1,131},{4,132},{5,135},{8,136},{9,139},{12,140},{13,143},... | collective-permute-start | bytes 1769480 | tf_op jit(solution)/shard_map/ppermute | solution.py:48
  17.4 7.8 %collective-permute-start.21 = (bf16[192,1024]{1,0:T(8,128)(2,1)S(1)}, bf16[192,1024]{1,0:T(8,128)(2,1)S(1)}, u32[]{:S(2)}, u32[]{:S(2)}) collective-permute-start(bf16[192,1024]{1,0:T(8,128)(2,1)S(1)} %collective-permute-done.20), channel_id=1, source_target_pairs={{0,4},{1,29},{4,0},{5,9},{8,12},{9,5},{12,8},{13,17},{16,20},{17,1... | collective-permute-start | bytes 1179656 | tf_op jit(solution)/shard_map/ppermute | solution.py:48
  20.6 21.7 %collective-permute-start.10 = (bf16[2,192,768]{2,1,0:T(8,128)(2,1)S(1)}, bf16[2,192,768]{2,1,0:T(8,128)(2,1)S(1)}, u32[]{:S(2)}, u32[]{:S(2)}) collective-permute-start(bf16[2,192,768]{2,1,0:T(8,128)(2,1)S(1)} %pad_maximum_fusion.4.refs_9_), channel_id=1, source_target_pairs={{0,130},{1,129},{4,134},{5,133},{8,138},{9,137},{12,142},{13,141},... | collective-permute-start | bytes 1769480 | tf_op jit(solution)/shard_map/ppermute | solution.py:48
  22.2 17.3 %collective-permute-start.4 = (bf16[2,192,768]{2,1,0:T(8,128)(2,1)S(1)}, bf16[2,192,768]{2,1,0:T(8,128)(2,1)S(1)}, u32[]{:S(2)}, u32[]{:S(2)}) collective-permute-start(bf16[2,192,768]{2,1,0:T(8,128)(2,1)S(1)} %pad_maximum_fusion.3.refs_1_), channel_id=1, source_target_pairs={{0,130},{1,129},{4,134},{5,133},{8,138},{9,137},{12,142},{13,141},... | collective-permute-start | bytes 1769480 | tf_op jit(solution)/shard_map/ppermute | solution.py:48
  24.0 70.1 %copy-start.1 = (s32[6]{0:T(128)S(1)}, s32[6]{0:T(128)}, u32[]{:S(2)}) copy-start(s32[6]{0:T(128)} %stack.63.place.refs_0_) | copy-start | bytes 76
  25.2 18.7 %collective-permute-start.1 = (bf16[2,192,768]{2,1,0:T(8,128)(2,1)S(1)}, bf16[2,192,768]{2,1,0:T(8,128)(2,1)S(1)}, u32[]{:S(2)}, u32[]{:S(2)}) collective-permute-start(bf16[2,192,768]{2,1,0:T(8,128)(2,1)S(1)} %pad_maximum_fusion.3.refs_1_), channel_id=1, source_target_pairs={{0,32},{1,97},{4,36},{5,101},{8,40},{9,105},{12,44},{13,109},{16,4... | collective-permute-start | bytes 1769480 | tf_op jit(solution)/shard_map/ppermute | solution.py:48
  26.1 19.8 %collective-permute-start.17 = (bf16[2,192,1024]{2,1,0:T(8,128)(2,1)S(1)}, bf16[2,192,1024]{2,1,0:T(8,128)(2,1)S(1)}, u32[]{:S(2)}, u32[]{:S(2)}) collective-permute-start(bf16[2,192,1024]{2,1,0:T(8,128)(2,1)S(1)} %pad_maximum_fusion.1.refs_17_), channel_id=1, source_target_pairs={{0,28},{1,5},{4,8},{5,1},{8,4},{9,13},{12,16},{13,9},{16,12},{17,2... | collective-permute-start | bytes 2359304 | tf_op jit(solution)/shard_map/ppermute | solution.py:48
  32.1 20.4 %collective-permute-start.22 = (bf16[2,192,1024]{2,1,0:T(8,128)(2,1)S(1)}, bf16[2,192,1024]{2,1,0:T(8,128)(2,1)S(1)}, u32[]{:S(2)}, u32[]{:S(2)}) collective-permute-start(bf16[2,192,1024]{2,1,0:T(8,128)(2,1)S(1)} %pad_maximum_fusion.2.refs_21_), channel_id=1, source_target_pairs={{0,28},{1,5},{4,8},{5,1},{8,4},{9,13},{12,16},{13,9},{16,12},{17,2... | collective-permute-start | bytes 2359304 | tf_op jit(solution)/shard_map/ppermute | solution.py:48
  39.5 13.1 %collective-permute-start.2 = (bf16[2,192,768]{2,1,0:T(8,128)(2,1)S(1)}, bf16[2,192,768]{2,1,0:T(8,128)(2,1)S(1)}, u32[]{:S(2)}, u32[]{:S(2)}) collective-permute-start(bf16[2,192,768]{2,1,0:T(8,128)(2,1)S(1)} %pad_maximum_fusion.3.refs_1_), channel_id=1, source_target_pairs={{0,96},{1,33},{4,100},{5,37},{8,104},{9,41},{12,108},{13,45},{16,1... | collective-permute-start | bytes 1769480 | tf_op jit(solution)/shard_map/ppermute | solution.py:48
  42.4 13.7 %collective-permute-start.13 = (bf16[2,192,768]{2,1,0:T(8,128)(2,1)S(1)}, bf16[2,192,768]{2,1,0:T(8,128)(2,1)S(1)}, u32[]{:S(2)}, u32[]{:S(2)}) collective-permute-start(bf16[2,192,768]{2,1,0:T(8,128)(2,1)S(1)} %collective-permute-done.12.refs_13_), channel_id=1, source_target_pairs={{0,128},{1,131},{4,132},{5,135},{8,136},{9,139},{12,140},{13,143},... | collective-permute-start | bytes 1769480 | tf_op jit(solution)/shard_map/ppermute | solution.py:48
  43.9 14.3 %collective-permute-start.11 = (bf16[2,192,768]{2,1,0:T(8,128)(2,1)S(1)}, bf16[2,192,768]{2,1,0:T(8,128)(2,1)S(1)}, u32[]{:S(2)}, u32[]{:S(2)}) collective-permute-start(bf16[2,192,768]{2,1,0:T(8,128)(2,1)S(1)} %collective-permute-done.9.refs_10_), channel_id=1, source_target_pairs={{0,130},{1,129},{4,134},{5,133},{8,138},{9,137},{12,142},{13,141},... | collective-permute-start | bytes 1769480 | tf_op jit(solution)/shard_map/ppermute | solution.py:48
  46.0 14.1 %collective-permute-start.18 = (bf16[2,192,1024]{2,1,0:T(8,128)(2,1)S(1)}, bf16[2,192,1024]{2,1,0:T(8,128)(2,1)S(1)}, u32[]{:S(2)}, u32[]{:S(2)}) collective-permute-start(bf16[2,192,1024]{2,1,0:T(8,128)(2,1)S(1)} %collective-permute-done.17.refs_18_), channel_id=1, source_target_pairs={{0,4},{1,29},{4,0},{5,9},{8,12},{9,5},{12,8},{13,17},{16,20},{17,1... | collective-permute-start | bytes 2359304 | tf_op jit(solution)/shard_map/ppermute | solution.py:48
  52.6 49.1 %copy-start = (bf16[2,192,1024]{2,1,0:T(8,128)(2,1)}, bf16[2,192,1024]{2,1,0:T(8,128)(2,1)S(1)}, u32[]{:S(2)}) copy-start(bf16[2,192,1024]{2,1,0:T(8,128)(2,1)S(1)} %collective-permute-done.22.refs_22_) | copy-start | bytes 2359300
  52.6 20.9 %collective-permute-start.23 = (bf16[2,192,1024]{2,1,0:T(8,128)(2,1)S(1)}, bf16[2,192,1024]{2,1,0:T(8,128)(2,1)S(1)}, u32[]{:S(2)}, u32[]{:S(2)}) collective-permute-start(bf16[2,192,1024]{2,1,0:T(8,128)(2,1)S(1)} %collective-permute-done.22.refs_22_), channel_id=1, source_target_pairs={{0,4},{1,29},{4,0},{5,9},{8,12},{9,5},{12,8},{13,17},{16,20},{17,1... | collective-permute-start | bytes 2359304 | tf_op jit(solution)/shard_map/ppermute | solution.py:48
  52.6 23.2 %collective-permute-start.14 = (bf16[2,192,768]{2,1,0:T(8,128)(2,1)S(1)}, bf16[2,192,768]{2,1,0:T(8,128)(2,1)S(1)}, u32[]{:S(2)}, u32[]{:S(2)}) collective-permute-start(bf16[2,192,768]{2,1,0:T(8,128)(2,1)S(1)} %collective-permute-done.12.refs_13_), channel_id=1, source_target_pairs={{0,130},{1,129},{4,134},{5,133},{8,138},{9,137},{12,142},{13,141},... | collective-permute-start | bytes 1769480 | tf_op jit(solution)/shard_map/ppermute | solution.py:48
  56.1 19.7 %collective-permute-start.5 = (bf16[2,192,768]{2,1,0:T(8,128)(2,1)S(1)}, bf16[2,192,768]{2,1,0:T(8,128)(2,1)S(1)}, u32[]{:S(2)}, u32[]{:S(2)}) collective-permute-start(bf16[2,192,768]{2,1,0:T(8,128)(2,1)S(1)} %collective-permute-done.4.refs_5_), channel_id=1, source_target_pairs={{0,32},{1,97},{4,36},{5,101},{8,40},{9,105},{12,44},{13,109},{16,4... | collective-permute-start | bytes 1769480 | tf_op jit(solution)/shard_map/ppermute | solution.py:48
  58.2 21.0 %collective-permute-start.3 = (bf16[2,192,768]{2,1,0:T(8,128)(2,1)S(1)}, bf16[2,192,768]{2,1,0:T(8,128)(2,1)S(1)}, u32[]{:S(2)}, u32[]{:S(2)}) collective-permute-start(bf16[2,192,768]{2,1,0:T(8,128)(2,1)S(1)} %collective-permute-done.1.refs_2_), channel_id=1, source_target_pairs={{0,96},{1,33},{4,100},{5,37},{8,104},{9,41},{12,108},{13,45},{16,1... | collective-permute-start | bytes 1769480 | tf_op jit(solution)/shard_map/ppermute | solution.py:48
  60.1 33.2 %collective-permute-start.19 = (bf16[2,192,1024]{2,1,0:T(8,128)(2,1)S(1)}, bf16[2,192,1024]{2,1,0:T(8,128)(2,1)S(1)}, u32[]{:S(2)}, u32[]{:S(2)}) collective-permute-start(bf16[2,192,1024]{2,1,0:T(8,128)(2,1)S(1)} %collective-permute-done.18.refs_19_), channel_id=1, source_target_pairs={{0,28},{1,5},{4,8},{5,1},{8,4},{9,13},{12,16},{13,9},{16,12},{17,2... | collective-permute-start | bytes 2359304 | tf_op jit(solution)/shard_map/ppermute | solution.py:48
  73.5 19.8 %copy-start.2 = (bf16[2,192,1024]{2,1,0:T(8,128)(2,1)}, bf16[2,192,1024]{2,1,0:T(8,128)(2,1)S(1)}, u32[]{:S(2)}) copy-start(bf16[2,192,1024]{2,1,0:T(8,128)(2,1)S(1)} %collective-permute-done.23.refs_23_) | copy-start | bytes 2359300
  73.5 19.8 %collective-permute-start.24 = (bf16[2,192,1024]{2,1,0:T(8,128)(2,1)S(1)}, bf16[2,192,1024]{2,1,0:T(8,128)(2,1)S(1)}, u32[]{:S(2)}, u32[]{:S(2)}) collective-permute-start(bf16[2,192,1024]{2,1,0:T(8,128)(2,1)S(1)} %collective-permute-done.23.refs_23_), channel_id=1, source_target_pairs={{0,28},{1,5},{4,8},{5,1},{8,4},{9,13},{12,16},{13,9},{16,12},{17,2... | collective-permute-start | bytes 2359304 | tf_op jit(solution)/shard_map/ppermute | solution.py:48
  75.8 11.1 %collective-permute-start.6 = (bf16[2,192,768]{2,1,0:T(8,128)(2,1)S(1)}, bf16[2,192,768]{2,1,0:T(8,128)(2,1)S(1)}, u32[]{:S(2)}, u32[]{:S(2)}) collective-permute-start(bf16[2,192,768]{2,1,0:T(8,128)(2,1)S(1)} %collective-permute-done.4.refs_5_), channel_id=1, source_target_pairs={{0,96},{1,33},{4,100},{5,37},{8,104},{9,41},{12,108},{13,45},{16,1... | collective-permute-start | bytes 1769480 | tf_op jit(solution)/shard_map/ppermute | solution.py:48
  75.8 11.2 %collective-permute-start.15 = (bf16[2,192,768]{2,1,0:T(8,128)(2,1)S(1)}, bf16[2,192,768]{2,1,0:T(8,128)(2,1)S(1)}, u32[]{:S(2)}, u32[]{:S(2)}) collective-permute-start(bf16[2,192,768]{2,1,0:T(8,128)(2,1)S(1)} %collective-permute-done.13.refs_14_), channel_id=1, source_target_pairs={{0,130},{1,129},{4,134},{5,133},{8,138},{9,137},{12,142},{13,141},... | collective-permute-start | bytes 1769480 | tf_op jit(solution)/shard_map/ppermute | solution.py:48
  79.1 14.1 %collective-permute-start.7 = (bf16[2,192,768]{2,1,0:T(8,128)(2,1)S(1)}, bf16[2,192,768]{2,1,0:T(8,128)(2,1)S(1)}, u32[]{:S(2)}, u32[]{:S(2)}) collective-permute-start(bf16[2,192,768]{2,1,0:T(8,128)(2,1)S(1)} %collective-permute-done.5.refs_6_), channel_id=1, source_target_pairs={{0,96},{1,33},{4,100},{5,37},{8,104},{9,41},{12,108},{13,45},{16,1... | collective-permute-start | bytes 1769480 | tf_op jit(solution)/shard_map/ppermute | solution.py:48
  93.3 0.9 copy-start.3
  101.6 8.1 %collective-permute-start.25 = (f32[768,512]{1,0:T(8,128)}, f32[768,512]{1,0:T(8,128)S(1)}, u32[]{:S(2)}, u32[]{:S(2)}) collective-permute-start(f32[768,512]{1,0:T(8,128)} %multiply_other.2), channel_id=1, source_target_pairs={{0,1},{1,0},{4,5},{5,4},{8,9},{9,8},{12,13},{13,12},{16,17},{17,16... | collective-permute-start | bytes 4718600 | tf_op jit(solution)/shard_map/ppermute | solution.py:48
  109.1 11.9 %collective-permute-start.27 = (f32[768,512]{1,0:T(8,128)}, f32[768,512]{1,0:T(8,128)S(1)}, u32[]{:S(2)}, u32[]{:S(2)}) collective-permute-start(f32[768,512]{1,0:T(8,128)} %multiply_other.3), channel_id=1, source_target_pairs={{0,1},{1,0},{4,5},{5,4},{8,9},{9,8},{12,13},{13,12},{16,17},{17,16... | collective-permute-start | bytes 4718600 | tf_op jit(solution)/shard_map/ppermute | solution.py:48
  109.6 1.2 copy-start.5
  118.0 12.6 %collective-permute-start.26 = (bf16[384,512]{1,0:T(8,128)(2,1)S(1)}, bf16[384,512]{1,0:T(8,128)(2,1)S(1)}, u32[]{:S(2)}, u32[]{:S(2)}) collective-permute-start(bf16[384,512]{1,0:T(8,128)(2,1)S(1)} %get-tuple-element.18), channel_id=1, source_target_pairs={{0,2},{1,3},{4,6},{5,7},{8,10},{9,11},{12,14},{13,15},{16,18},{17,... | collective-permute-start | bytes 1179656 | tf_op jit(solution)/shard_map/ppermute | solution.py:48
  121.0 1.1 copy-start.4
  129.3 12.4 %collective-permute-start.28 = (bf16[384,512]{1,0:T(8,128)(2,1)S(1)}, bf16[384,512]{1,0:T(8,128)(2,1)S(1)}, u32[]{:S(2)}, u32[]{:S(2)}) collective-permute-start(bf16[384,512]{1,0:T(8,128)(2,1)S(1)} %get-tuple-element.20), channel_id=1, source_target_pairs={{0,2},{1,3},{4,6},{5,7},{8,10},{9,11},{12,14},{13,15},{16,18},{17,... | collective-permute-start | bytes 1179656 | tf_op jit(solution)/shard_map/ppermute | solution.py:48

commit v2 on v1

v2 whole, which is shorter than its diff:
```python
import jax
import jax.numpy as jnp
from jax import lax
from jax.experimental import pallas as pl
from jax.experimental.pallas import tpu as pltpu
from jax.sharding import PartitionSpec as P

TW = 96
AXES = ("pair", "outv", "conv")
NX, NY, NZ = 4, 4, 8
RCHUNKS = 2
MIB = 1024 * 1024
VMEM = pltpu.MemorySpace.VMEM
SMEM = pltpu.MemorySpace.SMEM


def index_of(x, y, z, c):
    x, y, z = x % NX, y % NY, z % NZ
    return ((x % 2) * NY + y) * (NZ * 4) + z * 4 + (x // 2) * 2 + c


def moves(target):
    return [
        (index_of(x, y, z, c), index_of(*target(x, y, z, c)))
        for x in range(NX)
        for y in range(NY)
        for z in range(NZ)
        for c in range(2)
    ]


def sign(i, c):
    return 1 - 2 * ((i + c) % 2)


X_FIRST = moves(lambda x, y, z, c: (x + sign(x, c), y, z, c))
X_OTHER = moves(lambda x, y, z, c: (x - sign(x, c), y, z, c))
Y_FIRST = moves(lambda x, y, z, c: (x, y + sign(y, c), z, c))
Y_OTHER = moves(lambda x, y, z, c: (x, y - sign(y, c), z, c))
Z_FIRST = moves(lambda x, y, z, c: (x, y, z + sign(z, c), c))
Z_OTHER = moves(lambda x, y, z, c: (x, y, z - sign(z, c), c))
X_ACROSS = moves(lambda x, y, z, c: (x + 2, y, z, c))
CORE = moves(lambda x, y, z, c: (x, y, z, 1 - c))
RING4 = (0, 1, -1, -2)
RING8 = (0, 1, -1, -2, 2, 3, -3, -4)


def send(array, plan):
    return lax.ppermute(array, AXES, plan)


def mask_integrals_kernel(place, mask_ref, int_ref, first_ref, second_ref):
    width = int_ref.shape[1]
    half = width // 2
    tile = lax.broadcasted_iota(jnp.int32, (8, width), 1) // TW
    for j in range(int_ref.shape[0] // TW):
        column = place[0] * (int_ref.shape[0] // TW) + j
        row = jnp.zeros((8, width), jnp.float32)
        for k in range(width // TW):
            row = jnp.where(tile == k, mask_ref[k, column].astype(jnp.float32), row)
        row = row[0:1, :].astype(jnp.bfloat16)
        rows = pl.ds(j * TW, TW)
        first_ref[rows, :] = int_ref[rows, :half] * row[:, :half]
        second_ref[rows, :] = int_ref[rows, half:] * row[:, half:]


def mask_integrals(place, int_mask, int_t):
    rows, width = int_t.shape
    shape = jax.ShapeDtypeStruct((rows, width // 2), jnp.bfloat16)
    return pl.pallas_call(
        mask_integrals_kernel,
        in_specs=[pl.BlockSpec(memory_space=SMEM), pl.BlockSpec(memory_space=SMEM), pl.BlockSpec(memory_space=VMEM)],
        out_specs=[pl.BlockSpec(memory_space=VMEM)] * 2,
        out_shape=[shape, shape],
        compiler_params=pltpu.CompilerParams(vmem_limit_bytes=8 * MIB),
        name="mask_integrals",
    )(place, int_mask, int_t)


def mask_amplitudes_kernel(place, mask_ref, amp_ref, keep_ref, give_ref):
    width = keep_ref.shape[2]
    for j in range(amp_ref.shape[0] // TW):
        value = mask_ref[0, place[1] * (amp_ref.shape[0] // TW) + j].astype(jnp.float32)
        rows = pl.ds(j * TW, TW)
        row = jnp.full((1, width), value, jnp.float32).astype(jnp.bfloat16)
        for out_ref, side in ((keep_ref, place[2]), (give_ref, 1 - place[2])):
            for r in range(RCHUNKS):
                first = (side * RCHUNKS + r) * width
                out_ref[r, rows, :] = amp_ref[rows, pl.ds(pl.multiple_of(first, 128), width)] * row


def mask_amplitudes(place, amp_mask, amp_t):
    rows, width = amp_t.shape
    shape = jax.ShapeDtypeStruct((RCHUNKS, rows, width // (2 * RCHUNKS)), jnp.bfloat16)
    return pl.pallas_call(
        mask_amplitudes_kernel,
        in_specs=[pl.BlockSpec(memory_space=SMEM), pl.BlockSpec(memory_space=SMEM), pl.BlockSpec(memory_space=VMEM)],
        out_specs=[pl.BlockSpec(memory_space=VMEM)] * 2,
        out_shape=[shape] * 2,
        compiler_params=pltpu.CompilerParams(vmem_limit_bytes=8 * MIB),
        name="mask_amplitudes",
    )(place, amp_mask, amp_t)


def ring_of_eight(near):
    second = send(near, Z_OTHER)
    third = send(second, Z_FIRST)
    fourth = send(third, Z_OTHER)
    return [near, second, third, fourth]


def plane(own, first_axis, second_axis):
    near = jnp.stack([own, send(own, first_axis[0])])
    far = send(near, first_axis[1])
    pieces = []
    for group in (near, far):
        both = jnp.concatenate([group, send(group, second_axis[0])])
        pieces += [both, send(both, second_axis[1])]
    return pieces


def order_amplitudes_kernel(first_step, steps, place, *refs):
    pieces = refs[:steps]
    out_ref, sems = refs[-2:]
    z, x_hi, c = place[1], place[2], place[5]
    rows = pieces[0].shape[1]
    sz = 1 - 2 * ((z + c) % 2)
    copies = []
    for step, piece in enumerate(pieces):
        for chain in range(2):
            hi = x_hi if chain == 0 else 1 - x_hi
            for e in range(2):
                z_from = (z + sz * RING8[2 * (first_step + step) + e] + NZ) % NZ
                row = pl.multiple_of((hi * NZ + z_from) * rows, rows)
                copies.append(
                    pltpu.make_async_copy(
                        piece.at[2 * chain + e], out_ref.at[pl.ds(row, rows), :], sems.at[len(copies)]
                    )
                )
    for copy in copies:
        copy.start()
    for copy in copies:
        copy.wait()


def order_amplitudes(place, pieces):
    _, rows, width = pieces[0].shape
    any_spec, vmem_spec = pl.BlockSpec(memory_space=pl.ANY), pl.BlockSpec(memory_space=VMEM)
    out = pltpu.VMEM((16 * rows, width), jnp.bfloat16)
    held = None
    for first, steps in ((0, 3), (3, 1)):
        args = [place, *pieces[first : first + steps]] + ([] if held is None else [held])

        def kernel(*refs, first=first, steps=steps):
            order_amplitudes_kernel(first, steps, *refs)

        held = pl.pallas_call(
            kernel,
            in_specs=[pl.BlockSpec(memory_space=SMEM)] + [any_spec] * steps + [vmem_spec] * (held is not None),
            out_specs=vmem_spec,
            out_shape=out,
            scratch_shapes=[pltpu.SemaphoreType.DMA((4 * steps,))],
            input_output_aliases={} if held is None else {len(args) - 1: 0},
            cost_estimate=pl.CostEstimate(flops=0, bytes_accessed=16 * steps * rows * width, transcendentals=0),
            compiler_params=pltpu.CompilerParams(vmem_limit_bytes=MIB),
            name="order_amplitudes",
        )(*args)
    return held


def order_integrals_kernel(got, place, *refs):
    pieces = refs[:4]
    outs, sems = refs[-3:-1], refs[-1]
    x, y, c, x_hi = place[3], place[4], place[5], place[2]
    sx, sy = 1 - 2 * ((x + c) % 2), 1 - 2 * ((y + c) % 2)
    rows, depth = pieces[0].shape[1:]
    copies = []
    for half in range(2):
        for group in range(2):
            for step in range(2):
                for e in range(2):
                    near, far = RING4[2 * group + e], RING4[2 * got + step]
                    dx, dy = (near, far) if half == 0 else (far, near)
                    x_from, y_from = (x + sx * dx + NX) % NX, (y + sy * dy + NY) % NY
                    side = (x_from % 2 + x_hi + 1) % 2
                    row = pl.multiple_of((side * 2 + y_from % 2) * rows, rows)
                    col = pl.multiple_of((x_from // 2) * 2 * depth + half * depth, 128)
                    for own in range(2):
                        copy = pltpu.make_async_copy(
                            pieces[half * 2 + group].at[step * 2 + e],
                            outs[own].at[pl.ds(row, rows), pl.ds(col, depth)],
                            sems.at[len(copies)],
                        )
                        copies.append((y_from // 2 == (c if own else 1 - c), copy))
    for here, copy in copies:
        pl.when(here)(copy.start)
    for here, copy in copies:
        pl.when(here)(copy.wait)


def order_integrals(place, ints):
    any_spec, vmem_spec = pl.BlockSpec(memory_space=pl.ANY), pl.BlockSpec(memory_space=VMEM)
    out = pltpu.VMEM((768, 3072), jnp.bfloat16)
    held = []
    for got in range(2):
        args = [place, *ints[got::2], *held]

        def kernel(*refs, got=got):
            order_integrals_kernel(got, *refs)

        held = pl.pallas_call(
            kernel,
            in_specs=[pl.BlockSpec(memory_space=SMEM)] + [any_spec] * 4 + [vmem_spec] * len(held),
            out_specs=[vmem_spec] * 2,
            out_shape=[out] * 2,
            scratch_shapes=[pltpu.SemaphoreType.DMA((32,))],
            input_output_aliases={5: 0, 6: 1} if held else {},
            cost_estimate=pl.CostEstimate(flops=0, bytes_accessed=2 * 768 * 3072 * 2, transcendentals=0),
            compiler_params=pltpu.CompilerParams(vmem_limit_bytes=MIB),
            name="order_integrals",
        )(*args)
    return held


def multiply_kernel(own, int_ref, amp_ref, *refs):
    rows = 384
    for part in range(2):
        src = pl.ds(part * rows, rows)
        total = jnp.dot(int_ref[src, :], amp_ref[...], preferred_element_type=jnp.float32)
        if own:
            other_ref, outs = refs[0], refs[1:]
            outs[part][...] = (total + other_ref[src, :]).astype(jnp.bfloat16)
        else:
            refs[0][src, :] = total


def multiply(own, ints, amps, other=None):
    width = amps.shape[1]
    if own:
        shapes = [jax.ShapeDtypeStruct((384, width), jnp.bfloat16)] * 2
    else:
        shapes = [jax.ShapeDtypeStruct((768, width), jnp.float32)]
    vmem_spec = pl.BlockSpec(memory_space=VMEM)
    args = [ints, amps] + ([other] if own else [])

    def kernel(*refs):
        multiply_kernel(own, *refs)

    return pl.pallas_call(
        kernel,
        in_specs=[vmem_spec] * len(args),
        out_specs=[vmem_spec] * len(shapes),
        out_shape=shapes,
        cost_estimate=pl.CostEstimate(
            flops=2 * 768 * 3072 * width, bytes_accessed=768 * 3072 * 2 + 3072 * width * 2 + 768 * width * 4, transcendentals=0
        ),
        compiler_params=pltpu.CompilerParams(vmem_limit_bytes=12 * MIB),
        name="multiply_own" if own else "multiply_other",
    )(*args)


def body(amplitudes, integrals, amp_mask, int_mask):
    pair, z, conv = (lax.axis_index(name) for name in AXES)
    x_hi, core = conv // 2, conv % 2
    x_lo, y = pair // NY, pair % NY
    place = jnp.stack([pair, z, x_hi, x_hi * 2 + x_lo, y, core]).astype(jnp.int32)

    first, second = mask_integrals(place, int_mask, integrals.T)
    place, first, second = lax.optimization_barrier((place, first, second))
    keep, give = mask_amplitudes(place, amp_mask, amplitudes.T)
    keep_got = send(keep, Z_FIRST)
    partner = send(give, X_ACROSS)
    partner_got = send(partner, Z_FIRST)
    ints = plane(first, (X_FIRST, X_OTHER), (Y_FIRST, Y_OTHER)) + plane(second, (Y_FIRST, Y_OTHER), (X_FIRST, X_OTHER))
    amps = [
        order_amplitudes(place, ring_of_eight(jnp.stack([keep[r], keep_got[r], partner[r], partner_got[r]])))
        for r in range(RCHUNKS)
    ]
    other_ints, own_ints = order_integrals(place, ints)

    kept, received = [], []
    for columns in amps:
        (partial,) = multiply(False, other_ints, columns)
        theirs, mine = multiply(True, own_ints, columns, send(partial, CORE))
        kept.append(mine)
        received.append(send(theirs, X_ACROSS))
    low = [jnp.where(x_hi == 0, k, g) for k, g in zip(kept, received)]
    high = [jnp.where(x_hi == 0, g, k) for k, g in zip(kept, received)]
    return jnp.concatenate(low + high, axis=1)


def solution(mesh):
    placed = (
        P("pair", ("conv", "outv")),
        P("conv", ("outv", "pair")),
        P("pair", "conv"),
        P("conv", "outv"),
    )
    return jax.shard_map(
        body, mesh=mesh, in_specs=placed, out_specs=P(("outv", "conv"), "pair"), check_vma=False
    )
```

time: 143 us -> 134 us (0.937); the launches traced: 143 us -> 132 us
  starting transfers between devices: 59.3 us -> 49.2 us
  Pallas kernels: 33.3 us -> 25.4 us
  waiting for transfers between devices: 43.9 us -> 51.1 us
    ppermute x29 -> x25, starting transfers between devices: 59.3 us -> 49.2 us  [send(): return lax.ppermute(array, AXES, plan)]
    ppermute x29 -> x25, waiting for transfers between devices: 43.9 us -> 51.1 us  [send(): return lax.ppermute(array, AXES, plan)]
    pallas_call x4 -> x10, Pallas kernels: 29.2 us -> 24 us  [the longest x4 10.7 us: order_amplitudes(): pl.pallas_call(kernel, in_specs=[pl.BlockSpec(memory_space=SMEM)] + [any_...]
    pallas_call x1, Pallas kernels: 2.07 us -> 0.6 us  [mask_amplitudes(): pl.pallas_call(mask_amplitudes_kernel, in_specs=[pl.BlockSpec(memory_spac...]
    unnamed x16 -> x10, local copies, waits for them, and re-layouts: 3.2 us -> 3.63 us
  transfers between devices with their start and end apart: 29 -> 25, of which waited for: 11 -> 8; matrix products, arithmetic and copies ran while one was open for 1% -> 1% of each run, Pallas kernels for 17% -> 19%
where the time goes in v2:
time: 134 us; the launch traced here: 132 us
  waiting for transfers between devices  51.1 us (38%)
  starting transfers between devices  49.2 us (37%)
  Pallas kernels  25.4 us (19%)
  local copies, waits for them, and re-layouts  3.9 us (3%)
  other arithmetic  2 us (1%)
    ppermute x25, waiting for transfers between devices, send(): return lax.ppermute(array, AXES, plan)  51.1 us
    ppermute x25, starting transfers between devices, send(): return lax.ppermute(array, AXES, plan)  49.2 us
    pallas_call x4, Pallas kernels, order_amplitudes(): pl.pallas_call(kernel, in_specs=[pl.BlockSpec(memory_space=SMEM)] + [any_...  10.7 us
    pallas_call x4, Pallas kernels, multiply(): pl.pallas_call(kernel, in_specs=[vmem_spec] * len(args), out_specs=[vmem_...  10.4 us
    unnamed x10, local copies, waits for them, and re-layouts  3.63 us
    pallas_call x2, Pallas kernels, order_integrals(): pl.pallas_call(kernel, in_specs=[pl.BlockSpec(memory_space=SMEM)] + [any_...  2.96 us
  transfers between devices with their start and end apart: 25, of which 8 were waited for; matrix products, arithmetic and copies ran while one was open for 1% of the time, Pallas kernels for 19%

profile of v2, /device:TPU:24, one launch (start us, length us, event | category | flops | bytes accessed | tf_op | source)
XLA Modules:
  0.0 132.0 jit_solution(4800938030487876717)
XLA Ops:
  0.1 1.1 copy-done.1
  1.2 0.7 copy-done.2
  1.8 0.8 mask_integrals.1
  2.7 1.6 %collective-permute-start = (bf16[192,768]{1,0:T(8,128)(2,1)S(1)}, bf16[192,768]{1,0:T(8,128)(2,1)S(1)}, u32[]{:S(2)}, u32[]{:S(2)}) collective-permute-start(bf16[192,768]{1,0:T(8,128)(2,1)S(1)} %get-tuple-element.23), channel_id=1, source_target_pairs={{0,128},{1,131},{4,132},{5,135},{8,136},{9,139},{12,140},{13,143},... | collective-permute-start | bytes 884744 | tf_op jit(solution)/shard_map/ppermute | solution.py:49
  4.2 0.7 collective-permute-start.6
  5.0 1.1 copy-done
  6.1 0.7 copy-done.3
  6.8 0.6 mask_amplitudes.1
  7.4 2.8 %collective-permute-start.13 = (bf16[2,192,512]{2,1,0:T(8,128)(2,1)S(1)}, bf16[2,192,512]{2,1,0:T(8,128)(2,1)S(1)}, u32[]{:S(2)}, u32[]{:S(2)}) collective-permute-start(bf16[2,192,512]{2,1,0:T(8,128)(2,1)S(1)} %get-tuple-element.29), channel_id=1, source_target_pairs={{0,2},{1,3},{4,6},{5,7},{8,10},{9,11},{12,14},{13,15},{16,18},{17,... | collective-permute-start | bytes 1179656 | tf_op jit(solution)/shard_map/ppermute | solution.py:49
  10.2 1.9 %collective-permute-start.12 = (bf16[2,192,512]{2,1,0:T(8,128)(2,1)S(1)}, bf16[2,192,512]{2,1,0:T(8,128)(2,1)S(1)}, u32[]{:S(2)}, u32[]{:S(2)}) collective-permute-start(bf16[2,192,512]{2,1,0:T(8,128)(2,1)S(1)} %get-tuple-element.28), channel_id=1, source_target_pairs={{0,4},{1,29},{4,0},{5,9},{8,12},{9,5},{12,8},{13,17},{16,20},{17,1... | collective-permute-start | bytes 1179656 | tf_op jit(solution)/shard_map/ppermute | solution.py:49
  12.2 1.4 %collective-permute-start.1 = (bf16[2,192,768]{2,1,0:T(8,128)(2,1)S(1)}, bf16[2,192,768]{2,1,0:T(8,128)(2,1)S(1)}, u32[]{:S(2)}, u32[]{:S(2)}) collective-permute-start(bf16[2,192,768]{2,1,0:T(8,128)(2,1)S(1)} %pad_maximum_fusion.5), channel_id=1, source_target_pairs={{0,32},{1,97},{4,36},{5,101},{8,40},{9,105},{12,44},{13,109},{16,4... | collective-permute-start | bytes 1769480 | tf_op jit(solution)/shard_map/ppermute | solution.py:49
  13.6 0.5 collective-permute-start.3
  14.1 0.4 collective-permute-start.7
  14.5 5.7 %collective-permute-done.13 = bf16[2,192,512]{2,1,0:T(8,128)(2,1)S(1)} collective-permute-done((bf16[2,192,512]{2,1,0:T(8,128)(2,1)S(1)}, bf16[2,192,512]{2,1,0:T(8,128)(2,1)S(1)}, u32[]{:S(2)}, u32[]{:S(2)}) %collective-permute-start.13) | collective-permute-done | bytes 393248 | tf_op jit(solution)/shard_map/ppermute | solution.py:49
  20.2 1.9 %collective-permute-start.14 = (bf16[2,192,512]{2,1,0:T(8,128)(2,1)S(1)}, bf16[2,192,512]{2,1,0:T(8,128)(2,1)S(1)}, u32[]{:S(2)}, u32[]{:S(2)}) collective-permute-start(bf16[2,192,512]{2,1,0:T(8,128)(2,1)S(1)} %collective-permute-done.13), channel_id=1, source_target_pairs={{0,4},{1,29},{4,0},{5,9},{8,12},{9,5},{12,8},{13,17},{16,20},{17,1... | collective-permute-start | bytes 1179656 | tf_op jit(solution)/shard_map/ppermute | solution.py:49
  22.2 1.0 collective-permute-start.9
  23.2 4.8 %collective-permute-done.14 = bf16[2,192,512]{2,1,0:T(8,128)(2,1)S(1)} collective-permute-done((bf16[2,192,512]{2,1,0:T(8,128)(2,1)S(1)}, bf16[2,192,512]{2,1,0:T(8,128)(2,1)S(1)}, u32[]{:S(2)}, u32[]{:S(2)}) %collective-permute-start.14) | collective-permute-done | bytes 393248 | tf_op jit(solution)/shard_map/ppermute | solution.py:49
  28.1 5.9 %collective-permute-start.20 = (bf16[4,192,512]{2,1,0:T(8,128)(2,1)S(1)}, bf16[4,192,512]{2,1,0:T(8,128)(2,1)S(1)}, u32[]{:S(2)}, u32[]{:S(2)}) collective-permute-start(bf16[4,192,512]{2,1,0:T(8,128)(2,1)S(1)} %pad_maximum_fusion.4.refs_1_), channel_id=1, source_target_pairs={{0,28},{1,5},{4,8},{5,1},{8,4},{9,13},{12,16},{13,9},{16,12},{17,2... | collective-permute-start | bytes 2359304 | tf_op jit(solution)/shard_map/ppermute | solution.py:49
  34.1 0.1 pad_maximum_fusion.1.refs_1_
  34.2 1.0 collective-permute-start.2
  35.3 3.2 %collective-permute-start.15 = (bf16[4,192,512]{2,1,0:T(8,128)(2,1)S(1)}, bf16[4,192,512]{2,1,0:T(8,128)(2,1)S(1)}, u32[]{:S(2)}, u32[]{:S(2)}) collective-permute-start(bf16[4,192,512]{2,1,0:T(8,128)(2,1)S(1)} %pad_maximum_fusion.3.refs_1_), channel_id=1, source_target_pairs={{0,28},{1,5},{4,8},{5,1},{8,4},{9,13},{12,16},{13,9},{16,12},{17,2... | collective-permute-start | bytes 2359304 | tf_op jit(solution)/shard_map/ppermute | solution.py:49
  38.5 1.0 collective-permute-start.4
  39.5 0.2 collective-permute-start.10
  39.8 4.2 %collective-permute-done.20.refs_2_ = bf16[4,192,512]{2,1,0:T(8,128)(2,1)S(1)} collective-permute-done((bf16[4,192,512]{2,1,0:T(8,128)(2,1)S(1)}, bf16[4,192,512]{2,1,0:T(8,128)(2,1)S(1)}, u32[]{:S(2)}, u32[]{:S(2)}) %collective-permute-start.20) | collective-permute-done | bytes 786464 | tf_op jit(solution)/shard_map/ppermute | solution.py:49
  44.0 0.1 pad_maximum_fusion.2.refs_3_
  44.2 8.8 %collective-permute-done.4 = bf16[2,192,768]{2,1,0:T(8,128)(2,1)S(1)} collective-permute-done((bf16[2,192,768]{2,1,0:T(8,128)(2,1)S(1)}, bf16[2,192,768]{2,1,0:T(8,128)(2,1)S(1)}, u32[]{:S(2)}, u32[]{:S(2)}) %collective-permute-start.4) | collective-permute-done | bytes 589856 | tf_op jit(solution)/shard_map/ppermute | solution.py:49
  53.0 0.9 collective-permute-start.8
  53.9 5.4 %collective-permute-done.15.refs_2_ = bf16[4,192,512]{2,1,0:T(8,128)(2,1)S(1)} collective-permute-done((bf16[4,192,512]{2,1,0:T(8,128)(2,1)S(1)}, bf16[4,192,512]{2,1,0:T(8,128)(2,1)S(1)}, u32[]{:S(2)}, u32[]{:S(2)}) %collective-permute-start.15) | collective-permute-done | bytes 786464 | tf_op jit(solution)/shard_map/ppermute | solution.py:49
  59.5 7.2 %collective-permute-start.11 = (bf16[4,192,768]{2,1,0:T(8,128)(2,1)S(1)}, bf16[4,192,768]{2,1,0:T(8,128)(2,1)S(1)}, u32[]{:S(2)}, u32[]{:S(2)}) collective-permute-start(bf16[4,192,768]{2,1,0:T(8,128)(2,1)S(1)} %constant_dynamic-update-slice_fusion.2.refs_4_), channel_id=1, source_target_pairs={{0,130},{1,129},{4,134},{5,133},{8,138},{9,137},{12,142},{13,141},... | collective-permute-start | bytes 3538952 | tf_op jit(solution)/shard_map/ppermute | solution.py:49
  66.6 4.8 %collective-permute-start.22 = (bf16[4,192,512]{2,1,0:T(8,128)(2,1)S(1)}, bf16[4,192,512]{2,1,0:T(8,128)(2,1)S(1)}, u32[]{:S(2)}, u32[]{:S(2)}) collective-permute-start(bf16[4,192,512]{2,1,0:T(8,128)(2,1)S(1)} %collective-permute-done.21.refs_3_), channel_id=1, source_target_pairs={{0,28},{1,5},{4,8},{5,1},{8,4},{9,13},{12,16},{13,9},{16,12},{17,2... | collective-permute-start | bytes 2359304 | tf_op jit(solution)/shard_map/ppermute | solution.py:49
  71.4 7.5 %collective-permute-done.16.refs_3_ = bf16[4,192,512]{2,1,0:T(8,128)(2,1)S(1)} collective-permute-done((bf16[4,192,512]{2,1,0:T(8,128)(2,1)S(1)}, bf16[4,192,512]{2,1,0:T(8,128)(2,1)S(1)}, u32[]{:S(2)}, u32[]{:S(2)}) %collective-permute-start.16) | collective-permute-done | bytes 786464 | tf_op jit(solution)/shard_map/ppermute | solution.py:49
  78.9 3.8 %collective-permute-start.17 = (bf16[4,192,512]{2,1,0:T(8,128)(2,1)S(1)}, bf16[4,192,512]{2,1,0:T(8,128)(2,1)S(1)}, u32[]{:S(2)}, u32[]{:S(2)}) collective-permute-start(bf16[4,192,512]{2,1,0:T(8,128)(2,1)S(1)} %collective-permute-done.16.refs_3_), channel_id=1, source_target_pairs={{0,28},{1,5},{4,8},{5,1},{8,4},{9,13},{12,16},{13,9},{16,12},{17,2... | collective-permute-start | bytes 2359304 | tf_op jit(solution)/shard_map/ppermute | solution.py:49
  82.8 1.5 %order_integrals.2 = (bf16[768,3072]{1,0:T(8,128)(2,1)S(1)}, bf16[768,3072]{1,0:T(8,128)(2,1)S(1)}) custom-call(s32[6]{0:T(128)S(1)} %stack.51.place.refs_0_, bf16[4,192,768]{2,1,0:T(8,128)(2,1)S(1)} %pad_maximum_fusion.1.refs_1_, bf16[4,192,768]{2,1,0:T(8,128)(2,1)S(1)} %constant_dynamic-update-slice_fusion.refs_2_, ...), custom_call_target="tpu_custom_call" | custom-call | bytes 9437184 | tf_op jit(solution)/shard_map/order_integrals/pallas_call | solution.py:211
  84.2 3.7 %order_amplitudes.6.refs_2_ = bf16[3072,512]{1,0:T(8,128)(2,1)S(1)} custom-call(s32[6]{0:T(128)S(1)} %stack.51.place.refs_0_, bf16[4,192,512]{2,1,0:T(8,128)(2,1)S(1)} %pad_maximum_fusion.4.refs_1_, bf16[4,192,512]{2,1,0:T(8,128)(2,1)S(1)} %collective-permute-done.20.refs_2_, bf16[4,192,512]{2,1,0:T(8,128)(2,1)S(1)} %collective-permute-done.21.refs_3_), custom_call_target="tpu_custom_call" | custom-call | bytes 4718592 | tf_op jit(solution)/shard_map/order_amplitudes/pallas_call | solution.py:157
  88.0 1.5 %order_integrals.3 = (bf16[768,3072]{1,0:T(8,128)(2,1)S(1)}, bf16[768,3072]{1,0:T(8,128)(2,1)S(1)}) custom-call(s32[6]{0:T(128)S(1)} %stack.51.place.refs_0_, bf16[4,192,768]{2,1,0:T(8,128)(2,1)S(1)} %collective-permute-done.2.refs_1_, bf16[4,192,768]{2,1,0:T(8,128)(2,1)S(1)} %collective-permute-done.5.refs_2_, ...), custom_call_target="tpu_custom_call", output_to_operand_aliasing={{0}: (5, {}), {1}: (6, {})} | custom-call | bytes 9437184 | tf_op jit(solution)/shard_map/order_integrals/pallas_call | solution.py:211
  89.5 1.6 %order_amplitudes.7.refs_1_ = bf16[3072,512]{1,0:T(8,128)(2,1)S(1)} custom-call(s32[6]{0:T(128)S(1)} %stack.51.place.refs_0_, bf16[4,192,512]{2,1,0:T(8,128)(2,1)S(1)} %collective-permute-done.22.refs_1_, bf16[3072,512]{1,0:T(8,128)(2,1)S(1)} %order_amplitudes.6.refs_2_), custom_call_target="tpu_custom_call", output_to_operand_aliasing={{}: (2, {})} | custom-call | bytes 1572864 | tf_op jit(solution)/shard_map/order_amplitudes/pallas_call | solution.py:157
  91.2 2.6 %multiply_other.3 = f32[768,512]{1,0:T(8,128)S(1)} custom-call(bf16[768,3072]{1,0:T(8,128)(2,1)S(1)} %get-tuple-element.30.refs_0_, bf16[3072,512]{1,0:T(8,128)(2,1)S(1)} %order_amplitudes.7.refs_1_), custom_call_target="tpu_custom_call" | custom-call | flops 2415919104 | bytes 9437184 | tf_op jit(solution)/shard_map/multiply_other/pallas_call | solution.py:249
  93.8 3.7 %order_amplitudes.4.refs_2_ = bf16[3072,512]{1,0:T(8,128)(2,1)S(1)} custom-call(s32[6]{0:T(128)S(1)} %stack.51.place.refs_0_, bf16[4,192,512]{2,1,0:T(8,128)(2,1)S(1)} %pad_maximum_fusion.3.refs_1_, bf16[4,192,512]{2,1,0:T(8,128)(2,1)S(1)} %collective-permute-done.15.refs_2_, bf16[4,192,512]{2,1,0:T(8,128)(2,1)S(1)} %collective-permute-done.16.refs_3_), custom_call_target="tpu_custom_call" | custom-call | bytes 4718592 | tf_op jit(solution)/shard_map/order_amplitudes/pallas_call | solution.py:157
  97.6 1.6 %order_amplitudes.5.refs_1_ = bf16[3072,512]{1,0:T(8,128)(2,1)S(1)} custom-call(s32[6]{0:T(128)S(1)} %stack.51.place.refs_0_, bf16[4,192,512]{2,1,0:T(8,128)(2,1)S(1)} %collective-permute-done.17.refs_1_, bf16[3072,512]{1,0:T(8,128)(2,1)S(1)} %order_amplitudes.4.refs_2_), custom_call_target="tpu_custom_call", output_to_operand_aliasing={{}: (2, {})} | custom-call | bytes 1572864 | tf_op jit(solution)/shard_map/order_amplitudes/pallas_call | solution.py:157
  99.2 2.6 %multiply_other.2 = f32[768,512]{1,0:T(8,128)S(1)} custom-call(bf16[768,3072]{1,0:T(8,128)(2,1)S(1)} %get-tuple-element.30.refs_0_, bf16[3072,512]{1,0:T(8,128)(2,1)S(1)} %order_amplitudes.5.refs_1_), custom_call_target="tpu_custom_call" | custom-call | flops 2415919104 | bytes 9437184 | tf_op jit(solution)/shard_map/multiply_other/pallas_call | solution.py:249
  101.8 0.6 collective-permute-start.18
  102.4 2.6 %multiply_own.3 = (bf16[384,512]{1,0:T(8,128)(2,1)S(1)}, bf16[384,512]{1,0:T(8,128)(2,1)S(1)}) custom-call(bf16[768,3072]{1,0:T(8,128)(2,1)S(1)} %get-tuple-element.27.refs_0_, bf16[3072,512]{1,0:T(8,128)(2,1)S(1)} %order_amplitudes.7.refs_1_, f32[768,512]{1,0:T(8,128)S(1)} %collective-permute-done.23.refs_2_), custom_call_target="tpu_custom_call" | custom-call | flops 2415919104 | bytes 9437184 | tf_op jit(solution)/shard_map/multiply_own/pallas_call | solution.py:249
  105.0 7.8 %collective-permute-start.24 = (bf16[384,512]{1,0:T(8,128)(2,1)S(1)}, bf16[384,512]{1,0:T(8,128)(2,1)S(1)}, u32[]{:S(2)}, u32[]{:S(2)}) collective-permute-start(bf16[384,512]{1,0:T(8,128)(2,1)S(1)} %get-tuple-element.34), channel_id=1, source_target_pairs={{0,2},{1,3},{4,6},{5,7},{8,10},{9,11},{12,14},{13,15},{16,18},{17,... | collective-permute-start | bytes 1179656 | tf_op jit(solution)/shard_map/ppermute | solution.py:49
  112.8 2.6 %multiply_own.2 = (bf16[384,512]{1,0:T(8,128)(2,1)S(1)}, bf16[384,512]{1,0:T(8,128)(2,1)S(1)}) custom-call(bf16[768,3072]{1,0:T(8,128)(2,1)S(1)} %get-tuple-element.27.refs_0_, bf16[3072,512]{1,0:T(8,128)(2,1)S(1)} %order_amplitudes.5.refs_1_, f32[768,512]{1,0:T(8,128)S(1)} %collective-permute-done.18.refs_2_), custom_call_target="tpu_custom_call" | custom-call | flops 2415919104 | bytes 9437184 | tf_op jit(solution)/shard_map/multiply_own/pallas_call | solution.py:249
  115.4 0.4 collective-permute-start.19
  115.9 6.9 %collective-permute-done.24 = bf16[384,512]{1,0:T(8,128)(2,1)S(1)} collective-permute-done((bf16[384,512]{1,0:T(8,128)(2,1)S(1)}, bf16[384,512]{1,0:T(8,128)(2,1)S(1)}, u32[]{:S(2)}, u32[]{:S(2)}) %collective-permute-start.24) | collective-permute-done | bytes 393248 | tf_op jit(solution)/shard_map/ppermute | solution.py:49
  122.8 7.8 %collective-permute-done.19 = bf16[384,512]{1,0:T(8,128)(2,1)S(1)} collective-permute-done((bf16[384,512]{1,0:T(8,128)(2,1)S(1)}, bf16[384,512]{1,0:T(8,128)(2,1)S(1)}, u32[]{:S(2)}, u32[]{:S(2)}) %collective-permute-start.19) | collective-permute-done | bytes 393248 | tf_op jit(solution)/shard_map/ppermute | solution.py:49
  130.6 1.3 %pad_maximum_fusion = bf16[384,2048]{1,0:T(8,128)(2,1)} fusion(bf16[384,512]{1,0:T(8,128)(2,1)S(1)} %get-tuple-element.38, bf16[384,512]{1,0:T(8,128)(2,1)S(1)} %get-tuple-element.36, bf16[384,512]{1,0:T(8,128)(2,1)S(1)} %get-tuple-element.37, bf16[384,512]{1,0:T(8,128)(2,1)S(1)} %get-tuple-element.35), kind=kLoop, calls=%fused_computation | loop fusion | flops 6291456 | bytes 3145728 | tf_op jit(solution)/shard_map/concatenate | solution.py:289
  (40 shorter events, 1.0 us)
Async XLA Ops:
  0.1 1.1 copy-start.1
  1.2 0.7 copy-start.2
  2.7 9.5 %collective-permute-start = (bf16[192,768]{1,0:T(8,128)(2,1)S(1)}, bf16[192,768]{1,0:T(8,128)(2,1)S(1)}, u32[]{:S(2)}, u32[]{:S(2)}) collective-permute-start(bf16[192,768]{1,0:T(8,128)(2,1)S(1)} %get-tuple-element.23), channel_id=1, source_target_pairs={{0,128},{1,131},{4,132},{5,135},{8,136},{9,139},{12,140},{13,143},... | collective-permute-start | bytes 884744 | tf_op jit(solution)/shard_map/ppermute | solution.py:49
  4.2 9.8 %collective-permute-start.6 = (bf16[192,768]{1,0:T(8,128)(2,1)S(1)}, bf16[192,768]{1,0:T(8,128)(2,1)S(1)}, u32[]{:S(2)}, u32[]{:S(2)}) collective-permute-start(bf16[192,768]{1,0:T(8,128)(2,1)S(1)} %get-tuple-element.24), channel_id=1, source_target_pairs={{0,32},{1,97},{4,36},{5,101},{8,40},{9,105},{12,44},{13,109},{16,4... | collective-permute-start | bytes 884744 | tf_op jit(solution)/shard_map/ppermute | solution.py:49
  5.0 1.1 copy-start
  6.1 0.7 copy-start.3
  7.4 12.8 %collective-permute-start.13 = (bf16[2,192,512]{2,1,0:T(8,128)(2,1)S(1)}, bf16[2,192,512]{2,1,0:T(8,128)(2,1)S(1)}, u32[]{:S(2)}, u32[]{:S(2)}) collective-permute-start(bf16[2,192,512]{2,1,0:T(8,128)(2,1)S(1)} %get-tuple-element.29), channel_id=1, source_target_pairs={{0,2},{1,3},{4,6},{5,7},{8,10},{9,11},{12,14},{13,15},{16,18},{17,... | collective-permute-start | bytes 1179656 | tf_op jit(solution)/shard_map/ppermute | solution.py:49
  10.2 11.9 %collective-permute-start.12 = (bf16[2,192,512]{2,1,0:T(8,128)(2,1)S(1)}, bf16[2,192,512]{2,1,0:T(8,128)(2,1)S(1)}, u32[]{:S(2)}, u32[]{:S(2)}) collective-permute-start(bf16[2,192,512]{2,1,0:T(8,128)(2,1)S(1)} %get-tuple-element.28), channel_id=1, source_target_pairs={{0,4},{1,29},{4,0},{5,9},{8,12},{9,5},{12,8},{13,17},{16,20},{17,1... | collective-permute-start | bytes 1179656 | tf_op jit(solution)/shard_map/ppermute | solution.py:49
  12.2 21.8 %collective-permute-start.1 = (bf16[2,192,768]{2,1,0:T(8,128)(2,1)S(1)}, bf16[2,192,768]{2,1,0:T(8,128)(2,1)S(1)}, u32[]{:S(2)}, u32[]{:S(2)}) collective-permute-start(bf16[2,192,768]{2,1,0:T(8,128)(2,1)S(1)} %pad_maximum_fusion.5), channel_id=1, source_target_pairs={{0,32},{1,97},{4,36},{5,101},{8,40},{9,105},{12,44},{13,109},{16,4... | collective-permute-start | bytes 1769480 | tf_op jit(solution)/shard_map/ppermute | solution.py:49
  13.6 21.7 %collective-permute-start.3 = (bf16[2,192,768]{2,1,0:T(8,128)(2,1)S(1)}, bf16[2,192,768]{2,1,0:T(8,128)(2,1)S(1)}, u32[]{:S(2)}, u32[]{:S(2)}) collective-permute-start(bf16[2,192,768]{2,1,0:T(8,128)(2,1)S(1)} %pad_maximum_fusion.5), channel_id=1, source_target_pairs={{0,130},{1,129},{4,134},{5,133},{8,138},{9,137},{12,142},{13,141},... | collective-permute-start | bytes 1769480 | tf_op jit(solution)/shard_map/ppermute | solution.py:49
  14.1 24.4 %collective-permute-start.7 = (bf16[2,192,768]{2,1,0:T(8,128)(2,1)S(1)}, bf16[2,192,768]{2,1,0:T(8,128)(2,1)S(1)}, u32[]{:S(2)}, u32[]{:S(2)}) collective-permute-start(bf16[2,192,768]{2,1,0:T(8,128)(2,1)S(1)} %pad_maximum_fusion.6), channel_id=1, source_target_pairs={{0,128},{1,131},{4,132},{5,135},{8,136},{9,139},{12,140},{13,143},... | collective-permute-start | bytes 1769480 | tf_op jit(solution)/shard_map/ppermute | solution.py:49
  20.2 7.8 %collective-permute-start.14 = (bf16[2,192,512]{2,1,0:T(8,128)(2,1)S(1)}, bf16[2,192,512]{2,1,0:T(8,128)(2,1)S(1)}, u32[]{:S(2)}, u32[]{:S(2)}) collective-permute-start(bf16[2,192,512]{2,1,0:T(8,128)(2,1)S(1)} %collective-permute-done.13), channel_id=1, source_target_pairs={{0,4},{1,29},{4,0},{5,9},{8,12},{9,5},{12,8},{13,17},{16,20},{17,1... | collective-permute-start | bytes 1179656 | tf_op jit(solution)/shard_map/ppermute | solution.py:49
  22.2 17.3 %collective-permute-start.9 = (bf16[2,192,768]{2,1,0:T(8,128)(2,1)S(1)}, bf16[2,192,768]{2,1,0:T(8,128)(2,1)S(1)}, u32[]{:S(2)}, u32[]{:S(2)}) collective-permute-start(bf16[2,192,768]{2,1,0:T(8,128)(2,1)S(1)} %pad_maximum_fusion.6), channel_id=1, source_target_pairs={{0,96},{1,33},{4,100},{5,37},{8,104},{9,41},{12,108},{13,45},{16,1... | collective-permute-start | bytes 1769480 | tf_op jit(solution)/shard_map/ppermute | solution.py:49
  28.1 15.9 %collective-permute-start.20 = (bf16[4,192,512]{2,1,0:T(8,128)(2,1)S(1)}, bf16[4,192,512]{2,1,0:T(8,128)(2,1)S(1)}, u32[]{:S(2)}, u32[]{:S(2)}) collective-permute-start(bf16[4,192,512]{2,1,0:T(8,128)(2,1)S(1)} %pad_maximum_fusion.4.refs_1_), channel_id=1, source_target_pairs={{0,28},{1,5},{4,8},{5,1},{8,4},{9,13},{12,16},{13,9},{16,12},{17,2... | collective-permute-start | bytes 2359304 | tf_op jit(solution)/shard_map/ppermute | solution.py:49
  34.2 25.3 %collective-permute-start.2 = (bf16[4,192,768]{2,1,0:T(8,128)(2,1)S(1)}, bf16[4,192,768]{2,1,0:T(8,128)(2,1)S(1)}, u32[]{:S(2)}, u32[]{:S(2)}) collective-permute-start(bf16[4,192,768]{2,1,0:T(8,128)(2,1)S(1)} %pad_maximum_fusion.1.refs_1_), channel_id=1, source_target_pairs={{0,96},{1,33},{4,100},{5,37},{8,104},{9,41},{12,108},{13,45},{16,1... | collective-permute-start | bytes 3538952 | tf_op jit(solution)/shard_map/ppermute | solution.py:49
  35.3 24.0 %collective-permute-start.15 = (bf16[4,192,512]{2,1,0:T(8,128)(2,1)S(1)}, bf16[4,192,512]{2,1,0:T(8,128)(2,1)S(1)}, u32[]{:S(2)}, u32[]{:S(2)}) collective-permute-start(bf16[4,192,512]{2,1,0:T(8,128)(2,1)S(1)} %pad_maximum_fusion.3.refs_1_), channel_id=1, source_target_pairs={{0,28},{1,5},{4,8},{5,1},{8,4},{9,13},{12,16},{13,9},{16,12},{17,2... | collective-permute-start | bytes 2359304 | tf_op jit(solution)/shard_map/ppermute | solution.py:49
  38.5 14.5 %collective-permute-start.4 = (bf16[2,192,768]{2,1,0:T(8,128)(2,1)S(1)}, bf16[2,192,768]{2,1,0:T(8,128)(2,1)S(1)}, u32[]{:S(2)}, u32[]{:S(2)}) collective-permute-start(bf16[2,192,768]{2,1,0:T(8,128)(2,1)S(1)} %collective-permute-done.3), channel_id=1, source_target_pairs={{0,32},{1,97},{4,36},{5,101},{8,40},{9,105},{12,44},{13,109},{16,4... | collective-permute-start | bytes 1769480 | tf_op jit(solution)/shard_map/ppermute | solution.py:49
  39.5 19.8 %collective-permute-start.10 = (bf16[2,192,768]{2,1,0:T(8,128)(2,1)S(1)}, bf16[2,192,768]{2,1,0:T(8,128)(2,1)S(1)}, u32[]{:S(2)}, u32[]{:S(2)}) collective-permute-start(bf16[2,192,768]{2,1,0:T(8,128)(2,1)S(1)} %collective-permute-done.9), channel_id=1, source_target_pairs={{0,128},{1,131},{4,132},{5,135},{8,136},{9,139},{12,140},{13,143},... | collective-permute-start | bytes 1769480 | tf_op jit(solution)/shard_map/ppermute | solution.py:49
  44.0 22.6 %collective-permute-start.21 = (bf16[4,192,512]{2,1,0:T(8,128)(2,1)S(1)}, bf16[4,192,512]{2,1,0:T(8,128)(2,1)S(1)}, u32[]{:S(2)}, u32[]{:S(2)}) collective-permute-start(bf16[4,192,512]{2,1,0:T(8,128)(2,1)S(1)} %collective-permute-done.20.refs_2_), channel_id=1, source_target_pairs={{0,4},{1,29},{4,0},{5,9},{8,12},{9,5},{12,8},{13,17},{16,20},{17,1... | collective-permute-start | bytes 2359304 | tf_op jit(solution)/shard_map/ppermute | solution.py:49
  53.0 35.0 %collective-permute-start.8 = (bf16[4,192,768]{2,1,0:T(8,128)(2,1)S(1)}, bf16[4,192,768]{2,1,0:T(8,128)(2,1)S(1)}, u32[]{:S(2)}, u32[]{:S(2)}) collective-permute-start(bf16[4,192,768]{2,1,0:T(8,128)(2,1)S(1)} %pad_maximum_fusion.2.refs_3_), channel_id=1, source_target_pairs={{0,130},{1,129},{4,134},{5,133},{8,138},{9,137},{12,142},{13,141},... | collective-permute-start | bytes 3538952 | tf_op jit(solution)/shard_map/ppermute | solution.py:49
  59.3 19.7 %collective-permute-start.16 = (bf16[4,192,512]{2,1,0:T(8,128)(2,1)S(1)}, bf16[4,192,512]{2,1,0:T(8,128)(2,1)S(1)}, u32[]{:S(2)}, u32[]{:S(2)}) collective-permute-start(bf16[4,192,512]{2,1,0:T(8,128)(2,1)S(1)} %collective-permute-done.15.refs_2_), channel_id=1, source_target_pairs={{0,4},{1,29},{4,0},{5,9},{8,12},{9,5},{12,8},{13,17},{16,20},{17,1... | collective-permute-start | bytes 2359304 | tf_op jit(solution)/shard_map/ppermute | solution.py:49
  59.3 28.7 %collective-permute-start.5 = (bf16[4,192,768]{2,1,0:T(8,128)(2,1)S(1)}, bf16[4,192,768]{2,1,0:T(8,128)(2,1)S(1)}, u32[]{:S(2)}, u32[]{:S(2)}) collective-permute-start(bf16[4,192,768]{2,1,0:T(8,128)(2,1)S(1)} %constant_dynamic-update-slice_fusion.refs_2_), channel_id=1, source_target_pairs={{0,96},{1,33},{4,100},{5,37},{8,104},{9,41},{12,108},{13,45},{16,1... | collective-permute-start | bytes 3538952 | tf_op jit(solution)/shard_map/ppermute | solution.py:49
  59.5 28.5 %collective-permute-start.11 = (bf16[4,192,768]{2,1,0:T(8,128)(2,1)S(1)}, bf16[4,192,768]{2,1,0:T(8,128)(2,1)S(1)}, u32[]{:S(2)}, u32[]{:S(2)}) collective-permute-start(bf16[4,192,768]{2,1,0:T(8,128)(2,1)S(1)} %constant_dynamic-update-slice_fusion.2.refs_4_), channel_id=1, source_target_pairs={{0,130},{1,129},{4,134},{5,133},{8,138},{9,137},{12,142},{13,141},... | collective-permute-start | bytes 3538952 | tf_op jit(solution)/shard_map/ppermute | solution.py:49
  66.6 22.9 %collective-permute-start.22 = (bf16[4,192,512]{2,1,0:T(8,128)(2,1)S(1)}, bf16[4,192,512]{2,1,0:T(8,128)(2,1)S(1)}, u32[]{:S(2)}, u32[]{:S(2)}) collective-permute-start(bf16[4,192,512]{2,1,0:T(8,128)(2,1)S(1)} %collective-permute-done.21.refs_3_), channel_id=1, source_target_pairs={{0,28},{1,5},{4,8},{5,1},{8,4},{9,13},{12,16},{13,9},{16,12},{17,2... | collective-permute-start | bytes 2359304 | tf_op jit(solution)/shard_map/ppermute | solution.py:49
  78.9 18.7 %collective-permute-start.17 = (bf16[4,192,512]{2,1,0:T(8,128)(2,1)S(1)}, bf16[4,192,512]{2,1,0:T(8,128)(2,1)S(1)}, u32[]{:S(2)}, u32[]{:S(2)}) collective-permute-start(bf16[4,192,512]{2,1,0:T(8,128)(2,1)S(1)} %collective-permute-done.16.refs_3_), channel_id=1, source_target_pairs={{0,28},{1,5},{4,8},{5,1},{8,4},{9,13},{12,16},{13,9},{16,12},{17,2... | collective-permute-start | bytes 2359304 | tf_op jit(solution)/shard_map/ppermute | solution.py:49
  93.7 8.7 %collective-permute-start.23 = (f32[768,512]{1,0:T(8,128)S(1)}, f32[768,512]{1,0:T(8,128)S(1)}, u32[]{:S(2)}, u32[]{:S(2)}) collective-permute-start(f32[768,512]{1,0:T(8,128)S(1)} %multiply_other.3), channel_id=1, source_target_pairs={{0,1},{1,0},{4,5},{5,4},{8,9},{9,8},{12,13},{13,12},{16,17},{17,16... | collective-permute-start | bytes 4718600 | tf_op jit(solution)/shard_map/ppermute | solution.py:49
  101.8 11.0 %collective-permute-start.18 = (f32[768,512]{1,0:T(8,128)S(1)}, f32[768,512]{1,0:T(8,128)S(1)}, u32[]{:S(2)}, u32[]{:S(2)}) collective-permute-start(f32[768,512]{1,0:T(8,128)S(1)} %multiply_other.2), channel_id=1, source_target_pairs={{0,1},{1,0},{4,5},{5,4},{8,9},{9,8},{12,13},{13,12},{16,17},{17,16... | collective-permute-start | bytes 4718600 | tf_op jit(solution)/shard_map/ppermute | solution.py:49
  105.0 17.8 %collective-permute-start.24 = (bf16[384,512]{1,0:T(8,128)(2,1)S(1)}, bf16[384,512]{1,0:T(8,128)(2,1)S(1)}, u32[]{:S(2)}, u32[]{:S(2)}) collective-permute-start(bf16[384,512]{1,0:T(8,128)(2,1)S(1)} %get-tuple-element.34), channel_id=1, source_target_pairs={{0,2},{1,3},{4,6},{5,7},{8,10},{9,11},{12,14},{13,15},{16,18},{17,... | collective-permute-start | bytes 1179656 | tf_op jit(solution)/shard_map/ppermute | solution.py:49
  115.4 15.1 %collective-permute-start.19 = (bf16[384,512]{1,0:T(8,128)(2,1)S(1)}, bf16[384,512]{1,0:T(8,128)(2,1)S(1)}, u32[]{:S(2)}, u32[]{:S(2)}) collective-permute-start(bf16[384,512]{1,0:T(8,128)(2,1)S(1)} %get-tuple-element.32), channel_id=1, source_target_pairs={{0,2},{1,3},{4,6},{5,7},{8,10},{9,11},{12,14},{13,15},{16,18},{17,... | collective-permute-start | bytes 1179656 | tf_op jit(solution)/shard_map/ppermute | solution.py:49

commit v3 on v2

--- a/solution.py
+++ b/solution.py
@@ -9,6 +9,7 @@
 AXES = ("pair", "outv", "conv")
 NX, NY, NZ = 4, 4, 8
 RCHUNKS = 2
+DEPTH_X = 896
 MIB = 1024 * 1024
 VMEM = pltpu.MemorySpace.VMEM
 SMEM = pltpu.MemorySpace.SMEM
@@ -51,7 +52,7 @@
 
 def mask_integrals_kernel(place, mask_ref, int_ref, first_ref, second_ref):
     width = int_ref.shape[1]
-    half = width // 2
+    half = first_ref.shape[1]
     tile = lax.broadcasted_iota(jnp.int32, (8, width), 1) // TW
     for j in range(int_ref.shape[0] // TW):
         column = place[0] * (int_ref.shape[0] // TW) + j
@@ -66,12 +67,12 @@
 
 def mask_integrals(place, int_mask, int_t):
     rows, width = int_t.shape
-    shape = jax.ShapeDtypeStruct((rows, width // 2), jnp.bfloat16)
+    shapes = [jax.ShapeDtypeStruct((rows, depth), jnp.bfloat16) for depth in (DEPTH_X, width - DEPTH_X)]
     return pl.pallas_call(
         mask_integrals_kernel,
         in_specs=[pl.BlockSpec(memory_space=SMEM), pl.BlockSpec(memory_space=SMEM), pl.BlockSpec(memory_space=VMEM)],
         out_specs=[pl.BlockSpec(memory_space=VMEM)] * 2,
-        out_shape=[shape, shape],
+        out_shape=shapes,
         compiler_params=pltpu.CompilerParams(vmem_limit_bytes=8 * MIB),
         name="mask_integrals",
     )(place, int_mask, int_t)
@@ -100,6 +101,10 @@
         compiler_params=pltpu.CompilerParams(vmem_limit_bytes=8 * MIB),
         name="mask_amplitudes",
     )(place, amp_mask, amp_t)
+
+
+def after(array, *others):
+    return lax.optimization_barrier((array, *others))[0]
 
 
 def ring_of_eight(near):
@@ -132,40 +137,39 @@
             for e in range(2):
                 z_from = (z + sz * RING8[2 * (first_step + step) + e] + NZ) % NZ
                 row = pl.multiple_of((hi * NZ + z_from) * rows, rows)
-                copies.append(
-                    pltpu.make_async_copy(
-                        piece.at[2 * chain + e], out_ref.at[pl.ds(row, rows), :], sems.at[len(copies)]
+                for col in range(0, piece.shape[2], 128):
+                    copies.append(
+                        pltpu.make_async_copy(
+                            piece.at[2 * chain + e, :, pl.ds(col, 128)],
+                            out_ref.at[pl.ds(row, rows), pl.ds(col, 128)],
+                            sems.at[len(copies)],
+                        )
                     )
-                )
     for copy in copies:
         copy.start()
     for copy in copies:
         copy.wait()
 
 
-def order_amplitudes(place, pieces):
+def order_amplitudes(place, pieces, first_step, held=()):
     _, rows, width = pieces[0].shape
+    steps = len(pieces)
     any_spec, vmem_spec = pl.BlockSpec(memory_space=pl.ANY), pl.BlockSpec(memory_space=VMEM)
-    out = pltpu.VMEM((16 * rows, width), jnp.bfloat16)
-    held = None
-    for first, steps in ((0, 3), (3, 1)):
-        args = [place, *pieces[first : first + steps]] + ([] if held is None else [held])
-
-        def kernel(*refs, first=first, steps=steps):
-            order_amplitudes_kernel(first, steps, *refs)
-
-        held = pl.pallas_call(
-            kernel,
-            in_specs=[pl.BlockSpec(memory_space=SMEM)] + [any_spec] * steps + [vmem_spec] * (held is not None),
-            out_specs=vmem_spec,
-            out_shape=out,
-            scratch_shapes=[pltpu.SemaphoreType.DMA((4 * steps,))],
-            input_output_aliases={} if held is None else {len(args) - 1: 0},
-            cost_estimate=pl.CostEstimate(flops=0, bytes_accessed=16 * steps * rows * width, transcendentals=0),
-            compiler_params=pltpu.CompilerParams(vmem_limit_bytes=MIB),
-            name="order_amplitudes",
-        )(*args)
-    return held
+
+    def kernel(*refs):
+        order_amplitudes_kernel(first_step, steps, *refs)
+
+    return pl.pallas_call(
+        kernel,
+        in_specs=[pl.BlockSpec(memory_space=SMEM)] + [any_spec] * steps + [vmem_spec] * len(held),
+        out_specs=vmem_spec,
+        out_shape=pltpu.VMEM((16 * rows, width), jnp.bfloat16),
+        scratch_shapes=[pltpu.SemaphoreType.DMA((4 * steps * width // 128,))],
+        input_output_aliases={1 + steps: 0} if held else {},
+        cost_estimate=pl.CostEstimate(flops=0, bytes_accessed=16 * steps * rows * width, transcendentals=0),
+        compiler_params=pltpu.CompilerParams(vmem_limit_bytes=MIB),
+        name="order_amplitudes",
+    )(place, *pieces, *held)
 
 
 def order_integrals_kernel(got, place, *refs):
@@ -173,7 +177,7 @@
     outs, sems = refs[-3:-1], refs[-1]
     x, y, c, x_hi = place[3], place[4], place[5], place[2]
     sx, sy = 1 - 2 * ((x + c) % 2), 1 - 2 * ((y + c) % 2)
-    rows, depth = pieces[0].shape[1:]
+    rows, depths = pieces[0].shape[1], (pieces[0].shape[2], pieces[2].shape[2])
     copies = []
     for half in range(2):
         for group in range(2):
@@ -184,11 +188,11 @@
                     x_from, y_from = (x + sx * dx + NX) % NX, (y + sy * dy + NY) % NY
                     side = (x_from % 2 + x_hi + 1) % 2
                     row = pl.multiple_of((side * 2 + y_from % 2) * rows, rows)
-                    col = pl.multiple_of((x_from // 2) * 2 * depth + half * depth, 128)
+                    col = pl.multiple_of((x_from // 2) * sum(depths) + half * depths[0], 128)
                     for own in range(2):
                         copy = pltpu.make_async_copy(
                             pieces[half * 2 + group].at[step * 2 + e],
-                            outs[own].at[pl.ds(row, rows), pl.ds(col, depth)],
+                            outs[own].at[pl.ds(row, rows), pl.ds(col, depths[half])],
                             sems.at[len(copies)],
                         )
                         copies.append((y_from // 2 == (c if own else 1 - c), copy))
@@ -222,41 +226,30 @@
     return held
 
 
-def multiply_kernel(own, int_ref, amp_ref, *refs):
-    rows = 384
-    for part in range(2):
-        src = pl.ds(part * rows, rows)
-        total = jnp.dot(int_ref[src, :], amp_ref[...], preferred_element_type=jnp.float32)
-        if own:
-            other_ref, outs = refs[0], refs[1:]
-            outs[part][...] = (total + other_ref[src, :]).astype(jnp.bfloat16)
-        else:
-            refs[0][src, :] = total
-
-
-def multiply(own, ints, amps, other=None):
-    width = amps.shape[1]
-    if own:
-        shapes = [jax.ShapeDtypeStruct((384, width), jnp.bfloat16)] * 2
-    else:
-        shapes = [jax.ShapeDtypeStruct((768, width), jnp.float32)]
+def multiply_kernel(int_ref, amp_ref, *refs):
+    rows = int_ref.shape[0] // 2
+    other_refs, outs = refs[:-2], refs[-2:]
+    for side in range(2):
+        total = jnp.dot(int_ref[pl.ds(side * rows, rows), :], amp_ref[...], preferred_element_type=jnp.float32)
+        if other_refs:
+            total = (total + other_refs[side][...]).astype(jnp.bfloat16)
+        outs[side][...] = total
+
+
+def multiply(ints, amps, *other):
+    rows, depth, width = ints.shape[0] // 2, ints.shape[1], amps.shape[1]
     vmem_spec = pl.BlockSpec(memory_space=VMEM)
-    args = [ints, amps] + ([other] if own else [])
-
-    def kernel(*refs):
-        multiply_kernel(own, *refs)
-
-    return pl.pallas_call(
-        kernel,
-        in_specs=[vmem_spec] * len(args),
-        out_specs=[vmem_spec] * len(shapes),
-        out_shape=shapes,
+    return pl.pallas_call(
+        multiply_kernel,
+        in_specs=[vmem_spec] * (2 + len(other)),
+        out_specs=[vmem_spec] * 2,
+        out_shape=[jax.ShapeDtypeStruct((rows, width), jnp.bfloat16 if other else jnp.float32)] * 2,
         cost_estimate=pl.CostEstimate(
-            flops=2 * 768 * 3072 * width, bytes_accessed=768 * 3072 * 2 + 3072 * width * 2 + 768 * width * 4, transcendentals=0
+            flops=4 * rows * depth * width, bytes_accessed=(2 * rows + width) * depth * 2 + 8 * rows * width, transcendentals=0
         ),
         compiler_params=pltpu.CompilerParams(vmem_limit_bytes=12 * MIB),
-        name="multiply_own" if own else "multiply_other",
-    )(*args)
+        name="multiply_own" if other else "multiply_other",
+    )(ints, amps, *other)
 
 
 def body(amplitudes, integrals, amp_mask, int_mask):
@@ -272,16 +265,16 @@
     partner = send(give, X_ACROSS)
     partner_got = send(partner, Z_FIRST)
     ints = plane(first, (X_FIRST, X_OTHER), (Y_FIRST, Y_OTHER)) + plane(second, (Y_FIRST, Y_OTHER), (X_FIRST, X_OTHER))
-    amps = [
-        order_amplitudes(place, ring_of_eight(jnp.stack([keep[r], keep_got[r], partner[r], partner_got[r]])))
-        for r in range(RCHUNKS)
-    ]
+    rings = [ring_of_eight(jnp.stack([keep[r], keep_got[r], partner[r], partner_got[r]])) for r in range(RCHUNKS)]
+    held = [order_amplitudes(place, ring[:3], 0) for ring in rings]
+    held[0] = after(*held)
+    amps = [order_amplitudes(place, ring[3:], 3, [part]) for ring, part in zip(rings, held)]
     other_ints, own_ints = order_integrals(place, ints)
 
     kept, received = [], []
     for columns in amps:
-        (partial,) = multiply(False, other_ints, columns)
-        theirs, mine = multiply(True, own_ints, columns, send(partial, CORE))
+        partials = [send(partial, CORE) for partial in multiply(other_ints, columns)]
+        theirs, mine = multiply(own_ints, columns, *partials)
         kept.append(mine)
         received.append(send(theirs, X_ACROSS))
     low = [jnp.where(x_hi == 0, k, g) for k, g in zip(kept, received)]

time: 134 us -> 129 us (0.963)
  waiting for transfers between devices: 51.1 us -> 60.8 us
  starting transfers between devices: 49.2 us -> 39.6 us
  Pallas kernels: 25.4 us -> 19.8 us
    ppermute x25 -> x27, starting transfers between devices: 49.2 us -> 39.6 us  [send(): return lax.ppermute(array, AXES, plan)]
    ppermute x25 -> x27, waiting for transfers between devices: 51.1 us -> 60.8 us  [send(): return lax.ppermute(array, AXES, plan)]
    pallas_call x4, Pallas kernels: 10.7 us -> 4.76 us  [order_amplitudes(): pl.pallas_call(kernel, in_specs=[pl.BlockSpec(memory_space=SMEM)] + [any_...]
  transfers between devices with their start and end apart: 25 -> 27, of which waited for: 8 -> 9; matrix products, arithmetic and copies ran while one was open for 1% -> 1% of each run, Pallas kernels for 19% -> 15%
where the time goes in v3:
time: 129 us; the launch traced here: 126 us
  waiting for transfers between devices  60.8 us (47%)
  starting transfers between devices  39.6 us (31%)
  Pallas kernels  19.8 us (15%)
  local copies, waits for them, and re-layouts  3.99 us (3%)
  other arithmetic  2.07 us (2%)
    ppermute x27, waiting for transfers between devices, send(): return lax.ppermute(array, AXES, plan)  60.8 us
    ppermute x27, starting transfers between devices, send(): return lax.ppermute(array, AXES, plan)  39.6 us
    pallas_call x4, Pallas kernels, multiply(): pl.pallas_call(multiply_kernel, in_specs=[vmem_spec] * (2 + len(other)),...  10.4 us
    pallas_call x4, Pallas kernels, order_amplitudes(): pl.pallas_call(kernel, in_specs=[pl.BlockSpec(memory_space=SMEM)] + [any_...  4.76 us
    unnamed x10, local copies, waits for them, and re-layouts  3.65 us
    pallas_call x2, Pallas kernels, order_integrals(): pl.pallas_call(kernel, in_specs=[pl.BlockSpec(memory_space=SMEM)] + [any_...  3.24 us
  transfers between devices with their start and end apart: 27, of which 9 were waited for; matrix products, arithmetic and copies ran while one was open for 1% of the time, Pallas kernels for 15%

profile of v3, /device:TPU:24, one launch (start us, length us, event | category | flops | bytes accessed | tf_op | source)
XLA Modules:
  0.0 126.4 jit_solution(17772207465406362112)
XLA Ops:
  0.1 1.1 copy-done.1
  1.2 0.7 copy-done.2
  1.8 0.8 mask_integrals.1
  2.7 0.8 collective-permute-start.6
  3.5 1.5 %collective-permute-start = (bf16[192,896]{1,0:T(8,128)(2,1)S(1)}, bf16[192,896]{1,0:T(8,128)(2,1)S(1)}, u32[]{:S(2)}, u32[]{:S(2)}) collective-permute-start(bf16[192,896]{1,0:T(8,128)(2,1)S(1)} %get-tuple-element.28), channel_id=1, source_target_pairs={{0,128},{1,131},{4,132},{5,135},{8,136},{9,139},{12,140},{13,143},... | collective-permute-start | bytes 1032200 | tf_op jit(solution)/shard_map/ppermute | solution.py:50
  5.0 1.1 copy-done
  6.1 0.7 copy-done.3
  6.8 0.6 mask_amplitudes.1
  7.4 2.8 %collective-permute-start.13 = (bf16[2,192,512]{2,1,0:T(8,128)(2,1)S(1)}, bf16[2,192,512]{2,1,0:T(8,128)(2,1)S(1)}, u32[]{:S(2)}, u32[]{:S(2)}) collective-permute-start(bf16[2,192,512]{2,1,0:T(8,128)(2,1)S(1)} %get-tuple-element.34), channel_id=1, source_target_pairs={{0,2},{1,3},{4,6},{5,7},{8,10},{9,11},{12,14},{13,15},{16,18},{17,... | collective-permute-start | bytes 1179656 | tf_op jit(solution)/shard_map/ppermute | solution.py:50
  10.2 1.9 %collective-permute-start.12 = (bf16[2,192,512]{2,1,0:T(8,128)(2,1)S(1)}, bf16[2,192,512]{2,1,0:T(8,128)(2,1)S(1)}, u32[]{:S(2)}, u32[]{:S(2)}) collective-permute-start(bf16[2,192,512]{2,1,0:T(8,128)(2,1)S(1)} %get-tuple-element.33), channel_id=1, source_target_pairs={{0,4},{1,29},{4,0},{5,9},{8,12},{9,5},{12,8},{13,17},{16,20},{17,1... | collective-permute-start | bytes 1179656 | tf_op jit(solution)/shard_map/ppermute | solution.py:50
  12.2 1.1 collective-permute-start.9
  13.4 0.2 collective-permute-start.7
  13.7 1.2 collective-permute-start.3
  14.9 7.6 %collective-permute-done.13 = bf16[2,192,512]{2,1,0:T(8,128)(2,1)S(1)} collective-permute-done((bf16[2,192,512]{2,1,0:T(8,128)(2,1)S(1)}, bf16[2,192,512]{2,1,0:T(8,128)(2,1)S(1)}, u32[]{:S(2)}, u32[]{:S(2)}) %collective-permute-start.13) | collective-permute-done | bytes 393248 | tf_op jit(solution)/shard_map/ppermute | solution.py:50
  22.5 1.9 %collective-permute-start.14 = (bf16[2,192,512]{2,1,0:T(8,128)(2,1)S(1)}, bf16[2,192,512]{2,1,0:T(8,128)(2,1)S(1)}, u32[]{:S(2)}, u32[]{:S(2)}) collective-permute-start(bf16[2,192,512]{2,1,0:T(8,128)(2,1)S(1)} %collective-permute-done.13), channel_id=1, source_target_pairs={{0,4},{1,29},{4,0},{5,9},{8,12},{9,5},{12,8},{13,17},{16,20},{17,1... | collective-permute-start | bytes 1179656 | tf_op jit(solution)/shard_map/ppermute | solution.py:50
  24.5 1.8 %collective-permute-start.1 = (bf16[2,192,896]{2,1,0:T(8,128)(2,1)S(1)}, bf16[2,192,896]{2,1,0:T(8,128)(2,1)S(1)}, u32[]{:S(2)}, u32[]{:S(2)}) collective-permute-start(bf16[2,192,896]{2,1,0:T(8,128)(2,1)S(1)} %pad_maximum_fusion.5), channel_id=1, source_target_pairs={{0,32},{1,97},{4,36},{5,101},{8,40},{9,105},{12,44},{13,109},{16,4... | collective-permute-start | bytes 2064392 | tf_op jit(solution)/shard_map/ppermute | solution.py:50
  26.4 3.9 %collective-permute-done.14 = bf16[2,192,512]{2,1,0:T(8,128)(2,1)S(1)} collective-permute-done((bf16[2,192,512]{2,1,0:T(8,128)(2,1)S(1)}, bf16[2,192,512]{2,1,0:T(8,128)(2,1)S(1)}, u32[]{:S(2)}, u32[]{:S(2)}) %collective-permute-start.14) | collective-permute-done | bytes 393248 | tf_op jit(solution)/shard_map/ppermute | solution.py:50
  30.5 5.9 %collective-permute-start.15 = (bf16[4,192,512]{2,1,0:T(8,128)(2,1)S(1)}, bf16[4,192,512]{2,1,0:T(8,128)(2,1)S(1)}, u32[]{:S(2)}, u32[]{:S(2)}) collective-permute-start(bf16[4,192,512]{2,1,0:T(8,128)(2,1)S(1)} %pad_maximum_fusion.3.refs_1_), channel_id=1, source_target_pairs={{0,28},{1,5},{4,8},{5,1},{8,4},{9,13},{12,16},{13,9},{16,12},{17,2... | collective-permute-start | bytes 2359304 | tf_op jit(solution)/shard_map/ppermute | solution.py:50
  36.4 1.8 %collective-permute-start.4 = (bf16[2,192,896]{2,1,0:T(8,128)(2,1)S(1)}, bf16[2,192,896]{2,1,0:T(8,128)(2,1)S(1)}, u32[]{:S(2)}, u32[]{:S(2)}) collective-permute-start(bf16[2,192,896]{2,1,0:T(8,128)(2,1)S(1)} %collective-permute-done.3), channel_id=1, source_target_pairs={{0,32},{1,97},{4,36},{5,101},{8,40},{9,105},{12,44},{13,109},{16,4... | collective-permute-start | bytes 2064392 | tf_op jit(solution)/shard_map/ppermute | solution.py:50
  38.3 2.4 %collective-permute-start.18 = (bf16[4,192,512]{2,1,0:T(8,128)(2,1)S(1)}, bf16[4,192,512]{2,1,0:T(8,128)(2,1)S(1)}, u32[]{:S(2)}, u32[]{:S(2)}) collective-permute-start(bf16[4,192,512]{2,1,0:T(8,128)(2,1)S(1)} %pad_maximum_fusion.4.refs_1_), channel_id=1, source_target_pairs={{0,28},{1,5},{4,8},{5,1},{8,4},{9,13},{12,16},{13,9},{16,12},{17,2... | collective-permute-start | bytes 2359304 | tf_op jit(solution)/shard_map/ppermute | solution.py:50
  40.9 1.2 collective-permute-start.8
  42.4 4.0 %collective-permute-done.15.refs_2_ = bf16[4,192,512]{2,1,0:T(8,128)(2,1)S(1)} collective-permute-done((bf16[4,192,512]{2,1,0:T(8,128)(2,1)S(1)}, bf16[4,192,512]{2,1,0:T(8,128)(2,1)S(1)}, u32[]{:S(2)}, u32[]{:S(2)}) %collective-permute-start.15) | collective-permute-done | bytes 786464 | tf_op jit(solution)/shard_map/ppermute | solution.py:50
  46.4 0.9 collective-permute-done.4
  47.4 6.8 %collective-permute-done.10 = bf16[2,192,640]{2,1,0:T(8,128)(2,1)S(1)} collective-permute-done((bf16[2,192,640]{2,1,0:T(8,128)(2,1)S(1)}, bf16[2,192,640]{2,1,0:T(8,128)(2,1)S(1)}, u32[]{:S(2)}, u32[]{:S(2)}) %collective-permute-start.10) | collective-permute-done | bytes 491552 | tf_op jit(solution)/shard_map/ppermute | solution.py:50
  54.2 1.1 collective-permute-start.5
  55.4 7.5 %collective-permute-done.18.refs_2_ = bf16[4,192,512]{2,1,0:T(8,128)(2,1)S(1)} collective-permute-done((bf16[4,192,512]{2,1,0:T(8,128)(2,1)S(1)}, bf16[4,192,512]{2,1,0:T(8,128)(2,1)S(1)}, u32[]{:S(2)}, u32[]{:S(2)}) %collective-permute-start.18) | collective-permute-done | bytes 786464 | tf_op jit(solution)/shard_map/ppermute | solution.py:50
  63.1 1.0 collective-permute-start.11
  64.1 4.0 %collective-permute-start.17 = (bf16[4,192,512]{2,1,0:T(8,128)(2,1)S(1)}, bf16[4,192,512]{2,1,0:T(8,128)(2,1)S(1)}, u32[]{:S(2)}, u32[]{:S(2)}) collective-permute-start(bf16[4,192,512]{2,1,0:T(8,128)(2,1)S(1)} %collective-permute-done.16.refs_3_), channel_id=1, source_target_pairs={{0,28},{1,5},{4,8},{5,1},{8,4},{9,13},{12,16},{13,9},{16,12},{17,2... | collective-permute-start | bytes 2359304 | tf_op jit(solution)/shard_map/ppermute | solution.py:50
  68.1 15.1 %collective-permute-done.19.refs_3_ = bf16[4,192,512]{2,1,0:T(8,128)(2,1)S(1)} collective-permute-done((bf16[4,192,512]{2,1,0:T(8,128)(2,1)S(1)}, bf16[4,192,512]{2,1,0:T(8,128)(2,1)S(1)}, u32[]{:S(2)}, u32[]{:S(2)}) %collective-permute-start.19) | collective-permute-done | bytes 786464 | tf_op jit(solution)/shard_map/ppermute | solution.py:50
  83.3 3.5 %collective-permute-start.23 = (bf16[4,192,512]{2,1,0:T(8,128)(2,1)S(1)}, bf16[4,192,512]{2,1,0:T(8,128)(2,1)S(1)}, u32[]{:S(2)}, u32[]{:S(2)}) collective-permute-start(bf16[4,192,512]{2,1,0:T(8,128)(2,1)S(1)} %collective-permute-done.19.refs_3_), channel_id=1, source_target_pairs={{0,28},{1,5},{4,8},{5,1},{8,4},{9,13},{12,16},{13,9},{16,12},{17,2... | collective-permute-start | bytes 2359304 | tf_op jit(solution)/shard_map/ppermute | solution.py:50
  86.8 1.6 %order_integrals.2 = (bf16[768,3072]{1,0:T(8,128)(2,1)S(1)}, bf16[768,3072]{1,0:T(8,128)(2,1)S(1)}) custom-call(s32[6]{0:T(128)S(1)} %stack.51.place.refs_0_, bf16[4,192,896]{2,1,0:T(8,128)(2,1)S(1)} %pad_maximum_fusion.1.refs_1_, bf16[4,192,896]{2,1,0:T(8,128)(2,1)S(1)} %constant_dynamic-update-slice_fusion.refs_2_, ...), custom_call_target="tpu_custom_call" | custom-call | bytes 9437184 | tf_op jit(solution)/shard_map/order_integrals/pallas_call | solution.py:215
  88.4 1.5 %order_amplitudes.5.refs_2_ = bf16[3072,512]{1,0:T(8,128)(2,1)S(1)} custom-call(s32[6]{0:T(128)S(1)} %stack.51.place.refs_0_, bf16[4,192,512]{2,1,0:T(8,128)(2,1)S(1)} %pad_maximum_fusion.4.refs_1_, bf16[4,192,512]{2,1,0:T(8,128)(2,1)S(1)} %collective-permute-done.18.refs_2_, bf16[4,192,512]{2,1,0:T(8,128)(2,1)S(1)} %collective-permute-done.19.refs_3_), custom_call_target="tpu_custom_call" | custom-call | bytes 4718592 | tf_op jit(solution)/shard_map/order_amplitudes/pallas_call | solution.py:162
  90.0 1.5 %order_amplitudes.4.refs_2_ = bf16[3072,512]{1,0:T(8,128)(2,1)S(1)} custom-call(s32[6]{0:T(128)S(1)} %stack.51.place.refs_0_, bf16[4,192,512]{2,1,0:T(8,128)(2,1)S(1)} %pad_maximum_fusion.3.refs_1_, bf16[4,192,512]{2,1,0:T(8,128)(2,1)S(1)} %collective-permute-done.15.refs_2_, bf16[4,192,512]{2,1,0:T(8,128)(2,1)S(1)} %collective-permute-done.16.refs_3_), custom_call_target="tpu_custom_call" | custom-call | bytes 4718592 | tf_op jit(solution)/shard_map/order_amplitudes/pallas_call | solution.py:162
  91.5 1.6 %order_integrals.3 = (bf16[768,3072]{1,0:T(8,128)(2,1)S(1)}, bf16[768,3072]{1,0:T(8,128)(2,1)S(1)}) custom-call(s32[6]{0:T(128)S(1)} %stack.51.place.refs_0_, bf16[4,192,896]{2,1,0:T(8,128)(2,1)S(1)} %collective-permute-done.2.refs_1_, bf16[4,192,896]{2,1,0:T(8,128)(2,1)S(1)} %collective-permute-done.5.refs_2_, ...), custom_call_target="tpu_custom_call", output_to_operand_aliasing={{0}: (5, {}), {1}: (6, {})} | custom-call | bytes 9437184 | tf_op jit(solution)/shard_map/order_integrals/pallas_call | solution.py:215
  93.2 0.9 order_amplitudes.6.amp_ref
  94.0 2.6 %multiply_other.2 = (f32[384,512]{1,0:T(8,128)S(1)}, f32[384,512]{1,0:T(8,128)S(1)}) custom-call(bf16[768,3072]{1,0:T(8,128)(2,1)S(1)} %get-tuple-element.36.int_ref, bf16[3072,512]{1,0:T(8,128)(2,1)S(1)} %order_amplitudes.6.amp_ref), custom_call_target="tpu_custom_call" | custom-call | flops 2415919104 | bytes 9437184 | tf_op jit(solution)/shard_map/multiply_other/pallas_call | solution.py:242
  96.7 0.5 collective-permute-start.21
  97.2 0.9 order_amplitudes.7.amp_ref
  98.1 2.6 %multiply_other.3 = (f32[384,512]{1,0:T(8,128)S(1)}, f32[384,512]{1,0:T(8,128)S(1)}) custom-call(bf16[768,3072]{1,0:T(8,128)(2,1)S(1)} %get-tuple-element.36.int_ref, bf16[3072,512]{1,0:T(8,128)(2,1)S(1)} %order_amplitudes.7.amp_ref), custom_call_target="tpu_custom_call" | custom-call | flops 2415919104 | bytes 9437184 | tf_op jit(solution)/shard_map/multiply_other/pallas_call | solution.py:242
  100.7 0.2 collective-permute-start.24
  100.9 0.4 collective-permute-start.25
  101.3 2.6 %multiply_own.2 = (bf16[384,512]{1,0:T(8,128)(2,1)S(1)}, bf16[384,512]{1,0:T(8,128)(2,1)S(1)}) custom-call(bf16[768,3072]{1,0:T(8,128)(2,1)S(1)} %get-tuple-element.32.int_ref, bf16[3072,512]{1,0:T(8,128)(2,1)S(1)} %order_amplitudes.6.amp_ref, f32[384,512]{1,0:T(8,128)S(1)} %collective-permute-done.20.refs_0_, f32[384,512]{1,0:T(8,128)S(1)} %collective-permute-done.21.refs_1_), custom_call_target="tpu_custom_call" | custom-call | flops 2415919104 | bytes 9437184 | tf_op jit(solution)/shard_map/multiply_own/pallas_call | solution.py:242
  103.9 2.8 %collective-permute-start.22 = (bf16[384,512]{1,0:T(8,128)(2,1)S(1)}, bf16[384,512]{1,0:T(8,128)(2,1)S(1)}, u32[]{:S(2)}, u32[]{:S(2)}) collective-permute-start(bf16[384,512]{1,0:T(8,128)(2,1)S(1)} %get-tuple-element.40), channel_id=1, source_target_pairs={{0,2},{1,3},{4,6},{5,7},{8,10},{9,11},{12,14},{13,15},{16,18},{17,... | collective-permute-start | bytes 1179656 | tf_op jit(solution)/shard_map/ppermute | solution.py:50
  106.7 2.6 %multiply_own.3 = (bf16[384,512]{1,0:T(8,128)(2,1)S(1)}, bf16[384,512]{1,0:T(8,128)(2,1)S(1)}) custom-call(bf16[768,3072]{1,0:T(8,128)(2,1)S(1)} %get-tuple-element.32.int_ref, bf16[3072,512]{1,0:T(8,128)(2,1)S(1)} %order_amplitudes.7.amp_ref, f32[384,512]{1,0:T(8,128)S(1)} %collective-permute-done.24.refs_0_, f32[384,512]{1,0:T(8,128)S(1)} %collective-permute-done.25.refs_1_), custom_call_target="tpu_custom_call" | custom-call | flops 2415919104 | bytes 9437184 | tf_op jit(solution)/shard_map/multiply_own/pallas_call | solution.py:242
  109.3 0.9 collective-permute-start.26
  110.2 7.2 %collective-permute-done.22 = bf16[384,512]{1,0:T(8,128)(2,1)S(1)} collective-permute-done((bf16[384,512]{1,0:T(8,128)(2,1)S(1)}, bf16[384,512]{1,0:T(8,128)(2,1)S(1)}, u32[]{:S(2)}, u32[]{:S(2)}) %collective-permute-start.22) | collective-permute-done | bytes 393248 | tf_op jit(solution)/shard_map/ppermute | solution.py:50
  117.5 7.5 %collective-permute-done.26 = bf16[384,512]{1,0:T(8,128)(2,1)S(1)} collective-permute-done((bf16[384,512]{1,0:T(8,128)(2,1)S(1)}, bf16[384,512]{1,0:T(8,128)(2,1)S(1)}, u32[]{:S(2)}, u32[]{:S(2)}) %collective-permute-start.26) | collective-permute-done | bytes 393248 | tf_op jit(solution)/shard_map/ppermute | solution.py:50
  125.1 1.3 %pad_maximum_fusion = bf16[384,2048]{1,0:T(8,128)(2,1)} fusion(bf16[384,512]{1,0:T(8,128)(2,1)S(1)} %get-tuple-element.48, bf16[384,512]{1,0:T(8,128)(2,1)S(1)} %get-tuple-element.46, bf16[384,512]{1,0:T(8,128)(2,1)S(1)} %get-tuple-element.47, bf16[384,512]{1,0:T(8,128)(2,1)S(1)} %get-tuple-element.45), kind=kLoop, calls=%fused_computation | loop fusion | flops 6291456 | bytes 3145728 | tf_op jit(solution)/shard_map/concatenate | solution.py:282
  (44 shorter events, 1.5 us)
Async XLA Ops:
  0.1 1.1 copy-start.1
  1.2 0.7 copy-start.2
  2.7 9.5 %collective-permute-start.6 = (bf16[192,640]{1,0:T(8,128)(2,1)S(1)}, bf16[192,640]{1,0:T(8,128)(2,1)S(1)}, u32[]{:S(2)}, u32[]{:S(2)}) collective-permute-start(bf16[192,640]{1,0:T(8,128)(2,1)S(1)} %get-tuple-element.29), channel_id=1, source_target_pairs={{0,32},{1,97},{4,36},{5,101},{8,40},{9,105},{12,44},{13,109},{16,4... | collective-permute-start | bytes 737288 | tf_op jit(solution)/shard_map/ppermute | solution.py:50
  3.5 10.1 %collective-permute-start = (bf16[192,896]{1,0:T(8,128)(2,1)S(1)}, bf16[192,896]{1,0:T(8,128)(2,1)S(1)}, u32[]{:S(2)}, u32[]{:S(2)}) collective-permute-start(bf16[192,896]{1,0:T(8,128)(2,1)S(1)} %get-tuple-element.28), channel_id=1, source_target_pairs={{0,128},{1,131},{4,132},{5,135},{8,136},{9,139},{12,140},{13,143},... | collective-permute-start | bytes 1032200 | tf_op jit(solution)/shard_map/ppermute | solution.py:50
  5.0 1.1 copy-start
  6.1 0.7 copy-start.3
  7.4 15.1 %collective-permute-start.13 = (bf16[2,192,512]{2,1,0:T(8,128)(2,1)S(1)}, bf16[2,192,512]{2,1,0:T(8,128)(2,1)S(1)}, u32[]{:S(2)}, u32[]{:S(2)}) collective-permute-start(bf16[2,192,512]{2,1,0:T(8,128)(2,1)S(1)} %get-tuple-element.34), channel_id=1, source_target_pairs={{0,2},{1,3},{4,6},{5,7},{8,10},{9,11},{12,14},{13,15},{16,18},{17,... | collective-permute-start | bytes 1179656 | tf_op jit(solution)/shard_map/ppermute | solution.py:50
  10.2 14.3 %collective-permute-start.12 = (bf16[2,192,512]{2,1,0:T(8,128)(2,1)S(1)}, bf16[2,192,512]{2,1,0:T(8,128)(2,1)S(1)}, u32[]{:S(2)}, u32[]{:S(2)}) collective-permute-start(bf16[2,192,512]{2,1,0:T(8,128)(2,1)S(1)} %get-tuple-element.33), channel_id=1, source_target_pairs={{0,4},{1,29},{4,0},{5,9},{8,12},{9,5},{12,8},{13,17},{16,20},{17,1... | collective-permute-start | bytes 1179656 | tf_op jit(solution)/shard_map/ppermute | solution.py:50
  12.2 28.6 %collective-permute-start.9 = (bf16[2,192,640]{2,1,0:T(8,128)(2,1)S(1)}, bf16[2,192,640]{2,1,0:T(8,128)(2,1)S(1)}, u32[]{:S(2)}, u32[]{:S(2)}) collective-permute-start(bf16[2,192,640]{2,1,0:T(8,128)(2,1)S(1)} %pad_maximum_fusion.6), channel_id=1, source_target_pairs={{0,96},{1,33},{4,100},{5,37},{8,104},{9,41},{12,108},{13,45},{16,1... | collective-permute-start | bytes 1474568 | tf_op jit(solution)/shard_map/ppermute | solution.py:50
  13.4 24.9 %collective-permute-start.7 = (bf16[2,192,640]{2,1,0:T(8,128)(2,1)S(1)}, bf16[2,192,640]{2,1,0:T(8,128)(2,1)S(1)}, u32[]{:S(2)}, u32[]{:S(2)}) collective-permute-start(bf16[2,192,640]{2,1,0:T(8,128)(2,1)S(1)} %pad_maximum_fusion.6), channel_id=1, source_target_pairs={{0,128},{1,131},{4,132},{5,135},{8,136},{9,139},{12,140},{13,143},... | collective-permute-start | bytes 1474568 | tf_op jit(solution)/shard_map/ppermute | solution.py:50
  13.7 22.7 %collective-permute-start.3 = (bf16[2,192,896]{2,1,0:T(8,128)(2,1)S(1)}, bf16[2,192,896]{2,1,0:T(8,128)(2,1)S(1)}, u32[]{:S(2)}, u32[]{:S(2)}) collective-permute-start(bf16[2,192,896]{2,1,0:T(8,128)(2,1)S(1)} %pad_maximum_fusion.5), channel_id=1, source_target_pairs={{0,130},{1,129},{4,134},{5,133},{8,138},{9,137},{12,142},{13,141},... | collective-permute-start | bytes 2064392 | tf_op jit(solution)/shard_map/ppermute | solution.py:50
  22.5 7.8 %collective-permute-start.14 = (bf16[2,192,512]{2,1,0:T(8,128)(2,1)S(1)}, bf16[2,192,512]{2,1,0:T(8,128)(2,1)S(1)}, u32[]{:S(2)}, u32[]{:S(2)}) collective-permute-start(bf16[2,192,512]{2,1,0:T(8,128)(2,1)S(1)} %collective-permute-done.13), channel_id=1, source_target_pairs={{0,4},{1,29},{4,0},{5,9},{8,12},{9,5},{12,8},{13,17},{16,20},{17,1... | collective-permute-start | bytes 1179656 | tf_op jit(solution)/shard_map/ppermute | solution.py:50
  24.5 17.6 %collective-permute-start.1 = (bf16[2,192,896]{2,1,0:T(8,128)(2,1)S(1)}, bf16[2,192,896]{2,1,0:T(8,128)(2,1)S(1)}, u32[]{:S(2)}, u32[]{:S(2)}) collective-permute-start(bf16[2,192,896]{2,1,0:T(8,128)(2,1)S(1)} %pad_maximum_fusion.5), channel_id=1, source_target_pairs={{0,32},{1,97},{4,36},{5,101},{8,40},{9,105},{12,44},{13,109},{16,4... | collective-permute-start | bytes 2064392 | tf_op jit(solution)/shard_map/ppermute | solution.py:50
  30.5 15.9 %collective-permute-start.15 = (bf16[4,192,512]{2,1,0:T(8,128)(2,1)S(1)}, bf16[4,192,512]{2,1,0:T(8,128)(2,1)S(1)}, u32[]{:S(2)}, u32[]{:S(2)}) collective-permute-start(bf16[4,192,512]{2,1,0:T(8,128)(2,1)S(1)} %pad_maximum_fusion.3.refs_1_), channel_id=1, source_target_pairs={{0,28},{1,5},{4,8},{5,1},{8,4},{9,13},{12,16},{13,9},{16,12},{17,2... | collective-permute-start | bytes 2359304 | tf_op jit(solution)/shard_map/ppermute | solution.py:50
  36.4 10.9 %collective-permute-start.4 = (bf16[2,192,896]{2,1,0:T(8,128)(2,1)S(1)}, bf16[2,192,896]{2,1,0:T(8,128)(2,1)S(1)}, u32[]{:S(2)}, u32[]{:S(2)}) collective-permute-start(bf16[2,192,896]{2,1,0:T(8,128)(2,1)S(1)} %collective-permute-done.3), channel_id=1, source_target_pairs={{0,32},{1,97},{4,36},{5,101},{8,40},{9,105},{12,44},{13,109},{16,4... | collective-permute-start | bytes 2064392 | tf_op jit(solution)/shard_map/ppermute | solution.py:50
  38.3 24.6 %collective-permute-start.18 = (bf16[4,192,512]{2,1,0:T(8,128)(2,1)S(1)}, bf16[4,192,512]{2,1,0:T(8,128)(2,1)S(1)}, u32[]{:S(2)}, u32[]{:S(2)}) collective-permute-start(bf16[4,192,512]{2,1,0:T(8,128)(2,1)S(1)} %pad_maximum_fusion.4.refs_1_), channel_id=1, source_target_pairs={{0,28},{1,5},{4,8},{5,1},{8,4},{9,13},{12,16},{13,9},{16,12},{17,2... | collective-permute-start | bytes 2359304 | tf_op jit(solution)/shard_map/ppermute | solution.py:50
  40.9 22.2 %collective-permute-start.8 = (bf16[4,192,640]{2,1,0:T(8,128)(2,1)S(1)}, bf16[4,192,640]{2,1,0:T(8,128)(2,1)S(1)}, u32[]{:S(2)}, u32[]{:S(2)}) collective-permute-start(bf16[4,192,640]{2,1,0:T(8,128)(2,1)S(1)} %pad_maximum_fusion.2.refs_3_), channel_id=1, source_target_pairs={{0,130},{1,129},{4,134},{5,133},{8,138},{9,137},{12,142},{13,141},... | collective-permute-start | bytes 2949128 | tf_op jit(solution)/shard_map/ppermute | solution.py:50
  42.1 12.2 %collective-permute-start.10 = (bf16[2,192,640]{2,1,0:T(8,128)(2,1)S(1)}, bf16[2,192,640]{2,1,0:T(8,128)(2,1)S(1)}, u32[]{:S(2)}, u32[]{:S(2)}) collective-permute-start(bf16[2,192,640]{2,1,0:T(8,128)(2,1)S(1)} %collective-permute-done.9), channel_id=1, source_target_pairs={{0,128},{1,131},{4,132},{5,135},{8,136},{9,139},{12,140},{13,143},... | collective-permute-start | bytes 1474568 | tf_op jit(solution)/shard_map/ppermute | solution.py:50
  46.4 17.7 %collective-permute-start.16 = (bf16[4,192,512]{2,1,0:T(8,128)(2,1)S(1)}, bf16[4,192,512]{2,1,0:T(8,128)(2,1)S(1)}, u32[]{:S(2)}, u32[]{:S(2)}) collective-permute-start(bf16[4,192,512]{2,1,0:T(8,128)(2,1)S(1)} %collective-permute-done.15.refs_2_), channel_id=1, source_target_pairs={{0,4},{1,29},{4,0},{5,9},{8,12},{9,5},{12,8},{13,17},{16,20},{17,1... | collective-permute-start | bytes 2359304 | tf_op jit(solution)/shard_map/ppermute | solution.py:50
  47.3 44.2 %collective-permute-start.2 = (bf16[4,192,896]{2,1,0:T(8,128)(2,1)S(1)}, bf16[4,192,896]{2,1,0:T(8,128)(2,1)S(1)}, u32[]{:S(2)}, u32[]{:S(2)}) collective-permute-start(bf16[4,192,896]{2,1,0:T(8,128)(2,1)S(1)} %pad_maximum_fusion.1.refs_1_), channel_id=1, source_target_pairs={{0,96},{1,33},{4,100},{5,37},{8,104},{9,41},{12,108},{13,45},{16,1... | collective-permute-start | bytes 4128776 | tf_op jit(solution)/shard_map/ppermute | solution.py:50
  54.2 37.3 %collective-permute-start.5 = (bf16[4,192,896]{2,1,0:T(8,128)(2,1)S(1)}, bf16[4,192,896]{2,1,0:T(8,128)(2,1)S(1)}, u32[]{:S(2)}, u32[]{:S(2)}) collective-permute-start(bf16[4,192,896]{2,1,0:T(8,128)(2,1)S(1)} %constant_dynamic-update-slice_fusion.refs_2_), channel_id=1, source_target_pairs={{0,96},{1,33},{4,100},{5,37},{8,104},{9,41},{12,108},{13,45},{16,1... | collective-permute-start | bytes 4128776 | tf_op jit(solution)/shard_map/ppermute | solution.py:50
  62.9 20.4 %collective-permute-start.19 = (bf16[4,192,512]{2,1,0:T(8,128)(2,1)S(1)}, bf16[4,192,512]{2,1,0:T(8,128)(2,1)S(1)}, u32[]{:S(2)}, u32[]{:S(2)}) collective-permute-start(bf16[4,192,512]{2,1,0:T(8,128)(2,1)S(1)} %collective-permute-done.18.refs_2_), channel_id=1, source_target_pairs={{0,4},{1,29},{4,0},{5,9},{8,12},{9,5},{12,8},{13,17},{16,20},{17,1... | collective-permute-start | bytes 2359304 | tf_op jit(solution)/shard_map/ppermute | solution.py:50
  63.1 28.4 %collective-permute-start.11 = (bf16[4,192,640]{2,1,0:T(8,128)(2,1)S(1)}, bf16[4,192,640]{2,1,0:T(8,128)(2,1)S(1)}, u32[]{:S(2)}, u32[]{:S(2)}) collective-permute-start(bf16[4,192,640]{2,1,0:T(8,128)(2,1)S(1)} %constant_dynamic-update-slice_fusion.2.refs_4_), channel_id=1, source_target_pairs={{0,130},{1,129},{4,134},{5,133},{8,138},{9,137},{12,142},{13,141},... | collective-permute-start | bytes 2949128 | tf_op jit(solution)/shard_map/ppermute | solution.py:50
  64.1 29.0 %collective-permute-start.17 = (bf16[4,192,512]{2,1,0:T(8,128)(2,1)S(1)}, bf16[4,192,512]{2,1,0:T(8,128)(2,1)S(1)}, u32[]{:S(2)}, u32[]{:S(2)}) collective-permute-start(bf16[4,192,512]{2,1,0:T(8,128)(2,1)S(1)} %collective-permute-done.16.refs_3_), channel_id=1, source_target_pairs={{0,28},{1,5},{4,8},{5,1},{8,4},{9,13},{12,16},{13,9},{16,12},{17,2... | collective-permute-start | bytes 2359304 | tf_op jit(solution)/shard_map/ppermute | solution.py:50
  83.3 13.9 %collective-permute-start.23 = (bf16[4,192,512]{2,1,0:T(8,128)(2,1)S(1)}, bf16[4,192,512]{2,1,0:T(8,128)(2,1)S(1)}, u32[]{:S(2)}, u32[]{:S(2)}) collective-permute-start(bf16[4,192,512]{2,1,0:T(8,128)(2,1)S(1)} %collective-permute-done.19.refs_3_), channel_id=1, source_target_pairs={{0,28},{1,5},{4,8},{5,1},{8,4},{9,13},{12,16},{13,9},{16,12},{17,2... | collective-permute-start | bytes 2359304 | tf_op jit(solution)/shard_map/ppermute | solution.py:50
  96.6 4.7 %collective-permute-start.20 = (f32[384,512]{1,0:T(8,128)S(1)}, f32[384,512]{1,0:T(8,128)S(1)}, u32[]{:S(2)}, u32[]{:S(2)}) collective-permute-start(f32[384,512]{1,0:T(8,128)S(1)} %get-tuple-element.37), channel_id=1, source_target_pairs={{0,1},{1,0},{4,5},{5,4},{8,9},{9,8},{12,13},{13,12},{16,17},{17,16... | collective-permute-start | bytes 2359304 | tf_op jit(solution)/shard_map/ppermute | solution.py:50
  96.7 4.6 %collective-permute-start.21 = (f32[384,512]{1,0:T(8,128)S(1)}, f32[384,512]{1,0:T(8,128)S(1)}, u32[]{:S(2)}, u32[]{:S(2)}) collective-permute-start(f32[384,512]{1,0:T(8,128)S(1)} %get-tuple-element.38), channel_id=1, source_target_pairs={{0,1},{1,0},{4,5},{5,4},{8,9},{9,8},{12,13},{13,12},{16,17},{17,16... | collective-permute-start | bytes 2359304 | tf_op jit(solution)/shard_map/ppermute | solution.py:50
  100.7 6.0 %collective-permute-start.24 = (f32[384,512]{1,0:T(8,128)S(1)}, f32[384,512]{1,0:T(8,128)S(1)}, u32[]{:S(2)}, u32[]{:S(2)}) collective-permute-start(f32[384,512]{1,0:T(8,128)S(1)} %get-tuple-element.41), channel_id=1, source_target_pairs={{0,1},{1,0},{4,5},{5,4},{8,9},{9,8},{12,13},{13,12},{16,17},{17,16... | collective-permute-start | bytes 2359304 | tf_op jit(solution)/shard_map/ppermute | solution.py:50
  100.9 5.8 %collective-permute-start.25 = (f32[384,512]{1,0:T(8,128)S(1)}, f32[384,512]{1,0:T(8,128)S(1)}, u32[]{:S(2)}, u32[]{:S(2)}) collective-permute-start(f32[384,512]{1,0:T(8,128)S(1)} %get-tuple-element.42), channel_id=1, source_target_pairs={{0,1},{1,0},{4,5},{5,4},{8,9},{9,8},{12,13},{13,12},{16,17},{17,16... | collective-permute-start | bytes 2359304 | tf_op jit(solution)/shard_map/ppermute | solution.py:50
  103.9 13.6 %collective-permute-start.22 = (bf16[384,512]{1,0:T(8,128)(2,1)S(1)}, bf16[384,512]{1,0:T(8,128)(2,1)S(1)}, u32[]{:S(2)}, u32[]{:S(2)}) collective-permute-start(bf16[384,512]{1,0:T(8,128)(2,1)S(1)} %get-tuple-element.40), channel_id=1, source_target_pairs={{0,2},{1,3},{4,6},{5,7},{8,10},{9,11},{12,14},{13,15},{16,18},{17,... | collective-permute-start | bytes 1179656 | tf_op jit(solution)/shard_map/ppermute | solution.py:50
  109.3 15.8 %collective-permute-start.26 = (bf16[384,512]{1,0:T(8,128)(2,1)S(1)}, bf16[384,512]{1,0:T(8,128)(2,1)S(1)}, u32[]{:S(2)}, u32[]{:S(2)}) collective-permute-start(bf16[384,512]{1,0:T(8,128)(2,1)S(1)} %get-tuple-element.44), channel_id=1, source_target_pairs={{0,2},{1,3},{4,6},{5,7},{8,10},{9,11},{12,14},{13,15},{16,18},{17,... | collective-permute-start | bytes 1179656 | tf_op jit(solution)/shard_map/ppermute | solution.py:50

commit v4 on v3

--- a/solution.py
+++ b/solution.py
@@ -9,7 +9,7 @@
 AXES = ("pair", "outv", "conv")
 NX, NY, NZ = 4, 4, 8
 RCHUNKS = 2
-DEPTH_X = 896
+DEPTH_X = 768
 MIB = 1024 * 1024
 VMEM = pltpu.MemorySpace.VMEM
 SMEM = pltpu.MemorySpace.SMEM
@@ -79,20 +79,18 @@
 
 
 def mask_amplitudes_kernel(place, mask_ref, amp_ref, keep_ref, give_ref):
-    width = keep_ref.shape[2]
+    width = keep_ref.shape[1]
     for j in range(amp_ref.shape[0] // TW):
         value = mask_ref[0, place[1] * (amp_ref.shape[0] // TW) + j].astype(jnp.float32)
         rows = pl.ds(j * TW, TW)
         row = jnp.full((1, width), value, jnp.float32).astype(jnp.bfloat16)
-        for out_ref, side in ((keep_ref, place[2]), (give_ref, 1 - place[2])):
-            for r in range(RCHUNKS):
-                first = (side * RCHUNKS + r) * width
-                out_ref[r, rows, :] = amp_ref[rows, pl.ds(pl.multiple_of(first, 128), width)] * row
+        for out_ref, side in ((give_ref, 1 - place[2]), (keep_ref, place[2])):
+            out_ref[rows, :] = amp_ref[rows, pl.ds(pl.multiple_of(side * width, 128), width)] * row
 
 
 def mask_amplitudes(place, amp_mask, amp_t):
     rows, width = amp_t.shape
-    shape = jax.ShapeDtypeStruct((RCHUNKS, rows, width // (2 * RCHUNKS)), jnp.bfloat16)
+    shape = jax.ShapeDtypeStruct((rows, width // 2), jnp.bfloat16)
     return pl.pallas_call(
         mask_amplitudes_kernel,
         in_specs=[pl.BlockSpec(memory_space=SMEM), pl.BlockSpec(memory_space=SMEM), pl.BlockSpec(memory_space=VMEM)],
@@ -103,11 +101,8 @@
     )(place, amp_mask, amp_t)
 
 
-def after(array, *others):
-    return lax.optimization_barrier((array, *others))[0]
-
-
-def ring_of_eight(near):
+def ring_of_eight(own):
+    near = jnp.stack([own, send(own, Z_FIRST)])
     second = send(near, Z_OTHER)
     third = send(second, Z_FIRST)
     fourth = send(third, Z_OTHER)
@@ -124,52 +119,56 @@
     return pieces
 
 
-def order_amplitudes_kernel(first_step, steps, place, *refs):
-    pieces = refs[:steps]
+def order_amplitudes_kernel(origins, place, *refs):
+    pieces = refs[: len(origins)]
     out_ref, sems = refs[-2:]
     z, x_hi, c = place[1], place[2], place[5]
     rows = pieces[0].shape[1]
     sz = 1 - 2 * ((z + c) % 2)
     copies = []
-    for step, piece in enumerate(pieces):
-        for chain in range(2):
-            hi = x_hi if chain == 0 else 1 - x_hi
-            for e in range(2):
-                z_from = (z + sz * RING8[2 * (first_step + step) + e] + NZ) % NZ
-                row = pl.multiple_of((hi * NZ + z_from) * rows, rows)
-                for col in range(0, piece.shape[2], 128):
-                    copies.append(
-                        pltpu.make_async_copy(
-                            piece.at[2 * chain + e, :, pl.ds(col, 128)],
-                            out_ref.at[pl.ds(row, rows), pl.ds(col, 128)],
-                            sems.at[len(copies)],
-                        )
+    for (chain, step), piece in zip(origins, pieces):
+        hi = x_hi if chain == 0 else 1 - x_hi
+        for e in range(2):
+            z_from = (z + sz * RING8[2 * step + e] + NZ) % NZ
+            row = pl.multiple_of((hi * NZ + z_from) * rows, rows)
+            for col in range(0, piece.shape[2], 256):
+                copies.append(
+                    pltpu.make_async_copy(
+                        piece.at[e, :, pl.ds(col, 256)],
+                        out_ref.at[pl.ds(row, rows), pl.ds(col, 256)],
+                        sems.at[len(copies)],
                     )
+                )
     for copy in copies:
         copy.start()
     for copy in copies:
         copy.wait()
 
 
-def order_amplitudes(place, pieces, first_step, held=()):
-    _, rows, width = pieces[0].shape
-    steps = len(pieces)
+def order_amplitudes(place, chains):
+    _, rows, width = chains[0][0].shape
     any_spec, vmem_spec = pl.BlockSpec(memory_space=pl.ANY), pl.BlockSpec(memory_space=VMEM)
-
-    def kernel(*refs):
-        order_amplitudes_kernel(first_step, steps, *refs)
-
-    return pl.pallas_call(
-        kernel,
-        in_specs=[pl.BlockSpec(memory_space=SMEM)] + [any_spec] * steps + [vmem_spec] * len(held),
-        out_specs=vmem_spec,
-        out_shape=pltpu.VMEM((16 * rows, width), jnp.bfloat16),
-        scratch_shapes=[pltpu.SemaphoreType.DMA((4 * steps * width // 128,))],
-        input_output_aliases={1 + steps: 0} if held else {},
-        cost_estimate=pl.CostEstimate(flops=0, bytes_accessed=16 * steps * rows * width, transcendentals=0),
-        compiler_params=pltpu.CompilerParams(vmem_limit_bytes=MIB),
-        name="order_amplitudes",
-    )(place, *pieces, *held)
+    held = []
+    for origins in (((0, 0), (1, 0), (0, 1), (1, 1), (0, 2), (1, 2)), ((0, 3),), ((1, 3),)):
+        pieces = [chains[chain][step] for chain, step in origins]
+
+        def kernel(*refs, origins=origins):
+            order_amplitudes_kernel(origins, *refs)
+
+        held = [
+            pl.pallas_call(
+                kernel,
+                in_specs=[pl.BlockSpec(memory_space=SMEM)] + [any_spec] * len(pieces) + [vmem_spec] * len(held),
+                out_specs=vmem_spec,
+                out_shape=pltpu.VMEM((16 * rows, width), jnp.bfloat16),
+                scratch_shapes=[pltpu.SemaphoreType.DMA((2 * len(pieces) * width // 256,))],
+                input_output_aliases={1 + len(pieces): 0} if held else {},
+                cost_estimate=pl.CostEstimate(flops=0, bytes_accessed=8 * len(pieces) * rows * width, transcendentals=0),
+                compiler_params=pltpu.CompilerParams(vmem_limit_bytes=MIB),
+                name="order_amplitudes",
+            )(place, *pieces, *held)
+        ]
+    return held[0]
 
 
 def order_integrals_kernel(got, place, *refs):
@@ -226,21 +225,25 @@
     return held
 
 
-def multiply_kernel(int_ref, amp_ref, *refs):
+def multiply_kernel(cols, int_ref, amp_ref, *refs):
     rows = int_ref.shape[0] // 2
     other_refs, outs = refs[:-2], refs[-2:]
     for side in range(2):
-        total = jnp.dot(int_ref[pl.ds(side * rows, rows), :], amp_ref[...], preferred_element_type=jnp.float32)
+        total = jnp.dot(int_ref[pl.ds(side * rows, rows), :], amp_ref[:, cols], preferred_element_type=jnp.float32)
         if other_refs:
             total = (total + other_refs[side][...]).astype(jnp.bfloat16)
         outs[side][...] = total
 
 
-def multiply(ints, amps, *other):
-    rows, depth, width = ints.shape[0] // 2, ints.shape[1], amps.shape[1]
+def multiply(r, ints, amps, *other):
+    rows, depth, width = ints.shape[0] // 2, ints.shape[1], amps.shape[1] // RCHUNKS
     vmem_spec = pl.BlockSpec(memory_space=VMEM)
+
+    def kernel(*refs):
+        multiply_kernel(slice(r * width, (r + 1) * width), *refs)
+
     return pl.pallas_call(
-        multiply_kernel,
+        kernel,
         in_specs=[vmem_spec] * (2 + len(other)),
         out_specs=[vmem_spec] * 2,
         out_shape=[jax.ShapeDtypeStruct((rows, width), jnp.bfloat16 if other else jnp.float32)] * 2,
@@ -258,23 +261,18 @@
     x_lo, y = pair // NY, pair % NY
     place = jnp.stack([pair, z, x_hi, x_hi * 2 + x_lo, y, core]).astype(jnp.int32)
 
-    first, second = mask_integrals(place, int_mask, integrals.T)
-    place, first, second = lax.optimization_barrier((place, first, second))
     keep, give = mask_amplitudes(place, amp_mask, amplitudes.T)
-    keep_got = send(keep, Z_FIRST)
-    partner = send(give, X_ACROSS)
-    partner_got = send(partner, Z_FIRST)
+    int_t, keep, give = lax.optimization_barrier((integrals.T, keep, give))
+    first, second = mask_integrals(place, int_mask, int_t)
+    chains = [ring_of_eight(keep), ring_of_eight(send(give, X_ACROSS))]
     ints = plane(first, (X_FIRST, X_OTHER), (Y_FIRST, Y_OTHER)) + plane(second, (Y_FIRST, Y_OTHER), (X_FIRST, X_OTHER))
-    rings = [ring_of_eight(jnp.stack([keep[r], keep_got[r], partner[r], partner_got[r]])) for r in range(RCHUNKS)]
-    held = [order_amplitudes(place, ring[:3], 0) for ring in rings]
-    held[0] = after(*held)
-    amps = [order_amplitudes(place, ring[3:], 3, [part]) for ring, part in zip(rings, held)]
+    amps = order_amplitudes(place, chains)
     other_ints, own_ints = order_integrals(place, ints)
 
     kept, received = [], []
-    for columns in amps:
-        partials = [send(partial, CORE) for partial in multiply(other_ints, columns)]
-        theirs, mine = multiply(own_ints, columns, *partials)
+    for r in range(RCHUNKS):
+        partials = [send(partial, CORE) for partial in multiply(r, other_ints, amps)]
+        theirs, mine = multiply(r, own_ints, amps, *partials)
         kept.append(mine)
         received.append(send(theirs, X_ACROSS))
     low = [jnp.where(x_hi == 0, k, g) for k, g in zip(kept, received)]

time: 129 us -> 123 us (0.953)
  waiting for transfers between devices: 60.8 us -> 55.7 us
  starting transfers between devices: 39.6 us -> 41.6 us
  Pallas kernels: 19.8 us -> 18.1 us
    ppermute x27, waiting for transfers between devices: 60.8 us -> 55.7 us  [send(): return lax.ppermute(array, AXES, plan)]
    ppermute x27, starting transfers between devices: 39.6 us -> 41.6 us  [send(): return lax.ppermute(array, AXES, plan)]
    pallas_call x4 -> x3, Pallas kernels: 4.76 us -> 3.33 us  [order_amplitudes(): pl.pallas_call(kernel, in_specs=[pl.BlockSpec(memory_space=SMEM)] + [any_...]
  transfers between devices with their start and end apart: 27 -> 27, of which waited for: 9 -> 11; matrix products, arithmetic and copies ran while one was open for 1% -> 1% of each run, Pallas kernels for 15% -> 11%
where the time goes in v4:
time: 123 us; the launch traced here: 121 us
  waiting for transfers between devices  55.7 us (45%)
  starting transfers between devices  41.6 us (34%)
  Pallas kernels  18.1 us (15%)
  local copies, waits for them, and re-layouts  3.18 us (3%)
  other arithmetic  1.95 us (2%)
    ppermute x27, waiting for transfers between devices, send(): return lax.ppermute(array, AXES, plan)  55.7 us
    ppermute x27, starting transfers between devices, send(): return lax.ppermute(array, AXES, plan)  41.6 us
    pallas_call x4, Pallas kernels, multiply(): pl.pallas_call(kernel, in_specs=[vmem_spec] * (2 + len(other)), out_specs...  10.4 us
    pallas_call x3, Pallas kernels, order_amplitudes(): pl.pallas_call(kernel, in_specs=[pl.BlockSpec(memory_space=SMEM)] + [any_...  3.33 us
    unnamed x10, local copies, waits for them, and re-layouts  3.02 us
    pallas_call x2, Pallas kernels, order_integrals(): pl.pallas_call(kernel, in_specs=[pl.BlockSpec(memory_space=SMEM)] + [any_...  2.96 us
  transfers between devices with their start and end apart: 27, of which 11 were waited for; matrix products, arithmetic and copies ran while one was open for 1% of the time, Pallas kernels for 11%

profile of v4, /device:TPU:24, one launch (start us, length us, event | category | flops | bytes accessed | tf_op | source)
XLA Modules:
  0.0 120.7 jit_solution(6799702604227417522)
XLA Ops:
  0.1 1.1 copy-done
  1.2 0.7 copy-done.3
  1.9 0.6 mask_amplitudes.1
  2.5 0.5 copy-done.1
  2.9 0.7 copy-done.2
  3.6 0.8 mask_integrals.1
  4.5 1.6 %collective-permute-start = (bf16[192,768]{1,0:T(8,128)(2,1)S(1)}, bf16[192,768]{1,0:T(8,128)(2,1)S(1)}, u32[]{:S(2)}, u32[]{:S(2)}) collective-permute-start(bf16[192,768]{1,0:T(8,128)(2,1)S(1)} %get-tuple-element.27), channel_id=1, source_target_pairs={{0,128},{1,131},{4,132},{5,135},{8,136},{9,139},{12,140},{13,143},... | collective-permute-start | bytes 884744 | tf_op jit(solution)/shard_map/ppermute | solution.py:50
  6.0 1.9 %collective-permute-start.17 = (bf16[192,1024]{1,0:T(8,128)(2,1)S(1)}, bf16[192,1024]{1,0:T(8,128)(2,1)S(1)}, u32[]{:S(2)}, u32[]{:S(2)}) collective-permute-start(bf16[192,1024]{1,0:T(8,128)(2,1)S(1)} %get-tuple-element.33), channel_id=1, source_target_pairs={{0,4},{1,29},{4,0},{5,9},{8,12},{9,5},{12,8},{13,17},{16,20},{17,1... | collective-permute-start | bytes 1179656 | tf_op jit(solution)/shard_map/ppermute | solution.py:50
  7.9 2.7 %collective-permute-start.12 = (bf16[192,1024]{1,0:T(8,128)(2,1)S(1)}, bf16[192,1024]{1,0:T(8,128)(2,1)S(1)}, u32[]{:S(2)}, u32[]{:S(2)}) collective-permute-start(bf16[192,1024]{1,0:T(8,128)(2,1)S(1)} %get-tuple-element.32), channel_id=1, source_target_pairs={{0,2},{1,3},{4,6},{5,7},{8,10},{9,11},{12,14},{13,15},{16,18},{17,... | collective-permute-start | bytes 1179656 | tf_op jit(solution)/shard_map/ppermute | solution.py:50
  10.7 0.7 collective-permute-start.6
  11.5 1.4 %collective-permute-start.1 = (bf16[2,192,768]{2,1,0:T(8,128)(2,1)S(1)}, bf16[2,192,768]{2,1,0:T(8,128)(2,1)S(1)}, u32[]{:S(2)}, u32[]{:S(2)}) collective-permute-start(bf16[2,192,768]{2,1,0:T(8,128)(2,1)S(1)} %pad_maximum_fusion.5), channel_id=1, source_target_pairs={{0,32},{1,97},{4,36},{5,101},{8,40},{9,105},{12,44},{13,109},{16,4... | collective-permute-start | bytes 1769480 | tf_op jit(solution)/shard_map/ppermute | solution.py:50
  12.9 1.0 collective-permute-done.17
  13.9 6.8 %collective-permute-start.18 = (bf16[2,192,1024]{2,1,0:T(8,128)(2,1)S(1)}, bf16[2,192,1024]{2,1,0:T(8,128)(2,1)S(1)}, u32[]{:S(2)}, u32[]{:S(2)}) collective-permute-start(bf16[2,192,1024]{2,1,0:T(8,128)(2,1)S(1)} %pad_maximum_fusion.4.refs_1_), channel_id=1, source_target_pairs={{0,28},{1,5},{4,8},{5,1},{8,4},{9,13},{12,16},{13,9},{16,12},{17,2... | collective-permute-start | bytes 2359304 | tf_op jit(solution)/shard_map/ppermute | solution.py:50
  20.7 3.1 %collective-permute-start.13 = (bf16[192,1024]{1,0:T(8,128)(2,1)S(1)}, bf16[192,1024]{1,0:T(8,128)(2,1)S(1)}, u32[]{:S(2)}, u32[]{:S(2)}) collective-permute-start(bf16[192,1024]{1,0:T(8,128)(2,1)S(1)} %collective-permute-done.12), channel_id=1, source_target_pairs={{0,4},{1,29},{4,0},{5,9},{8,12},{9,5},{12,8},{13,17},{16,20},{17,1... | collective-permute-start | bytes 1179656 | tf_op jit(solution)/shard_map/ppermute | solution.py:50
  23.8 0.6 collective-permute-start.3
  24.5 0.2 collective-permute-start.7
  24.7 8.6 %collective-permute-done.13 = bf16[192,1024]{1,0:T(8,128)(2,1)S(1)} collective-permute-done((bf16[192,1024]{1,0:T(8,128)(2,1)S(1)}, bf16[192,1024]{1,0:T(8,128)(2,1)S(1)}, u32[]{:S(2)}, u32[]{:S(2)}) %collective-permute-start.13) | collective-permute-done | bytes 393248 | tf_op jit(solution)/shard_map/ppermute | solution.py:50
  33.3 0.2 collective-permute-start.9
  33.6 4.0 %collective-permute-start.14 = (bf16[2,192,1024]{2,1,0:T(8,128)(2,1)S(1)}, bf16[2,192,1024]{2,1,0:T(8,128)(2,1)S(1)}, u32[]{:S(2)}, u32[]{:S(2)}) collective-permute-start(bf16[2,192,1024]{2,1,0:T(8,128)(2,1)S(1)} %pad_maximum_fusion.3.refs_2_), channel_id=1, source_target_pairs={{0,28},{1,5},{4,8},{5,1},{8,4},{9,13},{12,16},{13,9},{16,12},{17,2... | collective-permute-start | bytes 2359304 | tf_op jit(solution)/shard_map/ppermute | solution.py:50
  37.6 1.9 %collective-permute-done.3 = bf16[2,192,768]{2,1,0:T(8,128)(2,1)S(1)} collective-permute-done((bf16[2,192,768]{2,1,0:T(8,128)(2,1)S(1)}, bf16[2,192,768]{2,1,0:T(8,128)(2,1)S(1)}, u32[]{:S(2)}, u32[]{:S(2)}) %collective-permute-start.3) | collective-permute-done | bytes 589856 | tf_op jit(solution)/shard_map/ppermute | solution.py:50
  39.5 0.6 collective-permute-start.4
  40.1 1.1 collective-permute-start.19
  41.6 3.4 %collective-permute-done.9 = bf16[2,192,768]{2,1,0:T(8,128)(2,1)S(1)} collective-permute-done((bf16[2,192,768]{2,1,0:T(8,128)(2,1)S(1)}, bf16[2,192,768]{2,1,0:T(8,128)(2,1)S(1)}, u32[]{:S(2)}, u32[]{:S(2)}) %collective-permute-start.9) | collective-permute-done | bytes 589856 | tf_op jit(solution)/shard_map/ppermute | solution.py:50
  45.1 8.8 %collective-permute-done.14.refs_4_ = bf16[2,192,1024]{2,1,0:T(8,128)(2,1)S(1)} collective-permute-done((bf16[2,192,1024]{2,1,0:T(8,128)(2,1)S(1)}, bf16[2,192,1024]{2,1,0:T(8,128)(2,1)S(1)}, u32[]{:S(2)}, u32[]{:S(2)}) %collective-permute-start.14) | collective-permute-done | bytes 786464 | tf_op jit(solution)/shard_map/ppermute | solution.py:50
  54.0 1.8 %collective-permute-done.4 = bf16[2,192,768]{2,1,0:T(8,128)(2,1)S(1)} collective-permute-done((bf16[2,192,768]{2,1,0:T(8,128)(2,1)S(1)}, bf16[2,192,768]{2,1,0:T(8,128)(2,1)S(1)}, u32[]{:S(2)}, u32[]{:S(2)}) %collective-permute-start.4) | collective-permute-done | bytes 589856 | tf_op jit(solution)/shard_map/ppermute | solution.py:50
  55.8 0.8 collective-permute-start.8
  56.7 2.9 %collective-permute-start.5 = (bf16[4,192,768]{2,1,0:T(8,128)(2,1)S(1)}, bf16[4,192,768]{2,1,0:T(8,128)(2,1)S(1)}, u32[]{:S(2)}, u32[]{:S(2)}) collective-permute-start(bf16[4,192,768]{2,1,0:T(8,128)(2,1)S(1)} %constant_dynamic-update-slice_fusion.refs_2_), channel_id=1, source_target_pairs={{0,96},{1,33},{4,100},{5,37},{8,104},{9,41},{12,108},{13,45},{16,1... | collective-permute-start | bytes 3538952 | tf_op jit(solution)/shard_map/ppermute | solution.py:50
  59.7 3.6 %collective-permute-done.2.refs_1_ = bf16[4,192,768]{2,1,0:T(8,128)(2,1)S(1)} collective-permute-done((bf16[4,192,768]{2,1,0:T(8,128)(2,1)S(1)}, bf16[4,192,768]{2,1,0:T(8,128)(2,1)S(1)}, u32[]{:S(2)}, u32[]{:S(2)}) %collective-permute-start.2) | collective-permute-done | bytes 1179680 | tf_op jit(solution)/shard_map/ppermute | solution.py:50
  63.3 5.5 %collective-permute-start.20 = (bf16[2,192,1024]{2,1,0:T(8,128)(2,1)S(1)}, bf16[2,192,1024]{2,1,0:T(8,128)(2,1)S(1)}, u32[]{:S(2)}, u32[]{:S(2)}) collective-permute-start(bf16[2,192,1024]{2,1,0:T(8,128)(2,1)S(1)} %collective-permute-done.19.refs_5_), channel_id=1, source_target_pairs={{0,28},{1,5},{4,8},{5,1},{8,4},{9,13},{12,16},{13,9},{16,12},{17,2... | collective-permute-start | bytes 2359304 | tf_op jit(solution)/shard_map/ppermute | solution.py:50
  68.8 2.0 %collective-permute-start.16 = (bf16[2,192,1024]{2,1,0:T(8,128)(2,1)S(1)}, bf16[2,192,1024]{2,1,0:T(8,128)(2,1)S(1)}, u32[]{:S(2)}, u32[]{:S(2)}) collective-permute-start(bf16[2,192,1024]{2,1,0:T(8,128)(2,1)S(1)} %collective-permute-done.15.refs_6_), channel_id=1, source_target_pairs={{0,28},{1,5},{4,8},{5,1},{8,4},{9,13},{12,16},{13,9},{16,12},{17,2... | collective-permute-start | bytes 2359304 | tf_op jit(solution)/shard_map/ppermute | solution.py:50
  70.8 1.5 %order_integrals.2 = (bf16[768,3072]{1,0:T(8,128)(2,1)S(1)}, bf16[768,3072]{1,0:T(8,128)(2,1)S(1)}) custom-call(s32[6]{0:T(128)S(1)} %stack.63.place.refs_0_, bf16[4,192,768]{2,1,0:T(8,128)(2,1)S(1)} %pad_maximum_fusion.1.refs_1_, bf16[4,192,768]{2,1,0:T(8,128)(2,1)S(1)} %constant_dynamic-update-slice_fusion.refs_2_, ...), custom_call_target="tpu_custom_call" | custom-call | bytes 9437184 | tf_op jit(solution)/shard_map/order_integrals/pallas_call | solution.py:214
  72.2 1.8 %order_amplitudes.3.refs_2_ = bf16[3072,1024]{1,0:T(8,128)(2,1)S(1)} custom-call(s32[6]{0:T(128)S(1)} %stack.63.place.refs_0_, bf16[2,192,1024]{2,1,0:T(8,128)(2,1)S(1)} %pad_maximum_fusion.4.refs_1_, bf16[2,192,1024]{2,1,0:T(8,128)(2,1)S(1)} %pad_maximum_fusion.3.refs_2_, bf16[2,192,1024]{2,1,0:T(8,128)(2,1)S(1)} %collective-permute-done.18.refs_3_, ...), custom_call_target="tpu_custom_call" | custom-call | bytes 9437184 | tf_op jit(solution)/shard_map/order_amplitudes/pallas_call | solution.py:159
  74.1 1.9 %collective-permute-done.5.refs_2_ = bf16[4,192,768]{2,1,0:T(8,128)(2,1)S(1)} collective-permute-done((bf16[4,192,768]{2,1,0:T(8,128)(2,1)S(1)}, bf16[4,192,768]{2,1,0:T(8,128)(2,1)S(1)}, u32[]{:S(2)}, u32[]{:S(2)}) %collective-permute-start.5) | collective-permute-done | bytes 1179680 | tf_op jit(solution)/shard_map/ppermute | solution.py:50
  76.0 9.9 %collective-permute-done.11.refs_4_ = bf16[4,192,768]{2,1,0:T(8,128)(2,1)S(1)} collective-permute-done((bf16[4,192,768]{2,1,0:T(8,128)(2,1)S(1)}, bf16[4,192,768]{2,1,0:T(8,128)(2,1)S(1)}, u32[]{:S(2)}, u32[]{:S(2)}) %collective-permute-start.11) | collective-permute-done | bytes 1179680 | tf_op jit(solution)/shard_map/ppermute | solution.py:50
  85.9 1.5 %order_integrals.3 = (bf16[768,3072]{1,0:T(8,128)(2,1)S(1)}, bf16[768,3072]{1,0:T(8,128)(2,1)S(1)}) custom-call(s32[6]{0:T(128)S(1)} %stack.63.place.refs_0_, bf16[4,192,768]{2,1,0:T(8,128)(2,1)S(1)} %collective-permute-done.2.refs_1_, bf16[4,192,768]{2,1,0:T(8,128)(2,1)S(1)} %collective-permute-done.5.refs_2_, ...), custom_call_target="tpu_custom_call", output_to_operand_aliasing={{0}: (5, {}), {1}: (6, {})} | custom-call | bytes 9437184 | tf_op jit(solution)/shard_map/order_integrals/pallas_call | solution.py:214
  87.4 0.8 order_amplitudes.4.refs_2_
  88.1 0.8 order_amplitudes.5.refs_1_
  88.9 2.6 %multiply_other.3 = (f32[384,512]{1,0:T(8,128)S(1)}, f32[384,512]{1,0:T(8,128)S(1)}) custom-call(bf16[768,3072]{1,0:T(8,128)(2,1)S(1)} %get-tuple-element.34.refs_0_, bf16[3072,1024]{1,0:T(8,128)(2,1)S(1)} %order_amplitudes.5.refs_1_), custom_call_target="tpu_custom_call" | custom-call | flops 2415919104 | bytes 9437184 | tf_op jit(solution)/shard_map/multiply_other/pallas_call | solution.py:245
  91.6 0.5 collective-permute-start.25
  92.1 2.6 %multiply_other.2 = (f32[384,512]{1,0:T(8,128)S(1)}, f32[384,512]{1,0:T(8,128)S(1)}) custom-call(bf16[768,3072]{1,0:T(8,128)(2,1)S(1)} %get-tuple-element.34.refs_0_, bf16[3072,1024]{1,0:T(8,128)(2,1)S(1)} %order_amplitudes.5.refs_1_), custom_call_target="tpu_custom_call" | custom-call | flops 2415919104 | bytes 9437184 | tf_op jit(solution)/shard_map/multiply_other/pallas_call | solution.py:245
  94.9 0.4 collective-permute-start.22
  95.3 2.6 %multiply_own.3 = (bf16[384,512]{1,0:T(8,128)(2,1)S(1)}, bf16[384,512]{1,0:T(8,128)(2,1)S(1)}) custom-call(bf16[768,3072]{1,0:T(8,128)(2,1)S(1)} %get-tuple-element.31.refs_0_, bf16[3072,1024]{1,0:T(8,128)(2,1)S(1)} %order_amplitudes.5.refs_1_, f32[384,512]{1,0:T(8,128)S(1)} %collective-permute-done.24.refs_2_, f32[384,512]{1,0:T(8,128)S(1)} %collective-permute-done.25.refs_3_), custom_call_target="tpu_custom_call" | custom-call | flops 2415919104 | bytes 9437184 | tf_op jit(solution)/shard_map/multiply_own/pallas_call | solution.py:245
  97.9 1.5 %collective-permute-start.26 = (bf16[384,512]{1,0:T(8,128)(2,1)S(1)}, bf16[384,512]{1,0:T(8,128)(2,1)S(1)}, u32[]{:S(2)}, u32[]{:S(2)}) collective-permute-start(bf16[384,512]{1,0:T(8,128)(2,1)S(1)} %get-tuple-element.42), channel_id=1, source_target_pairs={{0,2},{1,3},{4,6},{5,7},{8,10},{9,11},{12,14},{13,15},{16,18},{17,... | collective-permute-start | bytes 1179656 | tf_op jit(solution)/shard_map/ppermute | solution.py:50
  99.4 2.6 %multiply_own.2 = (bf16[384,512]{1,0:T(8,128)(2,1)S(1)}, bf16[384,512]{1,0:T(8,128)(2,1)S(1)}) custom-call(bf16[768,3072]{1,0:T(8,128)(2,1)S(1)} %get-tuple-element.31.refs_0_, bf16[3072,1024]{1,0:T(8,128)(2,1)S(1)} %order_amplitudes.5.refs_1_, f32[384,512]{1,0:T(8,128)S(1)} %collective-permute-done.21.refs_2_, f32[384,512]{1,0:T(8,128)S(1)} %collective-permute-done.22.refs_3_), custom_call_target="tpu_custom_call" | custom-call | flops 2415919104 | bytes 9437184 | tf_op jit(solution)/shard_map/multiply_own/pallas_call | solution.py:245
  102.0 2.4 %collective-permute-start.23 = (bf16[384,512]{1,0:T(8,128)(2,1)S(1)}, bf16[384,512]{1,0:T(8,128)(2,1)S(1)}, u32[]{:S(2)}, u32[]{:S(2)}) collective-permute-start(bf16[384,512]{1,0:T(8,128)(2,1)S(1)} %get-tuple-element.38), channel_id=1, source_target_pairs={{0,2},{1,3},{4,6},{5,7},{8,10},{9,11},{12,14},{13,15},{16,18},{17,... | collective-permute-start | bytes 1179656 | tf_op jit(solution)/shard_map/ppermute | solution.py:50
  104.5 7.2 %collective-permute-done.26 = bf16[384,512]{1,0:T(8,128)(2,1)S(1)} collective-permute-done((bf16[384,512]{1,0:T(8,128)(2,1)S(1)}, bf16[384,512]{1,0:T(8,128)(2,1)S(1)}, u32[]{:S(2)}, u32[]{:S(2)}) %collective-permute-start.26) | collective-permute-done | bytes 393248 | tf_op jit(solution)/shard_map/ppermute | solution.py:50
  111.8 7.5 %collective-permute-done.23 = bf16[384,512]{1,0:T(8,128)(2,1)S(1)} collective-permute-done((bf16[384,512]{1,0:T(8,128)(2,1)S(1)}, bf16[384,512]{1,0:T(8,128)(2,1)S(1)}, u32[]{:S(2)}, u32[]{:S(2)}) %collective-permute-start.23) | collective-permute-done | bytes 393248 | tf_op jit(solution)/shard_map/ppermute | solution.py:50
  119.3 1.3 %pad_maximum_fusion = bf16[384,2048]{1,0:T(8,128)(2,1)} fusion(bf16[384,512]{1,0:T(8,128)(2,1)S(1)} %get-tuple-element.46, bf16[384,512]{1,0:T(8,128)(2,1)S(1)} %get-tuple-element.44, bf16[384,512]{1,0:T(8,128)(2,1)S(1)} %get-tuple-element.45, bf16[384,512]{1,0:T(8,128)(2,1)S(1)} %get-tuple-element.43), kind=kLoop, calls=%fused_computation | loop fusion | flops 6291456 | bytes 3145728 | tf_op jit(solution)/shard_map/concatenate | solution.py:280
  (39 shorter events, 1.5 us)
Async XLA Ops:
  0.1 1.1 copy-start
  1.2 0.7 copy-start.3
  1.9 1.1 copy-start.1
  2.9 0.7 copy-start.2
  4.5 7.0 %collective-permute-start = (bf16[192,768]{1,0:T(8,128)(2,1)S(1)}, bf16[192,768]{1,0:T(8,128)(2,1)S(1)}, u32[]{:S(2)}, u32[]{:S(2)}) collective-permute-start(bf16[192,768]{1,0:T(8,128)(2,1)S(1)} %get-tuple-element.27), channel_id=1, source_target_pairs={{0,128},{1,131},{4,132},{5,135},{8,136},{9,139},{12,140},{13,143},... | collective-permute-start | bytes 884744 | tf_op jit(solution)/shard_map/ppermute | solution.py:50
  6.0 7.8 %collective-permute-start.17 = (bf16[192,1024]{1,0:T(8,128)(2,1)S(1)}, bf16[192,1024]{1,0:T(8,128)(2,1)S(1)}, u32[]{:S(2)}, u32[]{:S(2)}) collective-permute-start(bf16[192,1024]{1,0:T(8,128)(2,1)S(1)} %get-tuple-element.33), channel_id=1, source_target_pairs={{0,4},{1,29},{4,0},{5,9},{8,12},{9,5},{12,8},{13,17},{16,20},{17,1... | collective-permute-start | bytes 1179656 | tf_op jit(solution)/shard_map/ppermute | solution.py:50
  7.9 12.8 %collective-permute-start.12 = (bf16[192,1024]{1,0:T(8,128)(2,1)S(1)}, bf16[192,1024]{1,0:T(8,128)(2,1)S(1)}, u32[]{:S(2)}, u32[]{:S(2)}) collective-permute-start(bf16[192,1024]{1,0:T(8,128)(2,1)S(1)} %get-tuple-element.32), channel_id=1, source_target_pairs={{0,2},{1,3},{4,6},{5,7},{8,10},{9,11},{12,14},{13,15},{16,18},{17,... | collective-permute-start | bytes 1179656 | tf_op jit(solution)/shard_map/ppermute | solution.py:50
  10.7 13.7 %collective-permute-start.6 = (bf16[192,768]{1,0:T(8,128)(2,1)S(1)}, bf16[192,768]{1,0:T(8,128)(2,1)S(1)}, u32[]{:S(2)}, u32[]{:S(2)}) collective-permute-start(bf16[192,768]{1,0:T(8,128)(2,1)S(1)} %get-tuple-element.28), channel_id=1, source_target_pairs={{0,32},{1,97},{4,36},{5,101},{8,40},{9,105},{12,44},{13,109},{16,4... | collective-permute-start | bytes 884744 | tf_op jit(solution)/shard_map/ppermute | solution.py:50
  11.5 22.1 %collective-permute-start.1 = (bf16[2,192,768]{2,1,0:T(8,128)(2,1)S(1)}, bf16[2,192,768]{2,1,0:T(8,128)(2,1)S(1)}, u32[]{:S(2)}, u32[]{:S(2)}) collective-permute-start(bf16[2,192,768]{2,1,0:T(8,128)(2,1)S(1)} %pad_maximum_fusion.5), channel_id=1, source_target_pairs={{0,32},{1,97},{4,36},{5,101},{8,40},{9,105},{12,44},{13,109},{16,4... | collective-permute-start | bytes 1769480 | tf_op jit(solution)/shard_map/ppermute | solution.py:50
  13.9 26.3 %collective-permute-start.18 = (bf16[2,192,1024]{2,1,0:T(8,128)(2,1)S(1)}, bf16[2,192,1024]{2,1,0:T(8,128)(2,1)S(1)}, u32[]{:S(2)}, u32[]{:S(2)}) collective-permute-start(bf16[2,192,1024]{2,1,0:T(8,128)(2,1)S(1)} %pad_maximum_fusion.4.refs_1_), channel_id=1, source_target_pairs={{0,28},{1,5},{4,8},{5,1},{8,4},{9,13},{12,16},{13,9},{16,12},{17,2... | collective-permute-start | bytes 2359304 | tf_op jit(solution)/shard_map/ppermute | solution.py:50
  20.7 12.6 %collective-permute-start.13 = (bf16[192,1024]{1,0:T(8,128)(2,1)S(1)}, bf16[192,1024]{1,0:T(8,128)(2,1)S(1)}, u32[]{:S(2)}, u32[]{:S(2)}) collective-permute-start(bf16[192,1024]{1,0:T(8,128)(2,1)S(1)} %collective-permute-done.12), channel_id=1, source_target_pairs={{0,4},{1,29},{4,0},{5,9},{8,12},{9,5},{12,8},{13,17},{16,20},{17,1... | collective-permute-start | bytes 1179656 | tf_op jit(solution)/shard_map/ppermute | solution.py:50
  23.8 15.7 %collective-permute-start.3 = (bf16[2,192,768]{2,1,0:T(8,128)(2,1)S(1)}, bf16[2,192,768]{2,1,0:T(8,128)(2,1)S(1)}, u32[]{:S(2)}, u32[]{:S(2)}) collective-permute-start(bf16[2,192,768]{2,1,0:T(8,128)(2,1)S(1)} %pad_maximum_fusion.5), channel_id=1, source_target_pairs={{0,130},{1,129},{4,134},{5,133},{8,138},{9,137},{12,142},{13,141},... | collective-permute-start | bytes 1769480 | tf_op jit(solution)/shard_map/ppermute | solution.py:50
  24.5 16.9 %collective-permute-start.7 = (bf16[2,192,768]{2,1,0:T(8,128)(2,1)S(1)}, bf16[2,192,768]{2,1,0:T(8,128)(2,1)S(1)}, u32[]{:S(2)}, u32[]{:S(2)}) collective-permute-start(bf16[2,192,768]{2,1,0:T(8,128)(2,1)S(1)} %pad_maximum_fusion.6), channel_id=1, source_target_pairs={{0,128},{1,131},{4,132},{5,135},{8,136},{9,139},{12,140},{13,143},... | collective-permute-start | bytes 1769480 | tf_op jit(solution)/shard_map/ppermute | solution.py:50
  33.3 11.7 %collective-permute-start.9 = (bf16[2,192,768]{2,1,0:T(8,128)(2,1)S(1)}, bf16[2,192,768]{2,1,0:T(8,128)(2,1)S(1)}, u32[]{:S(2)}, u32[]{:S(2)}) collective-permute-start(bf16[2,192,768]{2,1,0:T(8,128)(2,1)S(1)} %pad_maximum_fusion.6), channel_id=1, source_target_pairs={{0,96},{1,33},{4,100},{5,37},{8,104},{9,41},{12,108},{13,45},{16,1... | collective-permute-start | bytes 1769480 | tf_op jit(solution)/shard_map/ppermute | solution.py:50
  33.6 20.3 %collective-permute-start.14 = (bf16[2,192,1024]{2,1,0:T(8,128)(2,1)S(1)}, bf16[2,192,1024]{2,1,0:T(8,128)(2,1)S(1)}, u32[]{:S(2)}, u32[]{:S(2)}) collective-permute-start(bf16[2,192,1024]{2,1,0:T(8,128)(2,1)S(1)} %pad_maximum_fusion.3.refs_2_), channel_id=1, source_target_pairs={{0,28},{1,5},{4,8},{5,1},{8,4},{9,13},{12,16},{13,9},{16,12},{17,2... | collective-permute-start | bytes 2359304 | tf_op jit(solution)/shard_map/ppermute | solution.py:50
  39.5 16.3 %collective-permute-start.4 = (bf16[2,192,768]{2,1,0:T(8,128)(2,1)S(1)}, bf16[2,192,768]{2,1,0:T(8,128)(2,1)S(1)}, u32[]{:S(2)}, u32[]{:S(2)}) collective-permute-start(bf16[2,192,768]{2,1,0:T(8,128)(2,1)S(1)} %collective-permute-done.3), channel_id=1, source_target_pairs={{0,32},{1,97},{4,36},{5,101},{8,40},{9,105},{12,44},{13,109},{16,4... | collective-permute-start | bytes 1769480 | tf_op jit(solution)/shard_map/ppermute | solution.py:50
  40.1 19.5 %collective-permute-start.19 = (bf16[2,192,1024]{2,1,0:T(8,128)(2,1)S(1)}, bf16[2,192,1024]{2,1,0:T(8,128)(2,1)S(1)}, u32[]{:S(2)}, u32[]{:S(2)}) collective-permute-start(bf16[2,192,1024]{2,1,0:T(8,128)(2,1)S(1)} %collective-permute-done.18.refs_3_), channel_id=1, source_target_pairs={{0,4},{1,29},{4,0},{5,9},{8,12},{9,5},{12,8},{13,17},{16,20},{17,1... | collective-permute-start | bytes 2359304 | tf_op jit(solution)/shard_map/ppermute | solution.py:50
  41.4 22.0 %collective-permute-start.2 = (bf16[4,192,768]{2,1,0:T(8,128)(2,1)S(1)}, bf16[4,192,768]{2,1,0:T(8,128)(2,1)S(1)}, u32[]{:S(2)}, u32[]{:S(2)}) collective-permute-start(bf16[4,192,768]{2,1,0:T(8,128)(2,1)S(1)} %pad_maximum_fusion.1.refs_1_), channel_id=1, source_target_pairs={{0,96},{1,33},{4,100},{5,37},{8,104},{9,41},{12,108},{13,45},{16,1... | collective-permute-start | bytes 3538952 | tf_op jit(solution)/shard_map/ppermute | solution.py:50
  45.0 11.7 %collective-permute-start.10 = (bf16[2,192,768]{2,1,0:T(8,128)(2,1)S(1)}, bf16[2,192,768]{2,1,0:T(8,128)(2,1)S(1)}, u32[]{:S(2)}, u32[]{:S(2)}) collective-permute-start(bf16[2,192,768]{2,1,0:T(8,128)(2,1)S(1)} %collective-permute-done.9), channel_id=1, source_target_pairs={{0,128},{1,131},{4,132},{5,135},{8,136},{9,139},{12,140},{13,143},... | collective-permute-start | bytes 1769480 | tf_op jit(solution)/shard_map/ppermute | solution.py:50
  53.9 14.9 %collective-permute-start.15 = (bf16[2,192,1024]{2,1,0:T(8,128)(2,1)S(1)}, bf16[2,192,1024]{2,1,0:T(8,128)(2,1)S(1)}, u32[]{:S(2)}, u32[]{:S(2)}) collective-permute-start(bf16[2,192,1024]{2,1,0:T(8,128)(2,1)S(1)} %collective-permute-done.14.refs_4_), channel_id=1, source_target_pairs={{0,4},{1,29},{4,0},{5,9},{8,12},{9,5},{12,8},{13,17},{16,20},{17,1... | collective-permute-start | bytes 2359304 | tf_op jit(solution)/shard_map/ppermute | solution.py:50
  55.8 18.2 %collective-permute-start.8 = (bf16[4,192,768]{2,1,0:T(8,128)(2,1)S(1)}, bf16[4,192,768]{2,1,0:T(8,128)(2,1)S(1)}, u32[]{:S(2)}, u32[]{:S(2)}) collective-permute-start(bf16[4,192,768]{2,1,0:T(8,128)(2,1)S(1)} %pad_maximum_fusion.2.refs_3_), channel_id=1, source_target_pairs={{0,130},{1,129},{4,134},{5,133},{8,138},{9,137},{12,142},{13,141},... | collective-permute-start | bytes 3538952 | tf_op jit(solution)/shard_map/ppermute | solution.py:50
  56.7 19.3 %collective-permute-start.5 = (bf16[4,192,768]{2,1,0:T(8,128)(2,1)S(1)}, bf16[4,192,768]{2,1,0:T(8,128)(2,1)S(1)}, u32[]{:S(2)}, u32[]{:S(2)}) collective-permute-start(bf16[4,192,768]{2,1,0:T(8,128)(2,1)S(1)} %constant_dynamic-update-slice_fusion.refs_2_), channel_id=1, source_target_pairs={{0,96},{1,33},{4,100},{5,37},{8,104},{9,41},{12,108},{13,45},{16,1... | collective-permute-start | bytes 3538952 | tf_op jit(solution)/shard_map/ppermute | solution.py:50
  59.6 26.3 %collective-permute-start.11 = (bf16[4,192,768]{2,1,0:T(8,128)(2,1)S(1)}, bf16[4,192,768]{2,1,0:T(8,128)(2,1)S(1)}, u32[]{:S(2)}, u32[]{:S(2)}) collective-permute-start(bf16[4,192,768]{2,1,0:T(8,128)(2,1)S(1)} %constant_dynamic-update-slice_fusion.2.refs_4_), channel_id=1, source_target_pairs={{0,130},{1,129},{4,134},{5,133},{8,138},{9,137},{12,142},{13,141},... | collective-permute-start | bytes 3538952 | tf_op jit(solution)/shard_map/ppermute | solution.py:50
  63.3 24.0 %collective-permute-start.20 = (bf16[2,192,1024]{2,1,0:T(8,128)(2,1)S(1)}, bf16[2,192,1024]{2,1,0:T(8,128)(2,1)S(1)}, u32[]{:S(2)}, u32[]{:S(2)}) collective-permute-start(bf16[2,192,1024]{2,1,0:T(8,128)(2,1)S(1)} %collective-permute-done.19.refs_5_), channel_id=1, source_target_pairs={{0,28},{1,5},{4,8},{5,1},{8,4},{9,13},{12,16},{13,9},{16,12},{17,2... | collective-permute-start | bytes 2359304 | tf_op jit(solution)/shard_map/ppermute | solution.py:50
  68.8 19.3 %collective-permute-start.16 = (bf16[2,192,1024]{2,1,0:T(8,128)(2,1)S(1)}, bf16[2,192,1024]{2,1,0:T(8,128)(2,1)S(1)}, u32[]{:S(2)}, u32[]{:S(2)}) collective-permute-start(bf16[2,192,1024]{2,1,0:T(8,128)(2,1)S(1)} %collective-permute-done.15.refs_6_), channel_id=1, source_target_pairs={{0,28},{1,5},{4,8},{5,1},{8,4},{9,13},{12,16},{13,9},{16,12},{17,2... | collective-permute-start | bytes 2359304 | tf_op jit(solution)/shard_map/ppermute | solution.py:50
  91.5 3.8 %collective-permute-start.24 = (f32[384,512]{1,0:T(8,128)S(1)}, f32[384,512]{1,0:T(8,128)S(1)}, u32[]{:S(2)}, u32[]{:S(2)}) collective-permute-start(f32[384,512]{1,0:T(8,128)S(1)} %get-tuple-element.39), channel_id=1, source_target_pairs={{0,1},{1,0},{4,5},{5,4},{8,9},{9,8},{12,13},{13,12},{16,17},{17,16... | collective-permute-start | bytes 2359304 | tf_op jit(solution)/shard_map/ppermute | solution.py:50
  91.6 3.7 %collective-permute-start.25 = (f32[384,512]{1,0:T(8,128)S(1)}, f32[384,512]{1,0:T(8,128)S(1)}, u32[]{:S(2)}, u32[]{:S(2)}) collective-permute-start(f32[384,512]{1,0:T(8,128)S(1)} %get-tuple-element.40), channel_id=1, source_target_pairs={{0,1},{1,0},{4,5},{5,4},{8,9},{9,8},{12,13},{13,12},{16,17},{17,16... | collective-permute-start | bytes 2359304 | tf_op jit(solution)/shard_map/ppermute | solution.py:50
  94.7 4.7 %collective-permute-start.21 = (f32[384,512]{1,0:T(8,128)S(1)}, f32[384,512]{1,0:T(8,128)S(1)}, u32[]{:S(2)}, u32[]{:S(2)}) collective-permute-start(f32[384,512]{1,0:T(8,128)S(1)} %get-tuple-element.35), channel_id=1, source_target_pairs={{0,1},{1,0},{4,5},{5,4},{8,9},{9,8},{12,13},{13,12},{16,17},{17,16... | collective-permute-start | bytes 2359304 | tf_op jit(solution)/shard_map/ppermute | solution.py:50
  94.9 4.5 %collective-permute-start.22 = (f32[384,512]{1,0:T(8,128)S(1)}, f32[384,512]{1,0:T(8,128)S(1)}, u32[]{:S(2)}, u32[]{:S(2)}) collective-permute-start(f32[384,512]{1,0:T(8,128)S(1)} %get-tuple-element.36), channel_id=1, source_target_pairs={{0,1},{1,0},{4,5},{5,4},{8,9},{9,8},{12,13},{13,12},{16,17},{17,16... | collective-permute-start | bytes 2359304 | tf_op jit(solution)/shard_map/ppermute | solution.py:50
  97.9 13.8 %collective-permute-start.26 = (bf16[384,512]{1,0:T(8,128)(2,1)S(1)}, bf16[384,512]{1,0:T(8,128)(2,1)S(1)}, u32[]{:S(2)}, u32[]{:S(2)}) collective-permute-start(bf16[384,512]{1,0:T(8,128)(2,1)S(1)} %get-tuple-element.42), channel_id=1, source_target_pairs={{0,2},{1,3},{4,6},{5,7},{8,10},{9,11},{12,14},{13,15},{16,18},{17,... | collective-permute-start | bytes 1179656 | tf_op jit(solution)/shard_map/ppermute | solution.py:50
  102.0 17.2 %collective-permute-start.23 = (bf16[384,512]{1,0:T(8,128)(2,1)S(1)}, bf16[384,512]{1,0:T(8,128)(2,1)S(1)}, u32[]{:S(2)}, u32[]{:S(2)}) collective-permute-start(bf16[384,512]{1,0:T(8,128)(2,1)S(1)} %get-tuple-element.38), channel_id=1, source_target_pairs={{0,2},{1,3},{4,6},{5,7},{8,10},{9,11},{12,14},{13,15},{16,18},{17,... | collective-permute-start | bytes 1179656 | tf_op jit(solution)/shard_map/ppermute | solution.py:50

commit v5 on v4

--- a/solution.py
+++ b/solution.py
@@ -227,17 +227,22 @@
 
 def multiply_kernel(cols, int_ref, amp_ref, *refs):
     rows = int_ref.shape[0] // 2
-    other_refs, outs = refs[:-2], refs[-2:]
     for side in range(2):
-        total = jnp.dot(int_ref[pl.ds(side * rows, rows), :], amp_ref[:, cols], preferred_element_type=jnp.float32)
-        if other_refs:
-            total = (total + other_refs[side][...]).astype(jnp.bfloat16)
-        outs[side][...] = total
+        src = pl.ds(side * rows, rows)
+        total = jnp.dot(int_ref[src, :], amp_ref[:, cols], preferred_element_type=jnp.float32)
+        if len(refs) == 3:
+            refs[1 + side][...] = (total + refs[0][src, :]).astype(jnp.bfloat16)
+        else:
+            refs[0][src, :] = total
 
 
 def multiply(r, ints, amps, *other):
     rows, depth, width = ints.shape[0] // 2, ints.shape[1], amps.shape[1] // RCHUNKS
     vmem_spec = pl.BlockSpec(memory_space=VMEM)
+    if other:
+        shapes = [jax.ShapeDtypeStruct((rows, width), jnp.bfloat16)] * 2
+    else:
+        shapes = [jax.ShapeDtypeStruct((2 * rows, width), jnp.float32)]
 
     def kernel(*refs):
         multiply_kernel(slice(r * width, (r + 1) * width), *refs)
@@ -245,8 +250,8 @@
     return pl.pallas_call(
         kernel,
         in_specs=[vmem_spec] * (2 + len(other)),
-        out_specs=[vmem_spec] * 2,
-        out_shape=[jax.ShapeDtypeStruct((rows, width), jnp.bfloat16 if other else jnp.float32)] * 2,
+        out_specs=[vmem_spec] * len(shapes),
+        out_shape=shapes,
         cost_estimate=pl.CostEstimate(
             flops=4 * rows * depth * width, bytes_accessed=(2 * rows + width) * depth * 2 + 8 * rows * width, transcendentals=0
         ),
@@ -271,8 +276,8 @@
 
     kept, received = [], []
     for r in range(RCHUNKS):
-        partials = [send(partial, CORE) for partial in multiply(r, other_ints, amps)]
-        theirs, mine = multiply(r, own_ints, amps, *partials)
+        (partial,) = multiply(r, other_ints, amps)
+        theirs, mine = multiply(r, own_ints, amps, send(partial, CORE))
         kept.append(mine)
         received.append(send(theirs, X_ACROSS))
     low = [jnp.where(x_hi == 0, k, g) for k, g in zip(kept, received)]

time: 123 us -> 122 us (level)
    ppermute x27 -> x25, starting transfers between devices: 41.6 us -> 40.8 us  [send(): return lax.ppermute(array, AXES, plan)]
    ppermute x27 -> x25, waiting for transfers between devices: 55.7 us -> 55.9 us  [send(): return lax.ppermute(array, AXES, plan)]
  transfers between devices with their start and end apart: 27 -> 25, of which waited for: 11 -> 12; matrix products, arithmetic and copies ran while one was open for 1% -> 1% of each run, Pallas kernels for 11% -> 11%
where the time goes in v5:
time: 122 us; the launch traced here: 120 us
  waiting for transfers between devices  55.9 us (46%)
  starting transfers between devices  40.8 us (33%)
  Pallas kernels  18.1 us (15%)
  local copies, waits for them, and re-layouts  3.18 us (3%)
  other arithmetic  1.95 us (2%)
    ppermute x25, waiting for transfers between devices, send(): return lax.ppermute(array, AXES, plan)  55.9 us
    ppermute x25, starting transfers between devices, send(): return lax.ppermute(array, AXES, plan)  40.8 us
    pallas_call x4, Pallas kernels, multiply(): pl.pallas_call(kernel, in_specs=[vmem_spec] * (2 + len(other)), out_specs...  10.4 us
    pallas_call x3, Pallas kernels, order_amplitudes(): pl.pallas_call(kernel, in_specs=[pl.BlockSpec(memory_space=SMEM)] + [any_...  3.33 us
    unnamed x10, local copies, waits for them, and re-layouts  3.02 us
    pallas_call x2, Pallas kernels, order_integrals(): pl.pallas_call(kernel, in_specs=[pl.BlockSpec(memory_space=SMEM)] + [any_...  2.96 us
  transfers between devices with their start and end apart: 25, of which 12 were waited for; matrix products, arithmetic and copies ran while one was open for 1% of the time, Pallas kernels for 11%

profile of v5, /device:TPU:24, one launch (start us, length us, event | category | flops | bytes accessed | tf_op | source)
XLA Modules:
  0.0 120.2 jit_solution(9063183150887727104)
XLA Ops:
  0.1 1.1 copy-done
  1.2 0.7 copy-done.3
  1.9 0.6 mask_amplitudes.1
  2.5 0.5 copy-done.1
  2.9 0.7 copy-done.2
  3.6 0.8 mask_integrals.1
  4.5 1.6 %collective-permute-start = (bf16[192,768]{1,0:T(8,128)(2,1)S(1)}, bf16[192,768]{1,0:T(8,128)(2,1)S(1)}, u32[]{:S(2)}, u32[]{:S(2)}) collective-permute-start(bf16[192,768]{1,0:T(8,128)(2,1)S(1)} %get-tuple-element.23), channel_id=1, source_target_pairs={{0,128},{1,131},{4,132},{5,135},{8,136},{9,139},{12,140},{13,143},... | collective-permute-start | bytes 884744 | tf_op jit(solution)/shard_map/ppermute | solution.py:50
  6.0 1.9 %collective-permute-start.17 = (bf16[192,1024]{1,0:T(8,128)(2,1)S(1)}, bf16[192,1024]{1,0:T(8,128)(2,1)S(1)}, u32[]{:S(2)}, u32[]{:S(2)}) collective-permute-start(bf16[192,1024]{1,0:T(8,128)(2,1)S(1)} %get-tuple-element.29), channel_id=1, source_target_pairs={{0,4},{1,29},{4,0},{5,9},{8,12},{9,5},{12,8},{13,17},{16,20},{17,1... | collective-permute-start | bytes 1179656 | tf_op jit(solution)/shard_map/ppermute | solution.py:50
  7.9 2.7 %collective-permute-start.12 = (bf16[192,1024]{1,0:T(8,128)(2,1)S(1)}, bf16[192,1024]{1,0:T(8,128)(2,1)S(1)}, u32[]{:S(2)}, u32[]{:S(2)}) collective-permute-start(bf16[192,1024]{1,0:T(8,128)(2,1)S(1)} %get-tuple-element.28), channel_id=1, source_target_pairs={{0,2},{1,3},{4,6},{5,7},{8,10},{9,11},{12,14},{13,15},{16,18},{17,... | collective-permute-start | bytes 1179656 | tf_op jit(solution)/shard_map/ppermute | solution.py:50
  10.7 0.7 collective-permute-start.6
  11.5 1.4 %collective-permute-start.1 = (bf16[2,192,768]{2,1,0:T(8,128)(2,1)S(1)}, bf16[2,192,768]{2,1,0:T(8,128)(2,1)S(1)}, u32[]{:S(2)}, u32[]{:S(2)}) collective-permute-start(bf16[2,192,768]{2,1,0:T(8,128)(2,1)S(1)} %pad_maximum_fusion.5), channel_id=1, source_target_pairs={{0,32},{1,97},{4,36},{5,101},{8,40},{9,105},{12,44},{13,109},{16,4... | collective-permute-start | bytes 1769480 | tf_op jit(solution)/shard_map/ppermute | solution.py:50
  12.9 1.0 collective-permute-done.17
  13.9 6.8 %collective-permute-start.18 = (bf16[2,192,1024]{2,1,0:T(8,128)(2,1)S(1)}, bf16[2,192,1024]{2,1,0:T(8,128)(2,1)S(1)}, u32[]{:S(2)}, u32[]{:S(2)}) collective-permute-start(bf16[2,192,1024]{2,1,0:T(8,128)(2,1)S(1)} %pad_maximum_fusion.4.refs_1_), channel_id=1, source_target_pairs={{0,28},{1,5},{4,8},{5,1},{8,4},{9,13},{12,16},{13,9},{16,12},{17,2... | collective-permute-start | bytes 2359304 | tf_op jit(solution)/shard_map/ppermute | solution.py:50
  20.7 3.1 %collective-permute-start.13 = (bf16[192,1024]{1,0:T(8,128)(2,1)S(1)}, bf16[192,1024]{1,0:T(8,128)(2,1)S(1)}, u32[]{:S(2)}, u32[]{:S(2)}) collective-permute-start(bf16[192,1024]{1,0:T(8,128)(2,1)S(1)} %collective-permute-done.12), channel_id=1, source_target_pairs={{0,4},{1,29},{4,0},{5,9},{8,12},{9,5},{12,8},{13,17},{16,20},{17,1... | collective-permute-start | bytes 1179656 | tf_op jit(solution)/shard_map/ppermute | solution.py:50
  23.8 0.6 collective-permute-start.3
  24.5 0.2 collective-permute-start.7
  24.7 8.6 %collective-permute-done.13 = bf16[192,1024]{1,0:T(8,128)(2,1)S(1)} collective-permute-done((bf16[192,1024]{1,0:T(8,128)(2,1)S(1)}, bf16[192,1024]{1,0:T(8,128)(2,1)S(1)}, u32[]{:S(2)}, u32[]{:S(2)}) %collective-permute-start.13) | collective-permute-done | bytes 393248 | tf_op jit(solution)/shard_map/ppermute | solution.py:50
  33.3 0.2 collective-permute-start.9
  33.6 4.0 %collective-permute-start.14 = (bf16[2,192,1024]{2,1,0:T(8,128)(2,1)S(1)}, bf16[2,192,1024]{2,1,0:T(8,128)(2,1)S(1)}, u32[]{:S(2)}, u32[]{:S(2)}) collective-permute-start(bf16[2,192,1024]{2,1,0:T(8,128)(2,1)S(1)} %pad_maximum_fusion.3.refs_2_), channel_id=1, source_target_pairs={{0,28},{1,5},{4,8},{5,1},{8,4},{9,13},{12,16},{13,9},{16,12},{17,2... | collective-permute-start | bytes 2359304 | tf_op jit(solution)/shard_map/ppermute | solution.py:50
  37.6 1.9 %collective-permute-done.3 = bf16[2,192,768]{2,1,0:T(8,128)(2,1)S(1)} collective-permute-done((bf16[2,192,768]{2,1,0:T(8,128)(2,1)S(1)}, bf16[2,192,768]{2,1,0:T(8,128)(2,1)S(1)}, u32[]{:S(2)}, u32[]{:S(2)}) %collective-permute-start.3) | collective-permute-done | bytes 589856 | tf_op jit(solution)/shard_map/ppermute | solution.py:50
  39.5 0.6 collective-permute-start.4
  40.1 1.1 collective-permute-start.19
  41.6 3.4 %collective-permute-done.9 = bf16[2,192,768]{2,1,0:T(8,128)(2,1)S(1)} collective-permute-done((bf16[2,192,768]{2,1,0:T(8,128)(2,1)S(1)}, bf16[2,192,768]{2,1,0:T(8,128)(2,1)S(1)}, u32[]{:S(2)}, u32[]{:S(2)}) %collective-permute-start.9) | collective-permute-done | bytes 589856 | tf_op jit(solution)/shard_map/ppermute | solution.py:50
  45.1 8.8 %collective-permute-done.14.refs_4_ = bf16[2,192,1024]{2,1,0:T(8,128)(2,1)S(1)} collective-permute-done((bf16[2,192,1024]{2,1,0:T(8,128)(2,1)S(1)}, bf16[2,192,1024]{2,1,0:T(8,128)(2,1)S(1)}, u32[]{:S(2)}, u32[]{:S(2)}) %collective-permute-start.14) | collective-permute-done | bytes 786464 | tf_op jit(solution)/shard_map/ppermute | solution.py:50
  54.0 1.8 %collective-permute-done.4 = bf16[2,192,768]{2,1,0:T(8,128)(2,1)S(1)} collective-permute-done((bf16[2,192,768]{2,1,0:T(8,128)(2,1)S(1)}, bf16[2,192,768]{2,1,0:T(8,128)(2,1)S(1)}, u32[]{:S(2)}, u32[]{:S(2)}) %collective-permute-start.4) | collective-permute-done | bytes 589856 | tf_op jit(solution)/shard_map/ppermute | solution.py:50
  55.8 0.8 collective-permute-start.8
  56.7 2.9 %collective-permute-start.5 = (bf16[4,192,768]{2,1,0:T(8,128)(2,1)S(1)}, bf16[4,192,768]{2,1,0:T(8,128)(2,1)S(1)}, u32[]{:S(2)}, u32[]{:S(2)}) collective-permute-start(bf16[4,192,768]{2,1,0:T(8,128)(2,1)S(1)} %constant_dynamic-update-slice_fusion.refs_2_), channel_id=1, source_target_pairs={{0,96},{1,33},{4,100},{5,37},{8,104},{9,41},{12,108},{13,45},{16,1... | collective-permute-start | bytes 3538952 | tf_op jit(solution)/shard_map/ppermute | solution.py:50
  59.7 3.6 %collective-permute-done.2.refs_1_ = bf16[4,192,768]{2,1,0:T(8,128)(2,1)S(1)} collective-permute-done((bf16[4,192,768]{2,1,0:T(8,128)(2,1)S(1)}, bf16[4,192,768]{2,1,0:T(8,128)(2,1)S(1)}, u32[]{:S(2)}, u32[]{:S(2)}) %collective-permute-start.2) | collective-permute-done | bytes 1179680 | tf_op jit(solution)/shard_map/ppermute | solution.py:50
  63.3 5.5 %collective-permute-start.20 = (bf16[2,192,1024]{2,1,0:T(8,128)(2,1)S(1)}, bf16[2,192,1024]{2,1,0:T(8,128)(2,1)S(1)}, u32[]{:S(2)}, u32[]{:S(2)}) collective-permute-start(bf16[2,192,1024]{2,1,0:T(8,128)(2,1)S(1)} %collective-permute-done.19.refs_5_), channel_id=1, source_target_pairs={{0,28},{1,5},{4,8},{5,1},{8,4},{9,13},{12,16},{13,9},{16,12},{17,2... | collective-permute-start | bytes 2359304 | tf_op jit(solution)/shard_map/ppermute | solution.py:50
  68.8 2.0 %collective-permute-start.16 = (bf16[2,192,1024]{2,1,0:T(8,128)(2,1)S(1)}, bf16[2,192,1024]{2,1,0:T(8,128)(2,1)S(1)}, u32[]{:S(2)}, u32[]{:S(2)}) collective-permute-start(bf16[2,192,1024]{2,1,0:T(8,128)(2,1)S(1)} %collective-permute-done.15.refs_6_), channel_id=1, source_target_pairs={{0,28},{1,5},{4,8},{5,1},{8,4},{9,13},{12,16},{13,9},{16,12},{17,2... | collective-permute-start | bytes 2359304 | tf_op jit(solution)/shard_map/ppermute | solution.py:50
  70.8 1.5 %order_integrals.2 = (bf16[768,3072]{1,0:T(8,128)(2,1)S(1)}, bf16[768,3072]{1,0:T(8,128)(2,1)S(1)}) custom-call(s32[6]{0:T(128)S(1)} %stack.63.place.refs_0_, bf16[4,192,768]{2,1,0:T(8,128)(2,1)S(1)} %pad_maximum_fusion.1.refs_1_, bf16[4,192,768]{2,1,0:T(8,128)(2,1)S(1)} %constant_dynamic-update-slice_fusion.refs_2_, ...), custom_call_target="tpu_custom_call" | custom-call | bytes 9437184 | tf_op jit(solution)/shard_map/order_integrals/pallas_call | solution.py:214
  72.2 1.8 %order_amplitudes.3.refs_2_ = bf16[3072,1024]{1,0:T(8,128)(2,1)S(1)} custom-call(s32[6]{0:T(128)S(1)} %stack.63.place.refs_0_, bf16[2,192,1024]{2,1,0:T(8,128)(2,1)S(1)} %pad_maximum_fusion.4.refs_1_, bf16[2,192,1024]{2,1,0:T(8,128)(2,1)S(1)} %pad_maximum_fusion.3.refs_2_, bf16[2,192,1024]{2,1,0:T(8,128)(2,1)S(1)} %collective-permute-done.18.refs_3_, ...), custom_call_target="tpu_custom_call" | custom-call | bytes 9437184 | tf_op jit(solution)/shard_map/order_amplitudes/pallas_call | solution.py:159
  74.1 1.9 %collective-permute-done.5.refs_2_ = bf16[4,192,768]{2,1,0:T(8,128)(2,1)S(1)} collective-permute-done((bf16[4,192,768]{2,1,0:T(8,128)(2,1)S(1)}, bf16[4,192,768]{2,1,0:T(8,128)(2,1)S(1)}, u32[]{:S(2)}, u32[]{:S(2)}) %collective-permute-start.5) | collective-permute-done | bytes 1179680 | tf_op jit(solution)/shard_map/ppermute | solution.py:50
  76.0 9.9 %collective-permute-done.11.refs_4_ = bf16[4,192,768]{2,1,0:T(8,128)(2,1)S(1)} collective-permute-done((bf16[4,192,768]{2,1,0:T(8,128)(2,1)S(1)}, bf16[4,192,768]{2,1,0:T(8,128)(2,1)S(1)}, u32[]{:S(2)}, u32[]{:S(2)}) %collective-permute-start.11) | collective-permute-done | bytes 1179680 | tf_op jit(solution)/shard_map/ppermute | solution.py:50
  85.9 1.5 %order_integrals.3 = (bf16[768,3072]{1,0:T(8,128)(2,1)S(1)}, bf16[768,3072]{1,0:T(8,128)(2,1)S(1)}) custom-call(s32[6]{0:T(128)S(1)} %stack.63.place.refs_0_, bf16[4,192,768]{2,1,0:T(8,128)(2,1)S(1)} %collective-permute-done.2.refs_1_, bf16[4,192,768]{2,1,0:T(8,128)(2,1)S(1)} %collective-permute-done.5.refs_2_, ...), custom_call_target="tpu_custom_call", output_to_operand_aliasing={{0}: (5, {}), {1}: (6, {})} | custom-call | bytes 9437184 | tf_op jit(solution)/shard_map/order_integrals/pallas_call | solution.py:214
  87.4 0.8 order_amplitudes.4.refs_2_
  88.1 0.8 order_amplitudes.5.refs_1_
  88.9 2.6 %multiply_other.3 = f32[768,512]{1,0:T(8,128)S(1)} custom-call(bf16[768,3072]{1,0:T(8,128)(2,1)S(1)} %get-tuple-element.30.refs_0_, bf16[3072,1024]{1,0:T(8,128)(2,1)S(1)} %order_amplitudes.5.refs_1_), custom_call_target="tpu_custom_call" | custom-call | flops 2415919104 | bytes 9437184 | tf_op jit(solution)/shard_map/multiply_other/pallas_call | solution.py:250
  91.6 2.6 %multiply_other.2 = f32[768,512]{1,0:T(8,128)S(1)} custom-call(bf16[768,3072]{1,0:T(8,128)(2,1)S(1)} %get-tuple-element.30.refs_0_, bf16[3072,1024]{1,0:T(8,128)(2,1)S(1)} %order_amplitudes.5.refs_1_), custom_call_target="tpu_custom_call" | custom-call | flops 2415919104 | bytes 9437184 | tf_op jit(solution)/shard_map/multiply_other/pallas_call | solution.py:250
  94.2 0.6 collective-permute-start.21
  94.8 0.2 collective-permute-done.23.refs_2_
  95.0 2.6 %multiply_own.3 = (bf16[384,512]{1,0:T(8,128)(2,1)S(1)}, bf16[384,512]{1,0:T(8,128)(2,1)S(1)}) custom-call(bf16[768,3072]{1,0:T(8,128)(2,1)S(1)} %get-tuple-element.27.refs_0_, bf16[3072,1024]{1,0:T(8,128)(2,1)S(1)} %order_amplitudes.5.refs_1_, f32[768,512]{1,0:T(8,128)S(1)} %collective-permute-done.23.refs_2_), custom_call_target="tpu_custom_call" | custom-call | flops 2415919104 | bytes 9437184 | tf_op jit(solution)/shard_map/multiply_own/pallas_call | solution.py:250
  97.6 1.3 %collective-permute-start.24 = (bf16[384,512]{1,0:T(8,128)(2,1)S(1)}, bf16[384,512]{1,0:T(8,128)(2,1)S(1)}, u32[]{:S(2)}, u32[]{:S(2)}) collective-permute-start(bf16[384,512]{1,0:T(8,128)(2,1)S(1)} %get-tuple-element.34), channel_id=1, source_target_pairs={{0,2},{1,3},{4,6},{5,7},{8,10},{9,11},{12,14},{13,15},{16,18},{17,... | collective-permute-start | bytes 1179656 | tf_op jit(solution)/shard_map/ppermute | solution.py:50
  98.9 2.6 %multiply_own.2 = (bf16[384,512]{1,0:T(8,128)(2,1)S(1)}, bf16[384,512]{1,0:T(8,128)(2,1)S(1)}) custom-call(bf16[768,3072]{1,0:T(8,128)(2,1)S(1)} %get-tuple-element.27.refs_0_, bf16[3072,1024]{1,0:T(8,128)(2,1)S(1)} %order_amplitudes.5.refs_1_, f32[768,512]{1,0:T(8,128)S(1)} %collective-permute-done.21.refs_2_), custom_call_target="tpu_custom_call" | custom-call | flops 2415919104 | bytes 9437184 | tf_op jit(solution)/shard_map/multiply_own/pallas_call | solution.py:250
  101.6 2.4 %collective-permute-start.22 = (bf16[384,512]{1,0:T(8,128)(2,1)S(1)}, bf16[384,512]{1,0:T(8,128)(2,1)S(1)}, u32[]{:S(2)}, u32[]{:S(2)}) collective-permute-start(bf16[384,512]{1,0:T(8,128)(2,1)S(1)} %get-tuple-element.32), channel_id=1, source_target_pairs={{0,2},{1,3},{4,6},{5,7},{8,10},{9,11},{12,14},{13,15},{16,18},{17,... | collective-permute-start | bytes 1179656 | tf_op jit(solution)/shard_map/ppermute | solution.py:50
  103.9 7.2 %collective-permute-done.24 = bf16[384,512]{1,0:T(8,128)(2,1)S(1)} collective-permute-done((bf16[384,512]{1,0:T(8,128)(2,1)S(1)}, bf16[384,512]{1,0:T(8,128)(2,1)S(1)}, u32[]{:S(2)}, u32[]{:S(2)}) %collective-permute-start.24) | collective-permute-done | bytes 393248 | tf_op jit(solution)/shard_map/ppermute | solution.py:50
  111.2 7.6 %collective-permute-done.22 = bf16[384,512]{1,0:T(8,128)(2,1)S(1)} collective-permute-done((bf16[384,512]{1,0:T(8,128)(2,1)S(1)}, bf16[384,512]{1,0:T(8,128)(2,1)S(1)}, u32[]{:S(2)}, u32[]{:S(2)}) %collective-permute-start.22) | collective-permute-done | bytes 393248 | tf_op jit(solution)/shard_map/ppermute | solution.py:50
  118.8 1.3 %pad_maximum_fusion = bf16[384,2048]{1,0:T(8,128)(2,1)} fusion(bf16[384,512]{1,0:T(8,128)(2,1)S(1)} %get-tuple-element.38, bf16[384,512]{1,0:T(8,128)(2,1)S(1)} %get-tuple-element.36, bf16[384,512]{1,0:T(8,128)(2,1)S(1)} %get-tuple-element.37, bf16[384,512]{1,0:T(8,128)(2,1)S(1)} %get-tuple-element.35), kind=kLoop, calls=%fused_computation | loop fusion | flops 6291456 | bytes 3145728 | tf_op jit(solution)/shard_map/concatenate | solution.py:285
  (35 shorter events, 1.3 us)
Async XLA Ops:
  0.1 1.1 copy-start
  1.2 0.7 copy-start.3
  1.9 1.1 copy-start.1
  2.9 0.7 copy-start.2
  4.5 7.0 %collective-permute-start = (bf16[192,768]{1,0:T(8,128)(2,1)S(1)}, bf16[192,768]{1,0:T(8,128)(2,1)S(1)}, u32[]{:S(2)}, u32[]{:S(2)}) collective-permute-start(bf16[192,768]{1,0:T(8,128)(2,1)S(1)} %get-tuple-element.23), channel_id=1, source_target_pairs={{0,128},{1,131},{4,132},{5,135},{8,136},{9,139},{12,140},{13,143},... | collective-permute-start | bytes 884744 | tf_op jit(solution)/shard_map/ppermute | solution.py:50
  6.0 7.8 %collective-permute-start.17 = (bf16[192,1024]{1,0:T(8,128)(2,1)S(1)}, bf16[192,1024]{1,0:T(8,128)(2,1)S(1)}, u32[]{:S(2)}, u32[]{:S(2)}) collective-permute-start(bf16[192,1024]{1,0:T(8,128)(2,1)S(1)} %get-tuple-element.29), channel_id=1, source_target_pairs={{0,4},{1,29},{4,0},{5,9},{8,12},{9,5},{12,8},{13,17},{16,20},{17,1... | collective-permute-start | bytes 1179656 | tf_op jit(solution)/shard_map/ppermute | solution.py:50
  7.9 12.8 %collective-permute-start.12 = (bf16[192,1024]{1,0:T(8,128)(2,1)S(1)}, bf16[192,1024]{1,0:T(8,128)(2,1)S(1)}, u32[]{:S(2)}, u32[]{:S(2)}) collective-permute-start(bf16[192,1024]{1,0:T(8,128)(2,1)S(1)} %get-tuple-element.28), channel_id=1, source_target_pairs={{0,2},{1,3},{4,6},{5,7},{8,10},{9,11},{12,14},{13,15},{16,18},{17,... | collective-permute-start | bytes 1179656 | tf_op jit(solution)/shard_map/ppermute | solution.py:50
  10.7 13.7 %collective-permute-start.6 = (bf16[192,768]{1,0:T(8,128)(2,1)S(1)}, bf16[192,768]{1,0:T(8,128)(2,1)S(1)}, u32[]{:S(2)}, u32[]{:S(2)}) collective-permute-start(bf16[192,768]{1,0:T(8,128)(2,1)S(1)} %get-tuple-element.24), channel_id=1, source_target_pairs={{0,32},{1,97},{4,36},{5,101},{8,40},{9,105},{12,44},{13,109},{16,4... | collective-permute-start | bytes 884744 | tf_op jit(solution)/shard_map/ppermute | solution.py:50
  11.5 22.1 %collective-permute-start.1 = (bf16[2,192,768]{2,1,0:T(8,128)(2,1)S(1)}, bf16[2,192,768]{2,1,0:T(8,128)(2,1)S(1)}, u32[]{:S(2)}, u32[]{:S(2)}) collective-permute-start(bf16[2,192,768]{2,1,0:T(8,128)(2,1)S(1)} %pad_maximum_fusion.5), channel_id=1, source_target_pairs={{0,32},{1,97},{4,36},{5,101},{8,40},{9,105},{12,44},{13,109},{16,4... | collective-permute-start | bytes 1769480 | tf_op jit(solution)/shard_map/ppermute | solution.py:50
  13.9 26.3 %collective-permute-start.18 = (bf16[2,192,1024]{2,1,0:T(8,128)(2,1)S(1)}, bf16[2,192,1024]{2,1,0:T(8,128)(2,1)S(1)}, u32[]{:S(2)}, u32[]{:S(2)}) collective-permute-start(bf16[2,192,1024]{2,1,0:T(8,128)(2,1)S(1)} %pad_maximum_fusion.4.refs_1_), channel_id=1, source_target_pairs={{0,28},{1,5},{4,8},{5,1},{8,4},{9,13},{12,16},{13,9},{16,12},{17,2... | collective-permute-start | bytes 2359304 | tf_op jit(solution)/shard_map/ppermute | solution.py:50
  20.7 12.6 %collective-permute-start.13 = (bf16[192,1024]{1,0:T(8,128)(2,1)S(1)}, bf16[192,1024]{1,0:T(8,128)(2,1)S(1)}, u32[]{:S(2)}, u32[]{:S(2)}) collective-permute-start(bf16[192,1024]{1,0:T(8,128)(2,1)S(1)} %collective-permute-done.12), channel_id=1, source_target_pairs={{0,4},{1,29},{4,0},{5,9},{8,12},{9,5},{12,8},{13,17},{16,20},{17,1... | collective-permute-start | bytes 1179656 | tf_op jit(solution)/shard_map/ppermute | solution.py:50
  23.8 15.7 %collective-permute-start.3 = (bf16[2,192,768]{2,1,0:T(8,128)(2,1)S(1)}, bf16[2,192,768]{2,1,0:T(8,128)(2,1)S(1)}, u32[]{:S(2)}, u32[]{:S(2)}) collective-permute-start(bf16[2,192,768]{2,1,0:T(8,128)(2,1)S(1)} %pad_maximum_fusion.5), channel_id=1, source_target_pairs={{0,130},{1,129},{4,134},{5,133},{8,138},{9,137},{12,142},{13,141},... | collective-permute-start | bytes 1769480 | tf_op jit(solution)/shard_map/ppermute | solution.py:50
  24.5 16.9 %collective-permute-start.7 = (bf16[2,192,768]{2,1,0:T(8,128)(2,1)S(1)}, bf16[2,192,768]{2,1,0:T(8,128)(2,1)S(1)}, u32[]{:S(2)}, u32[]{:S(2)}) collective-permute-start(bf16[2,192,768]{2,1,0:T(8,128)(2,1)S(1)} %pad_maximum_fusion.6), channel_id=1, source_target_pairs={{0,128},{1,131},{4,132},{5,135},{8,136},{9,139},{12,140},{13,143},... | collective-permute-start | bytes 1769480 | tf_op jit(solution)/shard_map/ppermute | solution.py:50
  33.3 11.7 %collective-permute-start.9 = (bf16[2,192,768]{2,1,0:T(8,128)(2,1)S(1)}, bf16[2,192,768]{2,1,0:T(8,128)(2,1)S(1)}, u32[]{:S(2)}, u32[]{:S(2)}) collective-permute-start(bf16[2,192,768]{2,1,0:T(8,128)(2,1)S(1)} %pad_maximum_fusion.6), channel_id=1, source_target_pairs={{0,96},{1,33},{4,100},{5,37},{8,104},{9,41},{12,108},{13,45},{16,1... | collective-permute-start | bytes 1769480 | tf_op jit(solution)/shard_map/ppermute | solution.py:50
  33.6 20.3 %collective-permute-start.14 = (bf16[2,192,1024]{2,1,0:T(8,128)(2,1)S(1)}, bf16[2,192,1024]{2,1,0:T(8,128)(2,1)S(1)}, u32[]{:S(2)}, u32[]{:S(2)}) collective-permute-start(bf16[2,192,1024]{2,1,0:T(8,128)(2,1)S(1)} %pad_maximum_fusion.3.refs_2_), channel_id=1, source_target_pairs={{0,28},{1,5},{4,8},{5,1},{8,4},{9,13},{12,16},{13,9},{16,12},{17,2... | collective-permute-start | bytes 2359304 | tf_op jit(solution)/shard_map/ppermute | solution.py:50
  39.5 16.3 %collective-permute-start.4 = (bf16[2,192,768]{2,1,0:T(8,128)(2,1)S(1)}, bf16[2,192,768]{2,1,0:T(8,128)(2,1)S(1)}, u32[]{:S(2)}, u32[]{:S(2)}) collective-permute-start(bf16[2,192,768]{2,1,0:T(8,128)(2,1)S(1)} %collective-permute-done.3), channel_id=1, source_target_pairs={{0,32},{1,97},{4,36},{5,101},{8,40},{9,105},{12,44},{13,109},{16,4... | collective-permute-start | bytes 1769480 | tf_op jit(solution)/shard_map/ppermute | solution.py:50
  40.1 19.5 %collective-permute-start.19 = (bf16[2,192,1024]{2,1,0:T(8,128)(2,1)S(1)}, bf16[2,192,1024]{2,1,0:T(8,128)(2,1)S(1)}, u32[]{:S(2)}, u32[]{:S(2)}) collective-permute-start(bf16[2,192,1024]{2,1,0:T(8,128)(2,1)S(1)} %collective-permute-done.18.refs_3_), channel_id=1, source_target_pairs={{0,4},{1,29},{4,0},{5,9},{8,12},{9,5},{12,8},{13,17},{16,20},{17,1... | collective-permute-start | bytes 2359304 | tf_op jit(solution)/shard_map/ppermute | solution.py:50
  41.4 22.0 %collective-permute-start.2 = (bf16[4,192,768]{2,1,0:T(8,128)(2,1)S(1)}, bf16[4,192,768]{2,1,0:T(8,128)(2,1)S(1)}, u32[]{:S(2)}, u32[]{:S(2)}) collective-permute-start(bf16[4,192,768]{2,1,0:T(8,128)(2,1)S(1)} %pad_maximum_fusion.1.refs_1_), channel_id=1, source_target_pairs={{0,96},{1,33},{4,100},{5,37},{8,104},{9,41},{12,108},{13,45},{16,1... | collective-permute-start | bytes 3538952 | tf_op jit(solution)/shard_map/ppermute | solution.py:50
  45.0 11.7 %collective-permute-start.10 = (bf16[2,192,768]{2,1,0:T(8,128)(2,1)S(1)}, bf16[2,192,768]{2,1,0:T(8,128)(2,1)S(1)}, u32[]{:S(2)}, u32[]{:S(2)}) collective-permute-start(bf16[2,192,768]{2,1,0:T(8,128)(2,1)S(1)} %collective-permute-done.9), channel_id=1, source_target_pairs={{0,128},{1,131},{4,132},{5,135},{8,136},{9,139},{12,140},{13,143},... | collective-permute-start | bytes 1769480 | tf_op jit(solution)/shard_map/ppermute | solution.py:50
  53.9 14.9 %collective-permute-start.15 = (bf16[2,192,1024]{2,1,0:T(8,128)(2,1)S(1)}, bf16[2,192,1024]{2,1,0:T(8,128)(2,1)S(1)}, u32[]{:S(2)}, u32[]{:S(2)}) collective-permute-start(bf16[2,192,1024]{2,1,0:T(8,128)(2,1)S(1)} %collective-permute-done.14.refs_4_), channel_id=1, source_target_pairs={{0,4},{1,29},{4,0},{5,9},{8,12},{9,5},{12,8},{13,17},{16,20},{17,1... | collective-permute-start | bytes 2359304 | tf_op jit(solution)/shard_map/ppermute | solution.py:50
  55.8 18.2 %collective-permute-start.8 = (bf16[4,192,768]{2,1,0:T(8,128)(2,1)S(1)}, bf16[4,192,768]{2,1,0:T(8,128)(2,1)S(1)}, u32[]{:S(2)}, u32[]{:S(2)}) collective-permute-start(bf16[4,192,768]{2,1,0:T(8,128)(2,1)S(1)} %pad_maximum_fusion.2.refs_3_), channel_id=1, source_target_pairs={{0,130},{1,129},{4,134},{5,133},{8,138},{9,137},{12,142},{13,141},... | collective-permute-start | bytes 3538952 | tf_op jit(solution)/shard_map/ppermute | solution.py:50
  56.7 19.3 %collective-permute-start.5 = (bf16[4,192,768]{2,1,0:T(8,128)(2,1)S(1)}, bf16[4,192,768]{2,1,0:T(8,128)(2,1)S(1)}, u32[]{:S(2)}, u32[]{:S(2)}) collective-permute-start(bf16[4,192,768]{2,1,0:T(8,128)(2,1)S(1)} %constant_dynamic-update-slice_fusion.refs_2_), channel_id=1, source_target_pairs={{0,96},{1,33},{4,100},{5,37},{8,104},{9,41},{12,108},{13,45},{16,1... | collective-permute-start | bytes 3538952 | tf_op jit(solution)/shard_map/ppermute | solution.py:50
  59.6 26.3 %collective-permute-start.11 = (bf16[4,192,768]{2,1,0:T(8,128)(2,1)S(1)}, bf16[4,192,768]{2,1,0:T(8,128)(2,1)S(1)}, u32[]{:S(2)}, u32[]{:S(2)}) collective-permute-start(bf16[4,192,768]{2,1,0:T(8,128)(2,1)S(1)} %constant_dynamic-update-slice_fusion.2.refs_4_), channel_id=1, source_target_pairs={{0,130},{1,129},{4,134},{5,133},{8,138},{9,137},{12,142},{13,141},... | collective-permute-start | bytes 3538952 | tf_op jit(solution)/shard_map/ppermute | solution.py:50
  63.3 24.0 %collective-permute-start.20 = (bf16[2,192,1024]{2,1,0:T(8,128)(2,1)S(1)}, bf16[2,192,1024]{2,1,0:T(8,128)(2,1)S(1)}, u32[]{:S(2)}, u32[]{:S(2)}) collective-permute-start(bf16[2,192,1024]{2,1,0:T(8,128)(2,1)S(1)} %collective-permute-done.19.refs_5_), channel_id=1, source_target_pairs={{0,28},{1,5},{4,8},{5,1},{8,4},{9,13},{12,16},{13,9},{16,12},{17,2... | collective-permute-start | bytes 2359304 | tf_op jit(solution)/shard_map/ppermute | solution.py:50
  68.8 19.3 %collective-permute-start.16 = (bf16[2,192,1024]{2,1,0:T(8,128)(2,1)S(1)}, bf16[2,192,1024]{2,1,0:T(8,128)(2,1)S(1)}, u32[]{:S(2)}, u32[]{:S(2)}) collective-permute-start(bf16[2,192,1024]{2,1,0:T(8,128)(2,1)S(1)} %collective-permute-done.15.refs_6_), channel_id=1, source_target_pairs={{0,28},{1,5},{4,8},{5,1},{8,4},{9,13},{12,16},{13,9},{16,12},{17,2... | collective-permute-start | bytes 2359304 | tf_op jit(solution)/shard_map/ppermute | solution.py:50
  91.5 3.5 %collective-permute-start.23 = (f32[768,512]{1,0:T(8,128)S(1)}, f32[768,512]{1,0:T(8,128)S(1)}, u32[]{:S(2)}, u32[]{:S(2)}) collective-permute-start(f32[768,512]{1,0:T(8,128)S(1)} %multiply_other.3), channel_id=1, source_target_pairs={{0,1},{1,0},{4,5},{5,4},{8,9},{9,8},{12,13},{13,12},{16,17},{17,16... | collective-permute-start | bytes 4718600 | tf_op jit(solution)/shard_map/ppermute | solution.py:50
  94.2 4.7 %collective-permute-start.21 = (f32[768,512]{1,0:T(8,128)S(1)}, f32[768,512]{1,0:T(8,128)S(1)}, u32[]{:S(2)}, u32[]{:S(2)}) collective-permute-start(f32[768,512]{1,0:T(8,128)S(1)} %multiply_other.2), channel_id=1, source_target_pairs={{0,1},{1,0},{4,5},{5,4},{8,9},{9,8},{12,13},{13,12},{16,17},{17,16... | collective-permute-start | bytes 4718600 | tf_op jit(solution)/shard_map/ppermute | solution.py:50
  97.6 13.6 %collective-permute-start.24 = (bf16[384,512]{1,0:T(8,128)(2,1)S(1)}, bf16[384,512]{1,0:T(8,128)(2,1)S(1)}, u32[]{:S(2)}, u32[]{:S(2)}) collective-permute-start(bf16[384,512]{1,0:T(8,128)(2,1)S(1)} %get-tuple-element.34), channel_id=1, source_target_pairs={{0,2},{1,3},{4,6},{5,7},{8,10},{9,11},{12,14},{13,15},{16,18},{17,... | collective-permute-start | bytes 1179656 | tf_op jit(solution)/shard_map/ppermute | solution.py:50
  101.6 17.2 %collective-permute-start.22 = (bf16[384,512]{1,0:T(8,128)(2,1)S(1)}, bf16[384,512]{1,0:T(8,128)(2,1)S(1)}, u32[]{:S(2)}, u32[]{:S(2)}) collective-permute-start(bf16[384,512]{1,0:T(8,128)(2,1)S(1)} %get-tuple-element.32), channel_id=1, source_target_pairs={{0,2},{1,3},{4,6},{5,7},{8,10},{9,11},{12,14},{13,15},{16,18},{17,... | collective-permute-start | bytes 1179656 | tf_op jit(solution)/shard_map/ppermute | solution.py:50

commit v6 on v5

--- a/solution.py
+++ b/solution.py
@@ -267,8 +267,7 @@
     place = jnp.stack([pair, z, x_hi, x_hi * 2 + x_lo, y, core]).astype(jnp.int32)
 
     keep, give = mask_amplitudes(place, amp_mask, amplitudes.T)
-    int_t, keep, give = lax.optimization_barrier((integrals.T, keep, give))
-    first, second = mask_integrals(place, int_mask, int_t)
+    first, second = mask_integrals(place, int_mask, integrals.T)
     chains = [ring_of_eight(keep), ring_of_eight(send(give, X_ACROSS))]
     ints = plane(first, (X_FIRST, X_OTHER), (Y_FIRST, Y_OTHER)) + plane(second, (Y_FIRST, Y_OTHER), (X_FIRST, X_OTHER))
     amps = order_amplitudes(place, chains)

time: 122 us -> 125 us (1.025)
  the two profiles are of different devices: /device:TPU:24 before, /device:TPU:6 now
where the time goes in v6:
time: 125 us; the launch traced here: 124 us
  starting transfers between devices  50.7 us (41%)
  waiting for transfers between devices  49.6 us (40%)
  Pallas kernels  18.1 us (14%)
  local copies, waits for them, and re-layouts  3.79 us (3%)
  other arithmetic  1.95 us (2%)
    ppermute x25, starting transfers between devices, send(): return lax.ppermute(array, AXES, plan)  50.7 us
    ppermute x25, waiting for transfers between devices, send(): return lax.ppermute(array, AXES, plan)  49.6 us
    pallas_call x4, Pallas kernels, multiply(): pl.pallas_call(kernel, in_specs=[vmem_spec] * (2 + len(other)), out_specs...  10.4 us
    unnamed x10, local copies, waits for them, and re-layouts  3.63 us
    pallas_call x3, Pallas kernels, order_amplitudes(): pl.pallas_call(kernel, in_specs=[pl.BlockSpec(memory_space=SMEM)] + [any_...  3.33 us
    pallas_call x2, Pallas kernels, order_integrals(): pl.pallas_call(kernel, in_specs=[pl.BlockSpec(memory_space=SMEM)] + [any_...  2.96 us
  transfers between devices with their start and end apart: 25, of which 12 were waited for; matrix products, arithmetic and copies ran while one was open for 1% of the time, Pallas kernels for 11%

profile of v6, /device:TPU:6, one launch (start us, length us, event | category | flops | bytes accessed | tf_op | source)
XLA Modules:
  0.0 124.3 jit_solution(6451163039180973818)
XLA Ops:
  0.1 1.1 copy-done.1
  1.2 0.7 copy-done.2
  1.8 0.8 mask_integrals.1
  2.7 0.9 collective-permute-start
  3.6 1.1 copy-done
  4.7 0.7 copy-done.3
  5.4 0.6 mask_amplitudes.1
  6.0 2.0 %collective-permute-start.17 = (bf16[192,1024]{1,0:T(8,128)(2,1)S(1)}, bf16[192,1024]{1,0:T(8,128)(2,1)S(1)}, u32[]{:S(2)}, u32[]{:S(2)}) collective-permute-start(bf16[192,1024]{1,0:T(8,128)(2,1)S(1)} %get-tuple-element.23), channel_id=1, source_target_pairs={{0,4},{1,29},{4,0},{5,9},{8,12},{9,5},{12,8},{13,17},{16,20},{17,1... | collective-permute-start | bytes 1179656 | tf_op jit(solution)/shard_map/ppermute | solution.py:50
  8.0 1.1 collective-permute-start.12
  9.1 1.6 %collective-permute-start.6 = (bf16[192,768]{1,0:T(8,128)(2,1)S(1)}, bf16[192,768]{1,0:T(8,128)(2,1)S(1)}, u32[]{:S(2)}, u32[]{:S(2)}) collective-permute-start(bf16[192,768]{1,0:T(8,128)(2,1)S(1)} %get-tuple-element.18), channel_id=1, source_target_pairs={{0,32},{1,97},{4,36},{5,101},{8,40},{9,105},{12,44},{13,109},{16,4... | collective-permute-start | bytes 884744 | tf_op jit(solution)/shard_map/ppermute | solution.py:50
  10.7 0.5 collective-permute-start.1
  11.3 2.6 %collective-permute-done.17 = bf16[192,1024]{1,0:T(8,128)(2,1)S(1)} collective-permute-done((bf16[192,1024]{1,0:T(8,128)(2,1)S(1)}, bf16[192,1024]{1,0:T(8,128)(2,1)S(1)}, u32[]{:S(2)}, u32[]{:S(2)}) %collective-permute-start.17) | collective-permute-done | bytes 393248 | tf_op jit(solution)/shard_map/ppermute | solution.py:50
  13.9 5.9 %collective-permute-start.18 = (bf16[2,192,1024]{2,1,0:T(8,128)(2,1)S(1)}, bf16[2,192,1024]{2,1,0:T(8,128)(2,1)S(1)}, u32[]{:S(2)}, u32[]{:S(2)}) collective-permute-start(bf16[2,192,1024]{2,1,0:T(8,128)(2,1)S(1)} %pad_maximum_fusion.4.refs_1_), channel_id=1, source_target_pairs={{0,28},{1,5},{4,8},{5,1},{8,4},{9,13},{12,16},{13,9},{16,12},{17,2... | collective-permute-start | bytes 2359304 | tf_op jit(solution)/shard_map/ppermute | solution.py:50
  19.9 1.5 %collective-permute-start.13 = (bf16[192,1024]{1,0:T(8,128)(2,1)S(1)}, bf16[192,1024]{1,0:T(8,128)(2,1)S(1)}, u32[]{:S(2)}, u32[]{:S(2)}) collective-permute-start(bf16[192,1024]{1,0:T(8,128)(2,1)S(1)} %collective-permute-done.12), channel_id=1, source_target_pairs={{0,4},{1,29},{4,0},{5,9},{8,12},{9,5},{12,8},{13,17},{16,20},{17,1... | collective-permute-start | bytes 1179656 | tf_op jit(solution)/shard_map/ppermute | solution.py:50
  21.4 0.5 collective-permute-start.3
  21.9 2.0 %collective-permute-start.7 = (bf16[2,192,768]{2,1,0:T(8,128)(2,1)S(1)}, bf16[2,192,768]{2,1,0:T(8,128)(2,1)S(1)}, u32[]{:S(2)}, u32[]{:S(2)}) collective-permute-start(bf16[2,192,768]{2,1,0:T(8,128)(2,1)S(1)} %pad_maximum_fusion.6), channel_id=1, source_target_pairs={{0,128},{1,131},{4,132},{5,135},{8,136},{9,139},{12,140},{13,143},... | collective-permute-start | bytes 1769480 | tf_op jit(solution)/shard_map/ppermute | solution.py:50
  23.9 7.8 %collective-permute-done.13 = bf16[192,1024]{1,0:T(8,128)(2,1)S(1)} collective-permute-done((bf16[192,1024]{1,0:T(8,128)(2,1)S(1)}, bf16[192,1024]{1,0:T(8,128)(2,1)S(1)}, u32[]{:S(2)}, u32[]{:S(2)}) %collective-permute-start.13) | collective-permute-done | bytes 393248 | tf_op jit(solution)/shard_map/ppermute | solution.py:50
  31.7 3.0 %collective-permute-start.9 = (bf16[2,192,768]{2,1,0:T(8,128)(2,1)S(1)}, bf16[2,192,768]{2,1,0:T(8,128)(2,1)S(1)}, u32[]{:S(2)}, u32[]{:S(2)}) collective-permute-start(bf16[2,192,768]{2,1,0:T(8,128)(2,1)S(1)} %pad_maximum_fusion.6), channel_id=1, source_target_pairs={{0,96},{1,33},{4,100},{5,37},{8,104},{9,41},{12,108},{13,45},{16,1... | collective-permute-start | bytes 1769480 | tf_op jit(solution)/shard_map/ppermute | solution.py:50
  34.8 3.0 %collective-permute-start.14 = (bf16[2,192,1024]{2,1,0:T(8,128)(2,1)S(1)}, bf16[2,192,1024]{2,1,0:T(8,128)(2,1)S(1)}, u32[]{:S(2)}, u32[]{:S(2)}) collective-permute-start(bf16[2,192,1024]{2,1,0:T(8,128)(2,1)S(1)} %pad_maximum_fusion.3.refs_2_), channel_id=1, source_target_pairs={{0,28},{1,5},{4,8},{5,1},{8,4},{9,13},{12,16},{13,9},{16,12},{17,2... | collective-permute-start | bytes 2359304 | tf_op jit(solution)/shard_map/ppermute | solution.py:50
  37.9 0.6 collective-permute-done.3
  38.4 1.6 %collective-permute-start.4 = (bf16[2,192,768]{2,1,0:T(8,128)(2,1)S(1)}, bf16[2,192,768]{2,1,0:T(8,128)(2,1)S(1)}, u32[]{:S(2)}, u32[]{:S(2)}) collective-permute-start(bf16[2,192,768]{2,1,0:T(8,128)(2,1)S(1)} %collective-permute-done.3), channel_id=1, source_target_pairs={{0,32},{1,97},{4,36},{5,101},{8,40},{9,105},{12,44},{13,109},{16,4... | collective-permute-start | bytes 1769480 | tf_op jit(solution)/shard_map/ppermute | solution.py:50
  40.1 2.3 %collective-permute-start.2 = (bf16[4,192,768]{2,1,0:T(8,128)(2,1)S(1)}, bf16[4,192,768]{2,1,0:T(8,128)(2,1)S(1)}, u32[]{:S(2)}, u32[]{:S(2)}) collective-permute-start(bf16[4,192,768]{2,1,0:T(8,128)(2,1)S(1)} %pad_maximum_fusion.1.refs_1_), channel_id=1, source_target_pairs={{0,96},{1,33},{4,100},{5,37},{8,104},{9,41},{12,108},{13,45},{16,1... | collective-permute-start | bytes 3538952 | tf_op jit(solution)/shard_map/ppermute | solution.py:50
  42.4 3.8 %collective-permute-done.9 = bf16[2,192,768]{2,1,0:T(8,128)(2,1)S(1)} collective-permute-done((bf16[2,192,768]{2,1,0:T(8,128)(2,1)S(1)}, bf16[2,192,768]{2,1,0:T(8,128)(2,1)S(1)}, u32[]{:S(2)}, u32[]{:S(2)}) %collective-permute-start.9) | collective-permute-done | bytes 589856 | tf_op jit(solution)/shard_map/ppermute | solution.py:50
  46.3 9.4 %collective-permute-done.14.refs_4_ = bf16[2,192,1024]{2,1,0:T(8,128)(2,1)S(1)} collective-permute-done((bf16[2,192,1024]{2,1,0:T(8,128)(2,1)S(1)}, bf16[2,192,1024]{2,1,0:T(8,128)(2,1)S(1)}, u32[]{:S(2)}, u32[]{:S(2)}) %collective-permute-start.14) | collective-permute-done | bytes 786464 | tf_op jit(solution)/shard_map/ppermute | solution.py:50
  55.7 0.1 pad_maximum_fusion.2.refs_3_
  55.8 1.1 collective-permute-start.8
  57.0 3.2 %collective-permute-start.5 = (bf16[4,192,768]{2,1,0:T(8,128)(2,1)S(1)}, bf16[4,192,768]{2,1,0:T(8,128)(2,1)S(1)}, u32[]{:S(2)}, u32[]{:S(2)}) collective-permute-start(bf16[4,192,768]{2,1,0:T(8,128)(2,1)S(1)} %constant_dynamic-update-slice_fusion.refs_2_), channel_id=1, source_target_pairs={{0,96},{1,33},{4,100},{5,37},{8,104},{9,41},{12,108},{13,45},{16,1... | collective-permute-start | bytes 3538952 | tf_op jit(solution)/shard_map/ppermute | solution.py:50
  60.3 1.0 collective-permute-start.11
  61.2 0.5 collective-permute-done.2.refs_1_
  61.8 12.1 %collective-permute-start.20 = (bf16[2,192,1024]{2,1,0:T(8,128)(2,1)S(1)}, bf16[2,192,1024]{2,1,0:T(8,128)(2,1)S(1)}, u32[]{:S(2)}, u32[]{:S(2)}) collective-permute-start(bf16[2,192,1024]{2,1,0:T(8,128)(2,1)S(1)} %collective-permute-done.19.refs_5_), channel_id=1, source_target_pairs={{0,28},{1,5},{4,8},{5,1},{8,4},{9,13},{12,16},{13,9},{16,12},{17,2... | collective-permute-start | bytes 2359304 | tf_op jit(solution)/shard_map/ppermute | solution.py:50
  73.9 3.1 %collective-permute-start.16 = (bf16[2,192,1024]{2,1,0:T(8,128)(2,1)S(1)}, bf16[2,192,1024]{2,1,0:T(8,128)(2,1)S(1)}, u32[]{:S(2)}, u32[]{:S(2)}) collective-permute-start(bf16[2,192,1024]{2,1,0:T(8,128)(2,1)S(1)} %collective-permute-done.15.refs_6_), channel_id=1, source_target_pairs={{0,28},{1,5},{4,8},{5,1},{8,4},{9,13},{12,16},{13,9},{16,12},{17,2... | collective-permute-start | bytes 2359304 | tf_op jit(solution)/shard_map/ppermute | solution.py:50
  77.0 1.5 %order_integrals.2 = (bf16[768,3072]{1,0:T(8,128)(2,1)S(1)}, bf16[768,3072]{1,0:T(8,128)(2,1)S(1)}) custom-call(s32[6]{0:T(128)S(1)} %stack.63.place.refs_0_, bf16[4,192,768]{2,1,0:T(8,128)(2,1)S(1)} %pad_maximum_fusion.1.refs_1_, bf16[4,192,768]{2,1,0:T(8,128)(2,1)S(1)} %constant_dynamic-update-slice_fusion.refs_2_, ...), custom_call_target="tpu_custom_call" | custom-call | bytes 9437184 | tf_op jit(solution)/shard_map/order_integrals/pallas_call | solution.py:214
  78.4 1.8 %order_amplitudes.3.refs_2_ = bf16[3072,1024]{1,0:T(8,128)(2,1)S(1)} custom-call(s32[6]{0:T(128)S(1)} %stack.63.place.refs_0_, bf16[2,192,1024]{2,1,0:T(8,128)(2,1)S(1)} %pad_maximum_fusion.4.refs_1_, bf16[2,192,1024]{2,1,0:T(8,128)(2,1)S(1)} %pad_maximum_fusion.3.refs_2_, bf16[2,192,1024]{2,1,0:T(8,128)(2,1)S(1)} %collective-permute-done.18.refs_3_, ...), custom_call_target="tpu_custom_call" | custom-call | bytes 9437184 | tf_op jit(solution)/shard_map/order_amplitudes/pallas_call | solution.py:159
  80.3 5.7 %collective-permute-done.11.refs_4_ = bf16[4,192,768]{2,1,0:T(8,128)(2,1)S(1)} collective-permute-done((bf16[4,192,768]{2,1,0:T(8,128)(2,1)S(1)}, bf16[4,192,768]{2,1,0:T(8,128)(2,1)S(1)}, u32[]{:S(2)}, u32[]{:S(2)}) %collective-permute-start.11) | collective-permute-done | bytes 1179680 | tf_op jit(solution)/shard_map/ppermute | solution.py:50
  86.0 1.5 %order_integrals.3 = (bf16[768,3072]{1,0:T(8,128)(2,1)S(1)}, bf16[768,3072]{1,0:T(8,128)(2,1)S(1)}) custom-call(s32[6]{0:T(128)S(1)} %stack.63.place.refs_0_, bf16[4,192,768]{2,1,0:T(8,128)(2,1)S(1)} %collective-permute-done.2.refs_1_, bf16[4,192,768]{2,1,0:T(8,128)(2,1)S(1)} %collective-permute-done.5.refs_2_, ...), custom_call_target="tpu_custom_call", output_to_operand_aliasing={{0}: (5, {}), {1}: (6, {})} | custom-call | bytes 9437184 | tf_op jit(solution)/shard_map/order_integrals/pallas_call | solution.py:214
  87.5 0.8 order_amplitudes.4.refs_2_
  88.2 4.0 %collective-permute-done.16.refs_1_ = bf16[2,192,1024]{2,1,0:T(8,128)(2,1)S(1)} collective-permute-done((bf16[2,192,1024]{2,1,0:T(8,128)(2,1)S(1)}, bf16[2,192,1024]{2,1,0:T(8,128)(2,1)S(1)}, u32[]{:S(2)}, u32[]{:S(2)}) %collective-permute-start.16) | collective-permute-done | bytes 786464 | tf_op jit(solution)/shard_map/ppermute | solution.py:50
  92.2 0.8 order_amplitudes.5.refs_1_
  93.0 2.6 %multiply_other.3 = f32[768,512]{1,0:T(8,128)S(1)} custom-call(bf16[768,3072]{1,0:T(8,128)(2,1)S(1)} %get-tuple-element.24.refs_0_, bf16[3072,1024]{1,0:T(8,128)(2,1)S(1)} %order_amplitudes.5.refs_1_), custom_call_target="tpu_custom_call" | custom-call | flops 2415919104 | bytes 9437184 | tf_op jit(solution)/shard_map/multiply_other/pallas_call | solution.py:250
  95.7 2.6 %multiply_other.2 = f32[768,512]{1,0:T(8,128)S(1)} custom-call(bf16[768,3072]{1,0:T(8,128)(2,1)S(1)} %get-tuple-element.24.refs_0_, bf16[3072,1024]{1,0:T(8,128)(2,1)S(1)} %order_amplitudes.5.refs_1_), custom_call_target="tpu_custom_call" | custom-call | flops 2415919104 | bytes 9437184 | tf_op jit(solution)/shard_map/multiply_other/pallas_call | solution.py:250
  98.3 0.6 collective-permute-start.21
  98.9 0.2 collective-permute-done.23.refs_2_
  99.1 2.6 %multiply_own.3 = (bf16[384,512]{1,0:T(8,128)(2,1)S(1)}, bf16[384,512]{1,0:T(8,128)(2,1)S(1)}) custom-call(bf16[768,3072]{1,0:T(8,128)(2,1)S(1)} %get-tuple-element.21.refs_0_, bf16[3072,1024]{1,0:T(8,128)(2,1)S(1)} %order_amplitudes.5.refs_1_, f32[768,512]{1,0:T(8,128)S(1)} %collective-permute-done.23.refs_2_), custom_call_target="tpu_custom_call" | custom-call | flops 2415919104 | bytes 9437184 | tf_op jit(solution)/shard_map/multiply_own/pallas_call | solution.py:250
  101.9 2.6 %multiply_own.2 = (bf16[384,512]{1,0:T(8,128)(2,1)S(1)}, bf16[384,512]{1,0:T(8,128)(2,1)S(1)}) custom-call(bf16[768,3072]{1,0:T(8,128)(2,1)S(1)} %get-tuple-element.21.refs_0_, bf16[3072,1024]{1,0:T(8,128)(2,1)S(1)} %order_amplitudes.5.refs_1_, f32[768,512]{1,0:T(8,128)S(1)} %collective-permute-done.21.refs_2_), custom_call_target="tpu_custom_call" | custom-call | flops 2415919104 | bytes 9437184 | tf_op jit(solution)/shard_map/multiply_own/pallas_call | solution.py:250
  104.5 3.5 %collective-permute-start.22 = (bf16[384,512]{1,0:T(8,128)(2,1)S(1)}, bf16[384,512]{1,0:T(8,128)(2,1)S(1)}, u32[]{:S(2)}, u32[]{:S(2)}) collective-permute-start(bf16[384,512]{1,0:T(8,128)(2,1)S(1)} %get-tuple-element.26), channel_id=1, source_target_pairs={{0,2},{1,3},{4,6},{5,7},{8,10},{9,11},{12,14},{13,15},{16,18},{17,... | collective-permute-start | bytes 1179656 | tf_op jit(solution)/shard_map/ppermute | solution.py:50
  108.0 7.2 %collective-permute-done.24 = bf16[384,512]{1,0:T(8,128)(2,1)S(1)} collective-permute-done((bf16[384,512]{1,0:T(8,128)(2,1)S(1)}, bf16[384,512]{1,0:T(8,128)(2,1)S(1)}, u32[]{:S(2)}, u32[]{:S(2)}) %collective-permute-start.24) | collective-permute-done | bytes 393248 | tf_op jit(solution)/shard_map/ppermute | solution.py:50
  115.3 7.6 %collective-permute-done.22 = bf16[384,512]{1,0:T(8,128)(2,1)S(1)} collective-permute-done((bf16[384,512]{1,0:T(8,128)(2,1)S(1)}, bf16[384,512]{1,0:T(8,128)(2,1)S(1)}, u32[]{:S(2)}, u32[]{:S(2)}) %collective-permute-start.22) | collective-permute-done | bytes 393248 | tf_op jit(solution)/shard_map/ppermute | solution.py:50
  122.9 1.3 %pad_maximum_fusion = bf16[384,2048]{1,0:T(8,128)(2,1)} fusion(bf16[384,512]{1,0:T(8,128)(2,1)S(1)} %get-tuple-element.32, bf16[384,512]{1,0:T(8,128)(2,1)S(1)} %get-tuple-element.30, bf16[384,512]{1,0:T(8,128)(2,1)S(1)} %get-tuple-element.31, bf16[384,512]{1,0:T(8,128)(2,1)S(1)} %get-tuple-element.29), kind=kLoop, calls=%fused_computation | loop fusion | flops 6291456 | bytes 3145728 | tf_op jit(solution)/shard_map/concatenate | solution.py:284
  (35 shorter events, 1.1 us)
Async XLA Ops:
  0.1 1.1 copy-start.1
  1.2 0.7 copy-start.2
  2.7 8.0 %collective-permute-start = (bf16[192,768]{1,0:T(8,128)(2,1)S(1)}, bf16[192,768]{1,0:T(8,128)(2,1)S(1)}, u32[]{:S(2)}, u32[]{:S(2)}) collective-permute-start(bf16[192,768]{1,0:T(8,128)(2,1)S(1)} %get-tuple-element.17), channel_id=1, source_target_pairs={{0,128},{1,131},{4,132},{5,135},{8,136},{9,139},{12,140},{13,143},... | collective-permute-start | bytes 884744 | tf_op jit(solution)/shard_map/ppermute | solution.py:50
  3.6 1.1 copy-start
  4.7 0.7 copy-start.3
  6.0 7.9 %collective-permute-start.17 = (bf16[192,1024]{1,0:T(8,128)(2,1)S(1)}, bf16[192,1024]{1,0:T(8,128)(2,1)S(1)}, u32[]{:S(2)}, u32[]{:S(2)}) collective-permute-start(bf16[192,1024]{1,0:T(8,128)(2,1)S(1)} %get-tuple-element.23), channel_id=1, source_target_pairs={{0,4},{1,29},{4,0},{5,9},{8,12},{9,5},{12,8},{13,17},{16,20},{17,1... | collective-permute-start | bytes 1179656 | tf_op jit(solution)/shard_map/ppermute | solution.py:50
  8.0 11.9 %collective-permute-start.12 = (bf16[192,1024]{1,0:T(8,128)(2,1)S(1)}, bf16[192,1024]{1,0:T(8,128)(2,1)S(1)}, u32[]{:S(2)}, u32[]{:S(2)}) collective-permute-start(bf16[192,1024]{1,0:T(8,128)(2,1)S(1)} %get-tuple-element.22), channel_id=1, source_target_pairs={{0,2},{1,3},{4,6},{5,7},{8,10},{9,11},{12,14},{13,15},{16,18},{17,... | collective-permute-start | bytes 1179656 | tf_op jit(solution)/shard_map/ppermute | solution.py:50
  9.1 12.8 %collective-permute-start.6 = (bf16[192,768]{1,0:T(8,128)(2,1)S(1)}, bf16[192,768]{1,0:T(8,128)(2,1)S(1)}, u32[]{:S(2)}, u32[]{:S(2)}) collective-permute-start(bf16[192,768]{1,0:T(8,128)(2,1)S(1)} %get-tuple-element.18), channel_id=1, source_target_pairs={{0,32},{1,97},{4,36},{5,101},{8,40},{9,105},{12,44},{13,109},{16,4... | collective-permute-start | bytes 884744 | tf_op jit(solution)/shard_map/ppermute | solution.py:50
  10.7 24.1 %collective-permute-start.1 = (bf16[2,192,768]{2,1,0:T(8,128)(2,1)S(1)}, bf16[2,192,768]{2,1,0:T(8,128)(2,1)S(1)}, u32[]{:S(2)}, u32[]{:S(2)}) collective-permute-start(bf16[2,192,768]{2,1,0:T(8,128)(2,1)S(1)} %pad_maximum_fusion.5), channel_id=1, source_target_pairs={{0,32},{1,97},{4,36},{5,101},{8,40},{9,105},{12,44},{13,109},{16,4... | collective-permute-start | bytes 1769480 | tf_op jit(solution)/shard_map/ppermute | solution.py:50
  13.9 26.1 %collective-permute-start.18 = (bf16[2,192,1024]{2,1,0:T(8,128)(2,1)S(1)}, bf16[2,192,1024]{2,1,0:T(8,128)(2,1)S(1)}, u32[]{:S(2)}, u32[]{:S(2)}) collective-permute-start(bf16[2,192,1024]{2,1,0:T(8,128)(2,1)S(1)} %pad_maximum_fusion.4.refs_1_), channel_id=1, source_target_pairs={{0,28},{1,5},{4,8},{5,1},{8,4},{9,13},{12,16},{13,9},{16,12},{17,2... | collective-permute-start | bytes 2359304 | tf_op jit(solution)/shard_map/ppermute | solution.py:50
  19.9 11.8 %collective-permute-start.13 = (bf16[192,1024]{1,0:T(8,128)(2,1)S(1)}, bf16[192,1024]{1,0:T(8,128)(2,1)S(1)}, u32[]{:S(2)}, u32[]{:S(2)}) collective-permute-start(bf16[192,1024]{1,0:T(8,128)(2,1)S(1)} %collective-permute-done.12), channel_id=1, source_target_pairs={{0,4},{1,29},{4,0},{5,9},{8,12},{9,5},{12,8},{13,17},{16,20},{17,1... | collective-permute-start | bytes 1179656 | tf_op jit(solution)/shard_map/ppermute | solution.py:50
  21.4 17.1 %collective-permute-start.3 = (bf16[2,192,768]{2,1,0:T(8,128)(2,1)S(1)}, bf16[2,192,768]{2,1,0:T(8,128)(2,1)S(1)}, u32[]{:S(2)}, u32[]{:S(2)}) collective-permute-start(bf16[2,192,768]{2,1,0:T(8,128)(2,1)S(1)} %pad_maximum_fusion.5), channel_id=1, source_target_pairs={{0,130},{1,129},{4,134},{5,133},{8,138},{9,137},{12,142},{13,141},... | collective-permute-start | bytes 1769480 | tf_op jit(solution)/shard_map/ppermute | solution.py:50
  21.9 18.2 %collective-permute-start.7 = (bf16[2,192,768]{2,1,0:T(8,128)(2,1)S(1)}, bf16[2,192,768]{2,1,0:T(8,128)(2,1)S(1)}, u32[]{:S(2)}, u32[]{:S(2)}) collective-permute-start(bf16[2,192,768]{2,1,0:T(8,128)(2,1)S(1)} %pad_maximum_fusion.6), channel_id=1, source_target_pairs={{0,128},{1,131},{4,132},{5,135},{8,136},{9,139},{12,140},{13,143},... | collective-permute-start | bytes 1769480 | tf_op jit(solution)/shard_map/ppermute | solution.py:50
  31.7 14.5 %collective-permute-start.9 = (bf16[2,192,768]{2,1,0:T(8,128)(2,1)S(1)}, bf16[2,192,768]{2,1,0:T(8,128)(2,1)S(1)}, u32[]{:S(2)}, u32[]{:S(2)}) collective-permute-start(bf16[2,192,768]{2,1,0:T(8,128)(2,1)S(1)} %pad_maximum_fusion.6), channel_id=1, source_target_pairs={{0,96},{1,33},{4,100},{5,37},{8,104},{9,41},{12,108},{13,45},{16,1... | collective-permute-start | bytes 1769480 | tf_op jit(solution)/shard_map/ppermute | solution.py:50
  34.8 20.9 %collective-permute-start.14 = (bf16[2,192,1024]{2,1,0:T(8,128)(2,1)S(1)}, bf16[2,192,1024]{2,1,0:T(8,128)(2,1)S(1)}, u32[]{:S(2)}, u32[]{:S(2)}) collective-permute-start(bf16[2,192,1024]{2,1,0:T(8,128)(2,1)S(1)} %pad_maximum_fusion.3.refs_2_), channel_id=1, source_target_pairs={{0,28},{1,5},{4,8},{5,1},{8,4},{9,13},{12,16},{13,9},{16,12},{17,2... | collective-permute-start | bytes 2359304 | tf_op jit(solution)/shard_map/ppermute | solution.py:50
  38.4 17.4 %collective-permute-start.4 = (bf16[2,192,768]{2,1,0:T(8,128)(2,1)S(1)}, bf16[2,192,768]{2,1,0:T(8,128)(2,1)S(1)}, u32[]{:S(2)}, u32[]{:S(2)}) collective-permute-start(bf16[2,192,768]{2,1,0:T(8,128)(2,1)S(1)} %collective-permute-done.3), channel_id=1, source_target_pairs={{0,32},{1,97},{4,36},{5,101},{8,40},{9,105},{12,44},{13,109},{16,4... | collective-permute-start | bytes 1769480 | tf_op jit(solution)/shard_map/ppermute | solution.py:50
  40.0 20.2 %collective-permute-start.19 = (bf16[2,192,1024]{2,1,0:T(8,128)(2,1)S(1)}, bf16[2,192,1024]{2,1,0:T(8,128)(2,1)S(1)}, u32[]{:S(2)}, u32[]{:S(2)}) collective-permute-start(bf16[2,192,1024]{2,1,0:T(8,128)(2,1)S(1)} %collective-permute-done.18.refs_3_), channel_id=1, source_target_pairs={{0,4},{1,29},{4,0},{5,9},{8,12},{9,5},{12,8},{13,17},{16,20},{17,1... | collective-permute-start | bytes 2359304 | tf_op jit(solution)/shard_map/ppermute | solution.py:50
  40.1 21.6 %collective-permute-start.2 = (bf16[4,192,768]{2,1,0:T(8,128)(2,1)S(1)}, bf16[4,192,768]{2,1,0:T(8,128)(2,1)S(1)}, u32[]{:S(2)}, u32[]{:S(2)}) collective-permute-start(bf16[4,192,768]{2,1,0:T(8,128)(2,1)S(1)} %pad_maximum_fusion.1.refs_1_), channel_id=1, source_target_pairs={{0,96},{1,33},{4,100},{5,37},{8,104},{9,41},{12,108},{13,45},{16,1... | collective-permute-start | bytes 3538952 | tf_op jit(solution)/shard_map/ppermute | solution.py:50
  46.2 10.8 %collective-permute-start.10 = (bf16[2,192,768]{2,1,0:T(8,128)(2,1)S(1)}, bf16[2,192,768]{2,1,0:T(8,128)(2,1)S(1)}, u32[]{:S(2)}, u32[]{:S(2)}) collective-permute-start(bf16[2,192,768]{2,1,0:T(8,128)(2,1)S(1)} %collective-permute-done.9), channel_id=1, source_target_pairs={{0,128},{1,131},{4,132},{5,135},{8,136},{9,139},{12,140},{13,143},... | collective-permute-start | bytes 1769480 | tf_op jit(solution)/shard_map/ppermute | solution.py:50
  55.7 18.2 %collective-permute-start.15 = (bf16[2,192,1024]{2,1,0:T(8,128)(2,1)S(1)}, bf16[2,192,1024]{2,1,0:T(8,128)(2,1)S(1)}, u32[]{:S(2)}, u32[]{:S(2)}) collective-permute-start(bf16[2,192,1024]{2,1,0:T(8,128)(2,1)S(1)} %collective-permute-done.14.refs_4_), channel_id=1, source_target_pairs={{0,4},{1,29},{4,0},{5,9},{8,12},{9,5},{12,8},{13,17},{16,20},{17,1... | collective-permute-start | bytes 2359304 | tf_op jit(solution)/shard_map/ppermute | solution.py:50
  55.8 24.4 %collective-permute-start.8 = (bf16[4,192,768]{2,1,0:T(8,128)(2,1)S(1)}, bf16[4,192,768]{2,1,0:T(8,128)(2,1)S(1)}, u32[]{:S(2)}, u32[]{:S(2)}) collective-permute-start(bf16[4,192,768]{2,1,0:T(8,128)(2,1)S(1)} %pad_maximum_fusion.2.refs_3_), channel_id=1, source_target_pairs={{0,130},{1,129},{4,134},{5,133},{8,138},{9,137},{12,142},{13,141},... | collective-permute-start | bytes 3538952 | tf_op jit(solution)/shard_map/ppermute | solution.py:50
  57.0 23.3 %collective-permute-start.5 = (bf16[4,192,768]{2,1,0:T(8,128)(2,1)S(1)}, bf16[4,192,768]{2,1,0:T(8,128)(2,1)S(1)}, u32[]{:S(2)}, u32[]{:S(2)}) collective-permute-start(bf16[4,192,768]{2,1,0:T(8,128)(2,1)S(1)} %constant_dynamic-update-slice_fusion.refs_2_), channel_id=1, source_target_pairs={{0,96},{1,33},{4,100},{5,37},{8,104},{9,41},{12,108},{13,45},{16,1... | collective-permute-start | bytes 3538952 | tf_op jit(solution)/shard_map/ppermute | solution.py:50
  60.3 25.7 %collective-permute-start.11 = (bf16[4,192,768]{2,1,0:T(8,128)(2,1)S(1)}, bf16[4,192,768]{2,1,0:T(8,128)(2,1)S(1)}, u32[]{:S(2)}, u32[]{:S(2)}) collective-permute-start(bf16[4,192,768]{2,1,0:T(8,128)(2,1)S(1)} %constant_dynamic-update-slice_fusion.2.refs_4_), channel_id=1, source_target_pairs={{0,130},{1,129},{4,134},{5,133},{8,138},{9,137},{12,142},{13,141},... | collective-permute-start | bytes 3538952 | tf_op jit(solution)/shard_map/ppermute | solution.py:50
  61.8 25.7 %collective-permute-start.20 = (bf16[2,192,1024]{2,1,0:T(8,128)(2,1)S(1)}, bf16[2,192,1024]{2,1,0:T(8,128)(2,1)S(1)}, u32[]{:S(2)}, u32[]{:S(2)}) collective-permute-start(bf16[2,192,1024]{2,1,0:T(8,128)(2,1)S(1)} %collective-permute-done.19.refs_5_), channel_id=1, source_target_pairs={{0,28},{1,5},{4,8},{5,1},{8,4},{9,13},{12,16},{13,9},{16,12},{17,2... | collective-permute-start | bytes 2359304 | tf_op jit(solution)/shard_map/ppermute | solution.py:50
  73.9 18.4 %collective-permute-start.16 = (bf16[2,192,1024]{2,1,0:T(8,128)(2,1)S(1)}, bf16[2,192,1024]{2,1,0:T(8,128)(2,1)S(1)}, u32[]{:S(2)}, u32[]{:S(2)}) collective-permute-start(bf16[2,192,1024]{2,1,0:T(8,128)(2,1)S(1)} %collective-permute-done.15.refs_6_), channel_id=1, source_target_pairs={{0,28},{1,5},{4,8},{5,1},{8,4},{9,13},{12,16},{13,9},{16,12},{17,2... | collective-permute-start | bytes 2359304 | tf_op jit(solution)/shard_map/ppermute | solution.py:50
  95.6 3.5 %collective-permute-start.23 = (f32[768,512]{1,0:T(8,128)S(1)}, f32[768,512]{1,0:T(8,128)S(1)}, u32[]{:S(2)}, u32[]{:S(2)}) collective-permute-start(f32[768,512]{1,0:T(8,128)S(1)} %multiply_other.3), channel_id=1, source_target_pairs={{0,1},{1,0},{4,5},{5,4},{8,9},{9,8},{12,13},{13,12},{16,17},{17,16... | collective-permute-start | bytes 4718600 | tf_op jit(solution)/shard_map/ppermute | solution.py:50
  98.3 3.6 %collective-permute-start.21 = (f32[768,512]{1,0:T(8,128)S(1)}, f32[768,512]{1,0:T(8,128)S(1)}, u32[]{:S(2)}, u32[]{:S(2)}) collective-permute-start(f32[768,512]{1,0:T(8,128)S(1)} %multiply_other.2), channel_id=1, source_target_pairs={{0,1},{1,0},{4,5},{5,4},{8,9},{9,8},{12,13},{13,12},{16,17},{17,16... | collective-permute-start | bytes 4718600 | tf_op jit(solution)/shard_map/ppermute | solution.py:50
  101.7 13.5 %collective-permute-start.24 = (bf16[384,512]{1,0:T(8,128)(2,1)S(1)}, bf16[384,512]{1,0:T(8,128)(2,1)S(1)}, u32[]{:S(2)}, u32[]{:S(2)}) collective-permute-start(bf16[384,512]{1,0:T(8,128)(2,1)S(1)} %get-tuple-element.28), channel_id=1, source_target_pairs={{0,2},{1,3},{4,6},{5,7},{8,10},{9,11},{12,14},{13,15},{16,18},{17,... | collective-permute-start | bytes 1179656 | tf_op jit(solution)/shard_map/ppermute | solution.py:50
  104.5 18.4 %collective-permute-start.22 = (bf16[384,512]{1,0:T(8,128)(2,1)S(1)}, bf16[384,512]{1,0:T(8,128)(2,1)S(1)}, u32[]{:S(2)}, u32[]{:S(2)}) collective-permute-start(bf16[384,512]{1,0:T(8,128)(2,1)S(1)} %get-tuple-element.26), channel_id=1, source_target_pairs={{0,2},{1,3},{4,6},{5,7},{8,10},{9,11},{12,14},{13,15},{16,18},{17,... | collective-permute-start | bytes 1179656 | tf_op jit(solution)/shard_map/ppermute | solution.py:50
